TPU v7x, 32 devices: a whole 2x2x4 slice. The times are simulated.
32 devices in a mesh: role: 4 (over y, core), shard: 8 (over z, x).
Axes of the slice: x: 2, y: 2, z: 4, core: 2. Of those that a mesh axis runs over, the one named last changes fastest.
Arguments:
- gradient: bfloat16 [2560, 2560], P('shard', 'role'), may hold values from -1200 to 1200
- left_old: float32 [2560, 2560], P('shard', 'role'), may hold values from -1 to 10, as said below
- right_old: float32 [2560, 2560], P('shard', 'role'), may hold values from -1 to 10, as said below
- basis_old: bfloat16 [2560, 512], P('shard', 'role'), may hold values from -1 to 1
Outputs:
- left_stat: float32 [2560, 2560], P('shard', 'role')
- right_stat: float32 [2560, 2560], P('shard', 'role')
- left_basis: float32 [2560, 512], P('shard', 'role')
Inputs may be any that keep to these rules, and one draw needn't show every extreme that they name: `left_old`: symmetric and positive definite. `right_old`: symmetric and positive definite.
All inputs are finite; a program needn't handle non-finite values.
Results may differ from a plain program's by a relative error of at most 0.0003.
Values may be sent and summed in bfloat16 or wider, within the bound.
No kernel may reach another device: no remote copies, remote signals or barrier semaphores. Data moves between devices by JAX's collectives and lax.ppermute only.
A program may use at most 64 MiB of HBM per device.

v0:
```python
import jax
import jax.numpy as jnp
from jax import lax
from jax.sharding import PartitionSpec as P

smoothing = 0.95
clip_ratio = 4.0
epsilon_value = 1e-06


def lower_gram(power_row, role_count, role_at):
    order_size = power_row.shape[1]
    tile_size = order_size // (2 * role_count)
    second_row = 2 * role_count - 1 - role_at

    def strip(tile_row):
        chosen = lax.dynamic_slice_in_dim(power_row, tile_row * tile_size, tile_size, 1)
        return lax.dot_general(
            chosen,
            power_row,
            (((0,), (0,)), ((), ())),
            precision=lax.Precision.HIGHEST,
            preferred_element_type=jnp.float32,
        )

    strip_first = strip(role_at)
    strip_second = strip(second_row)
    split_at = (role_at + 1) * tile_size
    packed_width = order_size + tile_size
    first_ext = jnp.concatenate(
        [strip_first, jnp.zeros((tile_size, tile_size), jnp.float32)], axis=1
    )
    padded_second = jnp.concatenate(
        [jnp.zeros((tile_size, order_size), jnp.float32), strip_second], axis=1
    )
    second_ext = lax.dynamic_slice_in_dim(padded_second, order_size - split_at, packed_width, 1)
    columns = lax.broadcasted_iota(jnp.int32, (tile_size, packed_width), 1)
    packed = jnp.where(columns < split_at, first_ext, second_ext)
    tile_sums = lax.psum(packed, "shard")
    strips = lax.all_gather(tile_sums, "role", axis=0, tiled=True)
    lower_part = jnp.zeros((order_size, order_size), jnp.float32)
    for member in range(role_count):
        packed_row = strips[member * tile_size : (member + 1) * tile_size]
        head = (member + 1) * tile_size
        other = 2 * role_count - 1 - member
        tail = (2 * role_count - member) * tile_size
        lower_part = lower_part.at[member * tile_size : head, :head].set(packed_row[:, :head])
        lower_part = lower_part.at[other * tile_size : (other + 1) * tile_size, :tail].set(
            packed_row[:, head : head + tail]
        )
    return jnp.tril(lower_part) + jnp.transpose(jnp.tril(lower_part, -1))


def on_device(gradient, left_old, right_old, basis_old):
    row_count, col_count = gradient.shape
    vec_count = basis_old.shape[1]
    order_size = row_count * lax.axis_size("shard")
    role_count = lax.axis_size("role")
    role_at = lax.axis_index("role")
    col_start = role_at * col_count
    vec_start = role_at * vec_count
    gradient_wide = gradient.astype(jnp.float32)
    squares = lax.psum(jnp.sum(gradient_wide * gradient_wide), ("role", "shard"))
    factor = jnp.minimum(
        1.0, clip_ratio * jnp.sqrt(jnp.float32(order_size)) / jnp.sqrt(squares + epsilon_value)
    )
    squared = factor * factor
    grad_row = lax.all_gather(gradient, "role", axis=1, tiled=True)
    left_part = lax.dot_general(
        gradient,
        lax.all_gather(gradient, "shard", axis=0, tiled=True),
        (((1,), (1,)), ((), ())),
        preferred_element_type=jnp.float32,
    )
    right_share = lax.psum_scatter(
        lax.dot_general(
            grad_row, gradient, (((0,), (0,)), ((), ())), preferred_element_type=jnp.float32
        ),
        "shard",
        scatter_dimension=0,
        tiled=True,
    )
    placed = lax.dynamic_update_slice_in_dim(
        jnp.zeros((row_count, order_size), jnp.float32), left_old, col_start, 1
    )
    left_row = lax.psum((1.0 - smoothing) * squared * left_part + smoothing * placed, "role")
    left_stat = lax.dynamic_slice_in_dim(left_row, col_start, col_count, 1)
    right_stat = smoothing * right_old + (1.0 - smoothing) * squared * right_share
    power_block = jnp.dot(
        left_row,
        lax.all_gather(basis_old, "shard", axis=0, tiled=True).astype(jnp.float32),
        precision=lax.Precision.HIGHEST,
    )
    power_row = lax.all_gather(power_block, "role", axis=1, tiled=True)
    gram_full = lower_gram(power_row, role_count, role_at)
    factor_lower = jnp.linalg.cholesky(gram_full)
    solved = jax.scipy.linalg.solve_triangular(factor_lower, power_row.T, lower=True)
    left_basis = lax.dynamic_slice_in_dim(solved, vec_start, vec_count, 0).T
    return (left_stat, right_stat, left_basis)


def solution(mesh):
    return jax.shard_map(
        on_device,
        mesh=mesh,
        in_specs=(P("shard", "role"), P("shard", "role"), P("shard", "role"), P("shard", "role")),
        out_specs=(P("shard", "role"), P("shard", "role"), P("shard", "role")),
        check_vma=False,
    )
```

profile of v0, /device:TPU:0, one launch (start us, length us, event | category | flops | bytes accessed | tf_op | source)
XLA Modules:
  0.0 411.2 jit_solution(2077507508806869421)
XLA Ops:
  7.9 1.8 multiply_reduce_fusion
  9.8 44.0 %psum.21 = f32[]{:T(128)} all-reduce(f32[]{:T(128)} %multiply_reduce_fusion), channel_id=1, replica_groups=mesh['role'=4,'shard'=8] {'role','shard'}, use_global_device_ids=true, to_apply=%region_1.0 | all-reduce | flops 1 | bytes 8 | tf_op jit(solution)/shard_map/psum | solution.py:63
  55.7 20.1 %all-gather.3.cloned.1.call-done = bf16[2560,640]{1,0:T(8,128)(2,1)} async-done(((bf16[320,640]{1,0:T(8,128)(2,1)}), bf16[2560,640]{1,0:T(8,128)(2,1)}) %all-gather.3.cloned.1.call-update) | async-done | bytes 3276816 | tf_op jit(solution)/shard_map/all_gather | solution.py:71
  75.8 5.2 %fusion = f32[320,2560]{1,0:T(8,128)} fusion(bf16[320,640]{1,0:T(8,128)(2,1)} %param.20, bf16[2560,640]{1,0:T(8,128)(2,1)} %all-gather.3.cloned.1.call-done, f32[320,2560]{1,0:T(8,128)S(1)} %constant_dynamic-update-slice_fusion.1, f32[]{:T(128)S(6)} %mul.51), kind=kOutput, calls=%fused_computation.3 | convolution fusion | flops 1051033600 | bytes 10240004 | tf_op jit(solution)/shard_map/dot_general | solution.py:69
  81.9 31.9 %all_gather.17 = bf16[2560,128]{1,0:T(8,128)(2,1)S(1)} all-gather(bf16[320,128]{1,0:T(8,128)(2,1)S(1)} %copy-done.3), channel_id=1, replica_groups=mesh['role'=4,'shard'=8] {'shard'}, dimensions={0}, use_global_device_ids=true | all-gather | bytes 737280 | tf_op jit(solution)/shard_map/all_gather | solution.py:91
  113.8 36.7 %all-reduce.7.cloned.1.call-done = f32[320,2560]{1,0:T(8,128)} async-done(((f32[320,2560]{1,0:T(8,128)}), f32[320,2560]{1,0:T(8,128)}) %all-reduce.7.cloned.1.call-update) | async-done | bytes 3276816 | tf_op jit(solution)/shard_map/psum | solution.py:86
  150.5 3.5 fusion.45
  154.0 7.2 %all_gather.18 = f32[320,512]{1,0:T(8,128)S(1)} all-gather(f32[320,128]{1,0:T(8,128)S(1)} %fusion.45), channel_id=1, replica_groups=mesh['role'=4,'shard'=8] {'role'}, dimensions={1}, use_global_device_ids=true | all-gather | bytes 819200 | tf_op jit(solution)/shard_map/all_gather | solution.py:94
  163.3 8.9 %all-gather.5.cloned.1.call-done = bf16[320,2560]{1,0:T(8,128)(2,1)} async-done(((bf16[320,640]{1,0:T(8,128)(2,1)}), bf16[320,2560]{1,0:T(8,128)(2,1)}) %all-gather.5.cloned.1.call-update) | async-done | bytes 1638416 | tf_op jit(solution)/shard_map/all_gather | solution.py:68
  172.2 6.3 %fusion.44 = f32[2560,640]{1,0:T(8,128)} fusion(bf16[320,2560]{1,0:T(8,128)(2,1)} %all-gather.5.cloned.1.call-done, bf16[320,640]{1,0:T(8,128)(2,1)S(1)} %copy-done), kind=kOutput, calls=%fused_computation.97 | convolution fusion | flops 1048576000 | bytes 8601600 | tf_op jit(solution)/shard_map/dot_general | solution.py:76
  178.5 2.1 constant_dynamic-slice_fusion.1
  180.6 65.4 %all-reduce.9.cloned.1.call-done = f32[64,576]{1,0:T(8,128)} async-done(((f32[64,576]{1,0:T(8,128)}), f32[64,576]{1,0:T(8,128)}) %all-reduce.9.cloned.1.call-update) | async-done | bytes 147472 | tf_op jit(solution)/shard_map/psum | solution.py:39
  246.0 8.1 %all_gather.19 = f32[256,576]{1,0:T(8,128)S(1)} all-gather(f32[64,576]{1,0:T(8,128)} %all-reduce.9.cloned.1.call-done), channel_id=1, replica_groups=mesh['role'=4,'shard'=8] {'role'}, dimensions={0}, use_global_device_ids=true | all-gather | bytes 737280 | tf_op jit(solution)/shard_map/all_gather | solution.py:40
  254.4 1.7 scatter.31
  256.0 1.6 scatter.34
  257.8 1.9 scatter.39
  259.7 1.3 copy.7
  261.1 1.4 bitcast_add_fusion.1
  264.1 11.7 %cholesky.103 = f32[128,128]{1,0:T(8,128)S(1)} custom-call(f32[128,128]{1,0:T(8,128)S(1)} %cholesky.263), custom_call_target="Cholesky" | custom-call | tf_op jit(solution)/shard_map/jit(cholesky)/cholesky | solution.py:96
  276.0 9.8 %custom-call.31 = f32[1,128,128]{1,2,0:T(8,128)S(1)} custom-call(f32[1,128,128]{2,1,0:T(8,128)S(1)} %get-tuple-element.126), custom_call_target="InvertDiagBlocksLowerTriangular" | custom-call | tf_op jit(solution)/shard_map/jit(cholesky)/cholesky | solution.py:96
  288.3 11.7 %cholesky.215 = f32[128,128]{1,0:T(8,128)S(1)} custom-call(f32[128,128]{1,0:T(8,128)S(1)} %cholesky.267), custom_call_target="Cholesky" | custom-call | tf_op jit(solution)/shard_map/jit(cholesky)/cholesky | solution.py:96
  300.1 10.0 %custom-call.32 = f32[1,128,128]{1,2,0:T(8,128)S(1)} custom-call(f32[1,128,128]{2,1,0:T(8,128)S(1)} %get-tuple-element.123), custom_call_target="InvertDiagBlocksLowerTriangular" | custom-call | tf_op jit(solution)/shard_map/jit(cholesky)/cholesky | solution.py:96
  311.7 11.7 %cholesky.236 = f32[128,128]{1,0:T(8,128)S(1)} custom-call(f32[128,128]{1,0:T(8,128)S(1)} %cholesky.272), custom_call_target="Cholesky" | custom-call | tf_op jit(solution)/shard_map/jit(cholesky)/cholesky | solution.py:96
  323.4 9.8 %custom-call.33 = f32[1,128,128]{1,2,0:T(8,128)S(1)} custom-call(f32[1,128,128]{2,1,0:T(8,128)S(1)} %get-tuple-element.120), custom_call_target="InvertDiagBlocksLowerTriangular" | custom-call | tf_op jit(solution)/shard_map/jit(cholesky)/cholesky | solution.py:96
  334.7 11.9 %cholesky.253 = f32[128,128]{1,0:T(8,128)S(1)} custom-call(f32[128,128]{1,0:T(8,128)S(1)} %convolution_subtract_fusion.5), custom_call_target="Cholesky" | custom-call | tf_op jit(solution)/shard_map/jit(cholesky)/cholesky | solution.py:96
  351.3 8.0 %while.9 = (s32[]{:T(128)}, f32[512,512]{1,0:T(8,128)S(1)}, s32[4,2]{0,1:T(2,128)S(1)}, f32[4,128,128]{2,1,0:T(8,128)S(1)}, s32[]{:T(128)}) while((s32[]{:T(128)}, f32[512,512]{1,0:T(8,128)S(1)}, s32[4,2]{0,1:T(2,128)S(1)}, f32[4,128,128]{2,1,0:T(8,128)S(1)}, s32[]{:T(128)}) %tuple.63), condition=%wide.while_cond.8, body=%wide.while_body.8.sunk | while | flops 2 | bytes 131181 | solution.py:97
  351.9 1.4 bitcast_dynamic-update-slice_fusion.2
  353.9 1.4 bitcast_dynamic-update-slice_fusion.2
  356.0 1.4 bitcast_dynamic-update-slice_fusion.2
  358.0 1.4 bitcast_dynamic-update-slice_fusion.2
  359.4 39.3 %custom-call.34 = f32[4,128,128]{1,2,0:T(8,128)S(1)} custom-call(f32[4,128,128]{2,1,0:T(8,128)S(1)} %get-tuple-element.106), custom_call_target="InvertDiagBlocksLowerTriangular" | custom-call | tf_op jit(solution)/shard_map/jit(_solve_triangular)/triangular_solve | solution.py:97
  401.9 2.4 multiply_add_fusion
  (75 shorter events, 20.4 us)
Async XLA Ops:
  7.2 68.6 %all-gather.3.cloned.1.call-start = ((), (), s32[]{:S(2)}) async-start(), calls=%async_computation.1 | async-start | bytes 3686400 | tf_op jit(solution)/shard_map/all_gather | solution.py:71
  7.9 142.6 %all-reduce.7.cloned.1.call-start = ((), (), s32[]{:S(2)}) async-start(), calls=%async_computation.2 | async-start | bytes 6553600 | tf_op jit(solution)/shard_map/psum | solution.py:86
  54.4 1.1 copy-start.2
  81.0 0.9 copy-start.3
  81.0 91.2 %all-gather.5.cloned.1.call-start = ((), (), s32[]{:S(2)}) async-start(), calls=%async_computation.3 | async-start | bytes 2048000 | tf_op jit(solution)/shard_map/all_gather | solution.py:68
  81.8 164.2 %all-reduce.9.cloned.1.call-start = ((), (), s32[]{:S(2)}) async-start(), calls=%async_computation.5 | async-start | bytes 327680 | tf_op jit(solution)/shard_map/psum | solution.py:39
  113.8 58.4 %copy-start = (bf16[320,640]{1,0:T(8,128)(2,1)S(1)}, bf16[320,640]{1,0:T(8,128)(2,1)}, u32[]{:S(2)}) copy-start(bf16[320,640]{1,0:T(8,128)(2,1)} %param.20) | copy-start | bytes 1228804
  163.3 238.6 %reduce-scatter.2.cloned.1.call-start = ((), (), s32[]{:S(2)}) async-start(), calls=%async_computation.4 | async-start | bytes 7372800 | tf_op jit(solution)/shard_map/reduce_scatter | solution.py:75
  263.1 1.0 copy-start.1
Sparse Core Ops, SparseCore 0:
  10.2 65.5 all-gather.2
  81.1 69.3 all-reduce.6
  152.1 20.0 all-gather.4
  176.0 69.9 all-reduce.8
  249.5 122.0 reduce-scatter.1
where the time goes:
time: 419 us; the launch traced here: 411 us
  waiting for transfers between devices  132 us (32%)
  other arithmetic  126 us (30%)
  blocking collectives  91.2 us (22%)
  matrix products  24.1 us (6%)
  local copies, waits for them, and re-layouts  19.6 us (5%)
  between operations  17.9 us (4%)
    another operation x14, other arithmetic, on_device(): factor_lower = jnp.linalg.cholesky(gram_full)  78.8 us
    psum x1, waiting for transfers between devices, lower_gram(): tile_sums = lax.psum(packed, 'shard')  65.4 us
    psum x1, blocking collectives, on_device(): lax.psum(jnp.sum(gradient_wide * gradient_wide), ('role', 'shard'))  44 us
    another operation x3, other arithmetic, on_device(): jax.scipy.linalg.solve_triangular(factor_lower, power_row.T, lower=True)  39.4 us
    psum x1, waiting for transfers between devices, on_device(): lax.psum((1.0 - smoothing) * squared * left_part + smoothing * placed, 'r...  36.7 us
    all_gather x1, blocking collectives, on_device(): lax.all_gather(basis_old, 'shard', axis=0, tiled=True).astype(jnp.float32)  31.9 us
    all_gather x1, waiting for transfers between devices, on_device(): lax.all_gather(gradient, 'shard', axis=0, tiled=True)  20.1 us
    all_gather x1, waiting for transfers between devices, on_device(): grad_row = lax.all_gather(gradient, 'role', axis=1, tiled=True)  8.91 us
  transfers between devices with their start and end apart: 5, of which 4 were waited for; matrix products, arithmetic and copies ran while one was open for 39% of the time, Pallas kernels for 0%

commit v1 on v0

--- a/solution.py
+++ b/solution.py
@@ -1,11 +1,102 @@
 import jax
 import jax.numpy as jnp
 from jax import lax
+from jax.experimental import pallas as pl
+from jax.experimental.pallas import tpu as pltpu
 from jax.sharding import PartitionSpec as P
 
 smoothing = 0.95
 clip_ratio = 4.0
 epsilon_value = 1e-06
+
+
+HI = lax.Precision.HIGHEST
+BLOCK, PANEL = 128, 8
+
+def factor_block(t_ref):
+    w = PANEL
+    sub = lax.broadcasted_iota(jnp.int32, (w, 128), 0)
+    full = lambda v: jnp.broadcast_to(v, (w, 128))
+    for p in range(BLOCK // w):
+        c0 = p * w
+        left, right = t_ref[c0:c0 + w, 0:128], t_ref[c0:c0 + w, 128:256]
+        cols = [full(left[:, c0 + k:c0 + k + 1]) for k in range(w)]
+        e = {(i, k): full(cols[k][i:i + 1, :]) for i in range(w) for k in range(i + 1)}
+        l, inv, rs = {}, [], []
+        for j in range(w):
+            r = 1.0 / e[j, j]
+            inv.append(r); rs.append(lax.rsqrt(e[j, j]))
+            for i in range(j + 1, w):
+                l[i, j] = e[i, j] * r
+            for i in range(j + 1, w):
+                for k in range(j + 1, i + 1):
+                    e[i, k] = e[i, k] - l[i, j] * e[k, j]
+        li = {}
+        for k in range(w):
+            for i in range(k + 1, w):
+                acc = l[i, k]
+                for m in range(k + 1, i):
+                    acc = acc + l[i, m] * li[m, k]
+                li[i, k] = -acc
+        def pick(vals):
+            out = jnp.zeros((w, 128), jnp.float32)
+            for i, v in vals.items():
+                out = jnp.where(sub == i, v, out)
+            return out
+        zl, zr = left, right
+        for k in range(w - 1):
+            coef = pick({i: li[i, k] for i in range(k + 1, w)})
+            zl = zl + coef * full(left[k:k + 1, :])
+            zr = zr + coef * full(right[k:k + 1, :])
+        dinv = pick(dict(enumerate(inv)))
+        ul, ur = dinv * zl, dinv * zr
+        vl, vr = ul, ur
+        for k in range(1, w):
+            coef = pick({i: li[k, i] for i in range(k)})
+            vl = vl + coef * full(ul[k:k + 1, :])
+            vr = vr + coef * full(ur[k:k + 1, :])
+        vlb = [full(vl[k:k + 1, :]) for k in range(w)]
+        vrb = [full(vr[k:k + 1, :]) for k in range(w)]
+        for q in range(p + 1, BLOCK // w):
+            rows = slice(q * w, q * w + w)
+            al, ar = t_ref[rows, 0:128], t_ref[rows, 128:256]
+            nl, nr = al, ar
+            for k in range(w):
+                a = full(al[:, c0 + k:c0 + k + 1])
+                nl = nl - a * vlb[k]
+                nr = nr - a * vrb[k]
+            t_ref[rows, 0:128] = nl
+            t_ref[rows, 128:256] = nr
+        scale = pick(dict(enumerate(rs)))
+        t_ref[c0:c0 + w, 0:128] = scale * zl
+        t_ref[c0:c0 + w, 128:256] = scale * zr
+
+def chol_kernel(g_ref, o_ref, m_ref, t_ref):
+    n = g_ref.shape[0]
+    nb = n // BLOCK
+    m_ref[:, :n] = g_ref[...]
+    m_ref[:, n:] = (lax.broadcasted_iota(jnp.int32, (n, n), 0) == lax.broadcasted_iota(jnp.int32, (n, n), 1)).astype(jnp.float32)
+    eye = (lax.broadcasted_iota(jnp.int32, (BLOCK, BLOCK), 0) == lax.broadcasted_iota(jnp.int32, (BLOCK, BLOCK), 1)).astype(jnp.float32)
+    @pl.loop(0, nb)
+    def _(b):
+        r0 = pl.multiple_of(b * BLOCK, BLOCK)
+        t_ref[:, 0:BLOCK] = m_ref[pl.ds(r0, BLOCK), pl.ds(r0, BLOCK)]
+        t_ref[:, BLOCK:] = eye
+        factor_block(t_ref)
+        for c in range(nb):
+            @pl.when(b == c)
+            def _():
+                lo, hi = c * BLOCK, n + (c + 1) * BLOCK
+                rows = jnp.dot(t_ref[:, BLOCK:], m_ref[lo:lo + BLOCK, lo:hi], precision=HI, preferred_element_type=jnp.float32)
+                m_ref[lo:lo + BLOCK, lo:hi] = rows
+                if c + 1 < nb:
+                    m_ref[lo + BLOCK:, lo + BLOCK:hi] -= lax.dot_general(rows[:, BLOCK:n - lo], rows[:, BLOCK:], (((0,), (0,)), ((), ())), precision=HI, preferred_element_type=jnp.float32)
+    o_ref[...] = m_ref[:, n:]
+
+def inverse_factor(gram):
+    n = gram.shape[0]
+    return pl.pallas_call(chol_kernel, out_shape=jax.ShapeDtypeStruct((n, n), jnp.float32),
+        scratch_shapes=[pltpu.VMEM((n, 2 * n), jnp.float32), pltpu.VMEM((BLOCK, 2 * BLOCK), jnp.float32)])(gram)
 
 
 def lower_gram(power_row, role_count, role_at):
@@ -93,9 +184,11 @@
     )
     power_row = lax.all_gather(power_block, "role", axis=1, tiled=True)
     gram_full = lower_gram(power_row, role_count, role_at)
-    factor_lower = jnp.linalg.cholesky(gram_full)
-    solved = jax.scipy.linalg.solve_triangular(factor_lower, power_row.T, lower=True)
-    left_basis = lax.dynamic_slice_in_dim(solved, vec_start, vec_count, 0).T
+    inverse = inverse_factor(gram_full)
+    mine = lax.dynamic_slice_in_dim(inverse, vec_start, vec_count, 0)
+    left_basis = lax.dot_general(
+        power_row, mine, (((1,), (1,)), ((), ())), precision=HI, preferred_element_type=jnp.float32
+    )
     return (left_stat, right_stat, left_basis)
 
 

time: 419 us -> 380 us (0.907); the launches traced: 411 us -> 380 us
  other arithmetic: 126 us -> 7.45 us
  waiting for transfers between devices: 132 us -> 200 us
  Pallas kernels: 0 us -> 24.1 us
  matrix products: 24.1 us -> 18.5 us
  local copies, waits for them, and re-layouts: 19.6 us -> 23.8 us
    another operation x17 -> x0, other arithmetic: 118 us -> none  [the longest x14 78.8 us: on_device(): factor_lower = jnp.linalg.cholesky(gram_full)]
    reduce_scatter x1, waiting for transfers between devices: 0.01 us -> 67.2 us  [on_device(): lax.psum_scatter(lax.dot_general(grad_row, gradient, (((0,), (0,)), ((),...]
    pallas_call x0 -> x1, Pallas kernels: none -> 24.1 us  [inverse_factor(): pl.pallas_call(chol_kernel, out_shape=jax.ShapeDtypeStruct((n, n), jnp.fl...]
    another operation x17 -> x0, local copies, waits for them, and re-layouts: 8.09 us -> none
    another operation x13 -> x0, matrix products: 7.94 us -> none  [the longest x6 5.5 us: on_device(): factor_lower = jnp.linalg.cholesky(gram_full)]
    scatter x4, local copies, waits for them, and re-layouts: 3.68 us -> 10.4 us  [lower_gram(): lower_part.at[other * tile_size:(other + 1) * tile_size, :tail]]
    scatter x4, local copies, waits for them, and re-layouts: 1.74 us -> 7.61 us  [lower_gram(): lower_part.at[member * tile_size:head, :head].set(packed_row[:, :head])]
  transfers between devices with their start and end apart: 5 -> 5, of which waited for: 4 -> 5; matrix products, arithmetic and copies ran while one was open for 39% -> 11% of each run, Pallas kernels for 0% -> 6%
where the time goes in v1:
time: 380 us
  waiting for transfers between devices  200 us (53%)
  blocking collectives  91.2 us (24%)
  Pallas kernels  24.1 us (6%)
  local copies, waits for them, and re-layouts  23.8 us (6%)
  matrix products  18.5 us (5%)
  between operations  14.7 us (4%)
  other arithmetic  7.45 us (2%)
    reduce_scatter x1, waiting for transfers between devices, on_device(): lax.psum_scatter(lax.dot_general(grad_row, gradient, (((0,), (0,)), ((),...  67.2 us
    psum x1, waiting for transfers between devices, lower_gram(): tile_sums = lax.psum(packed, 'shard')  65.4 us
    psum x1, blocking collectives, on_device(): lax.psum(jnp.sum(gradient_wide * gradient_wide), ('role', 'shard'))  44 us
    psum x1, waiting for transfers between devices, on_device(): lax.psum((1.0 - smoothing) * squared * left_part + smoothing * placed, 'r...  36.7 us
    all_gather x1, blocking collectives, on_device(): lax.all_gather(basis_old, 'shard', axis=0, tiled=True).astype(jnp.float32)  31.9 us
    pallas_call x1, Pallas kernels, inverse_factor(): pl.pallas_call(chol_kernel, out_shape=jax.ShapeDtypeStruct((n, n), jnp.fl...  24.1 us
    all_gather x1, waiting for transfers between devices, on_device(): lax.all_gather(gradient, 'shard', axis=0, tiled=True)  20.1 us
    scatter x4, local copies, waits for them, and re-layouts, lower_gram(): lower_part.at[other * tile_size:(other + 1) * tile_size, :tail]  10.4 us
  transfers between devices with their start and end apart: 5, of which 5 were waited for; matrix products, arithmetic and copies ran while one was open for 11% of the time, Pallas kernels for 6%

profile of v1, /device:TPU:0, one launch (start us, length us, event | category | flops | bytes accessed | tf_op | source)
XLA Modules:
  0.0 379.7 jit_solution(3597753432704722307)
XLA Ops:
  7.2 0.7 all-gather.3.cloned.1.call-update
  7.9 1.8 multiply_reduce_fusion
  9.8 44.0 %psum.21 = f32[]{:T(128)} all-reduce(f32[]{:T(128)} %multiply_reduce_fusion), channel_id=1, replica_groups=mesh['role'=4,'shard'=8] {'role','shard'}, use_global_device_ids=true, to_apply=%region_1.0 | all-reduce | flops 1 | bytes 8 | tf_op jit(solution)/shard_map/psum | solution.py:154
  54.8 0.8 copy-done.1
  55.7 20.1 %all-gather.3.cloned.1.call-done = bf16[2560,640]{1,0:T(8,128)(2,1)} async-done(((bf16[320,640]{1,0:T(8,128)(2,1)}), bf16[2560,640]{1,0:T(8,128)(2,1)}) %all-gather.3.cloned.1.call-update) | async-done | bytes 3276816 | tf_op jit(solution)/shard_map/all_gather | solution.py:162
  75.8 5.2 %fusion = f32[320,2560]{1,0:T(8,128)} fusion(bf16[320,640]{1,0:T(8,128)(2,1)} %param.20, bf16[2560,640]{1,0:T(8,128)(2,1)} %all-gather.3.cloned.1.call-done, f32[320,2560]{1,0:T(8,128)S(1)} %constant_dynamic-update-slice_fusion, f32[]{:T(128)S(6)} %mul.51), kind=kOutput, calls=%fused_computation.1 | convolution fusion | flops 1051033600 | bytes 10240004 | tf_op jit(solution)/shard_map/dot_general | solution.py:160
  81.0 0.7 all-gather.5.cloned.1.call-update
  81.9 31.9 %all_gather.17 = bf16[2560,128]{1,0:T(8,128)(2,1)S(1)} all-gather(bf16[320,128]{1,0:T(8,128)(2,1)S(1)} %copy-done.3), channel_id=1, replica_groups=mesh['role'=4,'shard'=8] {'shard'}, dimensions={0}, use_global_device_ids=true | all-gather | bytes 737280 | tf_op jit(solution)/shard_map/all_gather | solution.py:182
  113.8 36.7 %all-reduce.6.cloned.1.call-done = f32[320,2560]{1,0:T(8,128)} async-done(((f32[320,2560]{1,0:T(8,128)}), f32[320,2560]{1,0:T(8,128)}) %all-reduce.6.cloned.1.call-update) | async-done | bytes 3276816 | tf_op jit(solution)/shard_map/psum | solution.py:177
  150.5 3.5 fusion.13
  154.0 7.2 %all_gather.18 = f32[320,512]{1,0:T(8,128)S(1)} all-gather(f32[320,128]{1,0:T(8,128)S(1)} %fusion.13), channel_id=1, replica_groups=mesh['role'=4,'shard'=8] {'role'}, dimensions={1}, use_global_device_ids=true | all-gather | bytes 819200 | tf_op jit(solution)/shard_map/all_gather | solution.py:185
  161.2 0.6 fusion.5
  161.8 0.6 fusion.7
  162.4 0.8 fusion.4
  163.3 8.9 %all-gather.5.cloned.1.call-done = bf16[320,2560]{1,0:T(8,128)(2,1)} async-done(((bf16[320,640]{1,0:T(8,128)(2,1)}), bf16[320,2560]{1,0:T(8,128)(2,1)}) %all-gather.5.cloned.1.call-update) | async-done | bytes 1638416 | tf_op jit(solution)/shard_map/all_gather | solution.py:159
  172.2 6.3 %fusion.12 = f32[2560,640]{1,0:T(8,128)} fusion(bf16[320,2560]{1,0:T(8,128)(2,1)} %all-gather.5.cloned.1.call-done, bf16[320,640]{1,0:T(8,128)(2,1)S(1)} %copy-done), kind=kOutput, calls=%fused_computation.23 | convolution fusion | flops 1048576000 | bytes 8601600 | tf_op jit(solution)/shard_map/dot_general | solution.py:167
  178.5 2.1 constant_dynamic-slice_fusion
  180.6 65.4 %all-reduce.8.cloned.1.call-done = f32[64,576]{1,0:T(8,128)} async-done(((f32[64,576]{1,0:T(8,128)}), f32[64,576]{1,0:T(8,128)}) %all-reduce.8.cloned.1.call-update) | async-done | bytes 147472 | tf_op jit(solution)/shard_map/psum | solution.py:130
  246.0 8.1 %all_gather.19 = f32[256,576]{1,0:T(8,128)S(1)} all-gather(f32[64,576]{1,0:T(8,128)} %all-reduce.8.cloned.1.call-done), channel_id=1, replica_groups=mesh['role'=4,'shard'=8] {'role'}, dimensions={0}, use_global_device_ids=true | all-gather | bytes 737280 | tf_op jit(solution)/shard_map/all_gather | solution.py:131
  255.4 1.6 scatter.29
  257.0 2.0 scatter.30
  259.1 2.2 scatter.31
  261.3 2.2 scatter.34
  263.5 3.7 scatter.35
  267.2 3.2 scatter.36
  270.4 2.9 scatter.39
  273.4 1.4 copy.18
  274.8 2.6 bitcast_add_fusion.g_ref
  277.4 24.1 %shard_map.67 = f32[512,512]{1,0:T(8,128)} custom-call(f32[512,512]{1,0:T(8,128)} %bitcast_add_fusion.g_ref), custom_call_target="tpu_custom_call" | custom-call | tf_op jit(solution)/shard_map/pallas_call | solution.py:98
  301.5 2.3 fusion.2
  303.8 67.2 %reduce-scatter.2.cloned.1.call-done = f32[320,640]{1,0:T(8,128)} async-done(((f32[2560,640]{1,0:T(8,128)}), f32[320,640]{1,0:T(8,128)}) %reduce-scatter.2.cloned.1.call-update) | async-done | bytes 819216 | tf_op jit(solution)/shard_map/reduce_scatter | solution.py:166
  371.0 2.1 multiply_add_fusion
  (37 shorter events, 2.1 us)
Async XLA Ops:
  7.2 68.6 %all-gather.3.cloned.1.call-start = ((), (), s32[]{:S(2)}) async-start(), calls=%async_computation.1 | async-start | bytes 3686400 | tf_op jit(solution)/shard_map/all_gather | solution.py:162
  7.9 142.6 %all-reduce.6.cloned.1.call-start = ((), (), s32[]{:S(2)}) async-start(), calls=%async_computation.2 | async-start | bytes 6553600 | tf_op jit(solution)/shard_map/psum | solution.py:177
  54.4 1.1 copy-start.1
  81.0 0.9 copy-start.3
  81.0 91.2 %all-gather.5.cloned.1.call-start = ((), (), s32[]{:S(2)}) async-start(), calls=%async_computation.3 | async-start | bytes 2048000 | tf_op jit(solution)/shard_map/all_gather | solution.py:159
  81.7 164.2 %all-reduce.8.cloned.1.call-start = ((), (), s32[]{:S(2)}) async-start(), calls=%async_computation.5 | async-start | bytes 327680 | tf_op jit(solution)/shard_map/psum | solution.py:130
  113.8 58.4 %copy-start = (bf16[320,640]{1,0:T(8,128)(2,1)S(1)}, bf16[320,640]{1,0:T(8,128)(2,1)}, u32[]{:S(2)}) copy-start(bf16[320,640]{1,0:T(8,128)(2,1)} %param.20) | copy-start | bytes 1228804
  163.2 207.8 %reduce-scatter.2.cloned.1.call-start = ((), (), s32[]{:S(2)}) async-start(), calls=%async_computation.4 | async-start | bytes 7372800 | tf_op jit(solution)/shard_map/reduce_scatter | solution.py:166
  274.8 96.2 %copy-start.2 = (f32[320,640]{1,0:T(8,128)S(1)}, f32[320,640]{1,0:T(8,128)}, u32[]{:S(2)}) copy-start(f32[320,640]{1,0:T(8,128)} %param.22) | copy-start | bytes 2457604
Sparse Core Ops, SparseCore 0:
  10.2 65.5 all-gather.2
  81.1 69.3 all-reduce.5
  152.1 20.0 all-gather.4
  176.0 69.9 all-reduce.7
  249.4 121.5 reduce-scatter.1

commit v2 on v1

v2 whole, which is shorter than its diff:
```python
import functools

import jax
import jax.numpy as jnp
from jax import lax
from jax.experimental import pallas as pl
from jax.experimental.pallas import tpu as pltpu
from jax.sharding import PartitionSpec as P

smoothing = 0.95
clip_ratio = 4.0
epsilon_value = 1e-06
HI = lax.Precision.HIGHEST
BLOCK, PANEL = 128, 8


def factor_block(t_ref):
    w = PANEL
    sub = lax.broadcasted_iota(jnp.int32, (w, 128), 0)
    full = lambda v: jnp.broadcast_to(v, (w, 128))
    for p in range(BLOCK // w):
        c0 = p * w
        left, right = t_ref[c0:c0 + w, 0:128], t_ref[c0:c0 + w, 128:256]
        cols = [full(left[:, c0 + k:c0 + k + 1]) for k in range(w)]
        e = {(i, k): full(cols[k][i:i + 1, :]) for i in range(w) for k in range(i + 1)}
        l, inv, rs = {}, [], []
        for j in range(w):
            r = 1.0 / e[j, j]
            inv.append(r); rs.append(lax.rsqrt(e[j, j]))
            for i in range(j + 1, w):
                l[i, j] = e[i, j] * r
            for i in range(j + 1, w):
                for k in range(j + 1, i + 1):
                    e[i, k] = e[i, k] - l[i, j] * e[k, j]
        li = {}
        for k in range(w):
            for i in range(k + 1, w):
                acc = l[i, k]
                for m in range(k + 1, i):
                    acc = acc + l[i, m] * li[m, k]
                li[i, k] = -acc

        def pick(vals):
            out = jnp.zeros((w, 128), jnp.float32)
            for i, v in vals.items():
                out = jnp.where(sub == i, v, out)
            return out

        zl, zr = left, right
        for k in range(w - 1):
            coef = pick({i: li[i, k] for i in range(k + 1, w)})
            zl = zl + coef * full(left[k:k + 1, :])
            zr = zr + coef * full(right[k:k + 1, :])
        dinv = pick(dict(enumerate(inv)))
        ul, ur = dinv * zl, dinv * zr
        vl, vr = ul, ur
        for k in range(1, w):
            coef = pick({i: li[k, i] for i in range(k)})
            vl = vl + coef * full(ul[k:k + 1, :])
            vr = vr + coef * full(ur[k:k + 1, :])
        vlb = [full(vl[k:k + 1, :]) for k in range(w)]
        vrb = [full(vr[k:k + 1, :]) for k in range(w)]
        for q in range(p + 1, BLOCK // w):
            rows = slice(q * w, q * w + w)
            al, ar = t_ref[rows, 0:128], t_ref[rows, 128:256]
            nl, nr = al, ar
            for k in range(w):
                a = full(al[:, c0 + k:c0 + k + 1])
                nl = nl - a * vlb[k]
                nr = nr - a * vrb[k]
            t_ref[rows, 0:128] = nl
            t_ref[rows, 128:256] = nr
        scale = pick(dict(enumerate(rs)))
        t_ref[c0:c0 + w, 0:128] = scale * zl
        t_ref[c0:c0 + w, 128:256] = scale * zr


def strip_of(order, roles, role, which):
    height = order // (2 * roles)
    strip = role if which == 0 else 2 * roles - 1 - role
    return strip * height, height, strip * height // BLOCK * BLOCK


def packed_width(order, roles):
    return max(
        sum(order - strip_of(order, roles, role, which)[2] for which in (0, 1)) for role in range(roles)
    )


def gram_kernel(roles, power_ref, out_ref):
    order = power_ref.shape[1]
    here = lax.axis_index("role")
    for role in range(roles):

        @pl.when(here == role)
        def _():
            at = 0
            for which in (0, 1):
                row, height, first = strip_of(order, roles, role, which)
                out_ref[:, at : at + order - first] = lax.dot_general(
                    power_ref[:, row : row + height],
                    power_ref[:, first:],
                    (((0,), (0,)), ((), ())),
                    precision=HI,
                    preferred_element_type=jnp.float32,
                )
                at += order - first
            if at < out_ref.shape[1]:
                out_ref[:, at:] = jnp.zeros((out_ref.shape[0], out_ref.shape[1] - at), jnp.float32)


def basis_kernel(roles, packed_ref, power_ref, out_ref, m_ref, t_ref):
    n = power_ref.shape[1]
    nb = n // BLOCK
    for role in range(roles):
        at = 0
        for which in (0, 1):
            row, height, first = strip_of(n, roles, role, which)
            m_ref[row : row + height, first:n] = packed_ref[role, :, at : at + n - first]
            at += n - first
    m_ref[:, n:] = (
        lax.broadcasted_iota(jnp.int32, (n, n), 0) == lax.broadcasted_iota(jnp.int32, (n, n), 1)
    ).astype(jnp.float32)

    @pl.loop(0, nb)
    def _(b):
        start = pl.multiple_of(b * BLOCK, BLOCK)
        t_ref[:, :BLOCK] = m_ref[pl.ds(start, BLOCK), pl.ds(start, BLOCK)]
        t_ref[:, BLOCK:] = (
            lax.broadcasted_iota(jnp.int32, (BLOCK, BLOCK), 0)
            == lax.broadcasted_iota(jnp.int32, (BLOCK, BLOCK), 1)
        ).astype(jnp.float32)
        factor_block(t_ref)
        for c in range(nb):

            @pl.when(b == c)
            def _():
                lo, hi = c * BLOCK, n + (c + 1) * BLOCK
                rows = jnp.dot(
                    t_ref[:, BLOCK:],
                    m_ref[lo : lo + BLOCK, lo:hi],
                    precision=HI,
                    preferred_element_type=jnp.float32,
                )
                m_ref[lo : lo + BLOCK, lo:hi] = rows
                if c + 1 < nb:
                    m_ref[lo + BLOCK :, lo + BLOCK : hi] -= lax.dot_general(
                        rows[:, BLOCK : n - lo],
                        rows[:, BLOCK:],
                        (((0,), (0,)), ((), ())),
                        precision=HI,
                        preferred_element_type=jnp.float32,
                    )

    width = out_ref.shape[1]
    mine = pl.multiple_of(lax.axis_index("role") * width, BLOCK)
    out_ref[...] = lax.dot_general(
        power_ref[...],
        m_ref[pl.ds(mine, width), n:],
        (((1,), (1,)), ((), ())),
        precision=HI,
        preferred_element_type=jnp.float32,
    )


def split_three(value):
    high = lax.reduce_precision(value, 8, 7)
    rest = value - high
    middle = lax.reduce_precision(rest, 8, 7)
    return [v.astype(jnp.bfloat16) for v in (high, middle, rest - middle)]


def step(gradient, left_old, right_old, basis_old):
    rows, cols = gradient.shape
    vec = basis_old.shape[1]
    shards, roles = lax.axis_size("shard"), lax.axis_size("role")
    shard_at, role_at = lax.axis_index("shard"), lax.axis_index("role")
    order_size, order = rows * shards, vec * roles
    line = shards // 2
    line_at, side_at = shard_at // 2, shard_at % 2
    core_at = role_at % 2
    half_at = role_at // 2

    def other_side(value, first=0, last=line - 1):
        pairs = [(2 * z + x, 2 * z + 1 - x) for z in range(first, last + 1) for x in (0, 1)]
        return lax.ppermute(value, "shard", pairs)

    def along(value, first, last, by):
        pairs = [(2 * z + x, 2 * (z + by) + x) for z in range(first, last + 1) for x in (0, 1)]
        return lax.ppermute(value, "shard", pairs)

    def around(value, by):
        pairs = [(2 * z + x, 2 * ((z + by) % line) + x) for z in range(line) for x in (0, 1)]
        return lax.ppermute(value, "shard", pairs)

    def flip(value, axis, size, bit):
        return lax.ppermute(value, axis, [(i, i ^ bit) for i in range(size)])

    other_core = lambda value: flip(value, "role", roles, 1)
    other_half = lambda value: flip(value, "role", roles, 2)

    wide = gradient.astype(jnp.float32)
    parts = split_three(jnp.sum(wide * wide))
    tail = jnp.concatenate(
        [jnp.broadcast_to(v, (1, vec)) for v in parts] + [jnp.zeros((16 - len(parts), vec), jnp.bfloat16)]
    )
    message = jnp.concatenate([basis_old, tail])
    height = message.shape[0]
    beside = other_side(message)
    pair = jnp.where(side_at == 0, jnp.stack([message, beside]), jnp.stack([beside, message]))
    mine = lax.dynamic_update_slice(
        jnp.zeros((line, 2, height, vec), jnp.bfloat16), pair[None], (line_at, 0, 0, 0)
    )
    for by in range(1, line):
        got = around(pair, by)
        mine = lax.dynamic_update_slice(mine, got[None], ((line_at - by) % line, 0, 0, 0))
    yours = other_half(mine)
    two = jnp.where(
        half_at == 0, jnp.stack([mine, yours], axis=3), jnp.stack([yours, mine], axis=3)
    )
    their = other_core(two)
    four = jnp.where(
        core_at == 0, jnp.stack([two, their], axis=4), jnp.stack([their, two], axis=4)
    ).reshape(shards, height, order)
    sums = four[:, rows : rows + len(parts)].reshape(shards, len(parts), roles, vec)[..., 0]
    squares = jnp.sum(jnp.sum(sums.astype(jnp.float32), axis=1))
    factor = jnp.minimum(
        1.0, clip_ratio * jnp.sqrt(jnp.float32(order_size)) / jnp.sqrt(squares + epsilon_value)
    )
    weight = (1.0 - smoothing) * (factor * factor)
    basis = four[:, :rows]

    gathered = jnp.zeros((shards + 1, rows, cols), jnp.bfloat16)

    def put(gathered, value, z, x, valid):
        place = jnp.where(valid, 2 * z + x, shards)
        return lax.dynamic_update_slice(gathered, value[None], (place, 0, 0))

    gathered = put(gathered, gradient, line_at, side_at, True)
    low = high = gradient
    gathered = put(gathered, other_side(gradient), line_at, 1 - side_at, True)
    for by in range(1, line):
        low = along(low, by - 1, line - 2, 1)
        high = along(high, 1, line - by, -1)
        low_side = other_side(low, by, line - 1)
        high_side = other_side(high, 0, line - 1 - by)
        for value, z, x, valid in (
            (low, line_at - by, side_at, line_at >= by),
            (high, line_at + by, side_at, line_at + by < line),
            (low_side, line_at - by, 1 - side_at, line_at >= by),
            (high_side, line_at + by, 1 - side_at, line_at + by < line),
        ):
            gathered = put(gathered, value, z, x, valid)
    columns = gathered[:shards].reshape(order_size, cols)

    turned = lax.dot_general(
        columns,
        basis.reshape(order_size, order),
        (((0,), (0,)), ((), ())),
        preferred_element_type=jnp.float32,
    )
    per_role = cols // rows
    old_part = jnp.dot(
        left_old,
        lax.dynamic_slice_in_dim(basis, role_at * per_role, per_role, 0)
        .reshape(cols, order)
        .astype(jnp.float32),
        precision=HI,
    )
    new_part = sum(
        jnp.dot(gradient, part, preferred_element_type=jnp.float32) for part in split_three(turned)
    )
    part = smoothing * old_part + weight * new_part
    half_rows = rows // 2
    keep = lax.dynamic_slice_in_dim(part, core_at * half_rows, half_rows, 0)
    send = lax.dynamic_slice_in_dim(part, (1 - core_at) * half_rows, half_rows, 0)
    keep = keep + other_core(send)
    keep = keep + other_half(keep)
    across = other_core(keep)
    power = jnp.where(
        core_at == 0, jnp.concatenate([keep, across]), jnp.concatenate([across, keep])
    )

    strip_height = order // (2 * roles)
    packed = pl.pallas_call(
        functools.partial(gram_kernel, roles),
        out_shape=jax.ShapeDtypeStruct((strip_height, packed_width(order, roles)), jnp.float32),
    )(power)
    bit = 1
    while bit < shards:
        packed = packed + flip(packed, "shard", shards, bit)
        bit *= 2
    yours = other_half(packed)
    two = jnp.where(half_at == 0, jnp.stack([packed, yours]), jnp.stack([yours, packed]))
    their = other_core(two)
    strips = jnp.where(
        core_at == 0, jnp.stack([two, their], axis=1), jnp.stack([their, two], axis=1)
    ).reshape(roles, *packed.shape)
    left_basis = pl.pallas_call(
        functools.partial(basis_kernel, roles),
        out_shape=jax.ShapeDtypeStruct((rows, vec), jnp.float32),
        scratch_shapes=[
            pltpu.VMEM((order, 2 * order), jnp.float32),
            pltpu.VMEM((BLOCK, 2 * BLOCK), jnp.float32),
        ],
    )(strips, power)

    def left_for(half, core):
        at = (2 * half + core) * per_role
        block = lax.dynamic_slice_in_dim(gathered, at, per_role, 0).reshape(cols, cols)
        return lax.dot_general(
            gradient, block, (((1,), (1,)), ((), ())), preferred_element_type=jnp.float32
        )

    away = left_for(1 - half_at, core_at) + other_core(left_for(1 - half_at, 1 - core_at))
    here = left_for(half_at, core_at) + other_core(left_for(half_at, 1 - core_at))
    left_stat = smoothing * left_old + weight * (here + other_half(away))

    owner_of = lambda shard: shard * rows // cols
    owner = owner_of(shard_at)
    slab = lax.dynamic_slice_in_dim(columns, shard_at * rows - owner * cols, rows, 1)
    flat = lambda role, shard: role * shards + shard
    crossed = lax.ppermute(
        slab, ("role", "shard"),
        [(flat(owner_of(s), s), flat(owner_of(s) ^ 2, s)) for s in range(shards)],
    )
    slab = jnp.where(role_at == owner, slab, crossed)
    beside = lax.ppermute(
        slab, ("role", "shard"),
        [(flat(owner_of(s) ^ k, s), flat(owner_of(s) ^ k ^ 1, s)) for s in range(shards) for k in (0, 2)],
    )
    slab = jnp.where((role_at ^ owner) & 1 == 0, slab, beside)
    right_gram = lax.dot_general(
        slab, columns, (((0,), (0,)), ((), ())), preferred_element_type=jnp.float32
    )
    right_stat = smoothing * right_old + weight * right_gram
    return (left_stat, right_stat, left_basis)


def solution(mesh):
    return jax.shard_map(
        step,
        mesh=mesh,
        in_specs=(P("shard", "role"), P("shard", "role"), P("shard", "role"), P("shard", "role")),
        out_specs=(P("shard", "role"), P("shard", "role"), P("shard", "role")),
        check_vma=False,
    )
```

time: 380 us -> 206 us (0.54)
  waiting for transfers between devices: 200 us -> 61.8 us
  blocking collectives: 91.2 us -> 0 us
  starting transfers between devices: 0.2 us -> 42.6 us
  local copies, waits for them, and re-layouts: 23.8 us -> 34.3 us
  between operations: 14.7 us -> 6.79 us
  other arithmetic: 7.45 us -> 12.1 us
    psum x2 -> x0, waiting for transfers between devices: 102 us -> none  [the longest x1 65.4 us: lower_gram(): tile_sums = lax.psum(packed, 'shard')]
    reduce_scatter x1 -> x0, waiting for transfers between devices: 67.2 us -> none  [on_device(): lax.psum_scatter(lax.dot_general(grad_row, gradient, (((0,), (0,)), ((),...]
    ppermute x0 -> x32, waiting for transfers between devices: none -> 61.8 us  [the longest x13 29.4 us: flip(): return lax.ppermute(value, axis, [(i, i ^ bit) for i in range(size)])]
    all_gather x3 -> x0, blocking collectives: 47.2 us -> none  [the longest x1 31.9 us: on_device(): lax.all_gather(basis_old, 'shard', axis=0, tiled=True).astype(jnp.float32)]
    psum x1 -> x0, blocking collectives: 44 us -> none  [on_device(): lax.psum(jnp.sum(gradient_wide * gradient_wide), ('role', 'shard'))]
    ppermute x0 -> x32, starting transfers between devices: none -> 42.6 us  [the longest x8 14.4 us: other_side(): return lax.ppermute(value, 'shard', pairs)]
    all_gather x2 -> x0, waiting for transfers between devices: 29 us -> none  [the longest x1 20.1 us: on_device(): lax.all_gather(gradient, 'shard', axis=0, tiled=True)]
    scatter x8 -> x0, local copies, waits for them, and re-layouts: 18 us -> none  [the longest x4 10.4 us: lower_gram(): lower_part.at[other * tile_size:(other + 1) * tile_size, :tail]]
  transfers between devices with their start and end apart: 5 -> 32, of which waited for: 5 -> 11; matrix products, arithmetic and copies ran while one was open for 11% -> 28% of each run, Pallas kernels for 6% -> 13%
where the time goes in v2:
time: 206 us; the launch traced here: 205 us
  waiting for transfers between devices  61.8 us (30%)
  starting transfers between devices  42.6 us (21%)
  local copies, waits for them, and re-layouts  34.3 us (17%)
  Pallas kernels  27.1 us (13%)
  matrix products  20.7 us (10%)
  other arithmetic  12.1 us (6%)
  between operations  6.79 us (3%)
    ppermute x13, waiting for transfers between devices, flip(): return lax.ppermute(value, axis, [(i, i ^ bit) for i in range(size)])  29.4 us
    pallas_call x1, Pallas kernels, step(): pl.pallas_call(functools.partial(basis_kernel, roles), out_shape=jax.Shap...  24.5 us
    ppermute x3, waiting for transfers between devices, around(): return lax.ppermute(value, 'shard', pairs)  17.2 us
    ppermute x8, starting transfers between devices, other_side(): return lax.ppermute(value, 'shard', pairs)  14.4 us
    dynamic_update_slice x14, local copies, waits for them, and re-layouts, put(): return lax.dynamic_update_slice(gathered, value[None], (place, 0, 0))  11.1 us
    ppermute x6, waiting for transfers between devices, along(): return lax.ppermute(value, 'shard', pairs)  10.6 us
    ppermute x6, starting transfers between devices, along(): return lax.ppermute(value, 'shard', pairs)  9.19 us
    dot_general x4, matrix products, left_for(): lax.dot_general(gradient, block, (((1,), (1,)), ((), ())), preferred_elem...  5.97 us
  transfers between devices with their start and end apart: 32, of which 11 were waited for; matrix products, arithmetic and copies ran while one was open for 28% of the time, Pallas kernels for 13%

profile of v2, /device:TPU:0, one launch (start us, length us, event | category | flops | bytes accessed | tf_op | source)
XLA Modules:
  0.0 205.4 jit_solution(6865667524706667777)
XLA Ops:
  0.6 1.9 multiply_reduce_fusion
  8.5 3.0 %collective-permute-start = (bf16[336,128]{1,0:T(8,128)(2,1)S(1)}, bf16[336,128]{1,0:T(8,128)(2,1)S(1)}, u32[]{:S(2)}, u32[]{:S(2)}) collective-permute-start(bf16[336,128]{1,0:T(8,128)(2,1)S(1)} %concatenate.51), channel_id=1, source_target_pairs={{0,1},{1,0},{2,3},{3,2},{4,5},{5,4},{6,7},{7,6},{8,9},{9,8},{10,11... | collective-permute-start | bytes 258056 | tf_op jit(solution)/shard_map/ppermute | solution.py:186
  11.6 4.0 %collective-permute-start.7 = (bf16[320,640]{1,0:T(8,128)(2,1)}, bf16[320,640]{1,0:T(8,128)(2,1)S(1)}, u32[]{:S(2)}, u32[]{:S(2)}) collective-permute-start(bf16[320,640]{1,0:T(8,128)(2,1)} %param.4), channel_id=1, source_target_pairs={{0,2},{1,3},{2,4},{3,5},{4,6},{5,7},{8,10},{9,11},{10,12},{11,13},... | collective-permute-start | bytes 1228808 | tf_op jit(solution)/shard_map/ppermute | solution.py:190
  17.0 2.7 %collective-permute-start.1 = (bf16[2,336,128]{2,1,0:T(8,128)(2,1)S(1)}, bf16[2,336,128]{2,1,0:T(8,128)(2,1)S(1)}, u32[]{:S(2)}, u32[]{:S(2)}) collective-permute-start(bf16[2,336,128]{2,1,0:T(8,128)(2,1)S(1)} %maximum_select_fusion.8), channel_id=1, source_target_pairs={{0,2},{1,3},{2,4},{3,5},{4,6},{5,7},{6,0},{7,1},{8,10},{9,11},{10,... | collective-permute-start | bytes 516104 | tf_op jit(solution)/shard_map/ppermute | solution.py:194
  19.7 2.1 %broadcast_in_dim.78 = bf16[9,320,640]{2,1,0:T(8,128)(2,1)} broadcast(bf16[]{:T(256)} %constant.86.clone.1), dimensions={} | broadcast | bytes 3686402 | tf_op jit(solution)/shard_map/broadcast_in_dim | solution.py:233
  22.6 2.6 %collective-permute-start.2 = (bf16[2,336,128]{2,1,0:T(8,128)(2,1)S(1)}, bf16[2,336,128]{2,1,0:T(8,128)(2,1)S(1)}, u32[]{:S(2)}, u32[]{:S(2)}) collective-permute-start(bf16[2,336,128]{2,1,0:T(8,128)(2,1)S(1)} %maximum_select_fusion.8), channel_id=1, source_target_pairs={{0,4},{1,5},{2,6},{3,7},{4,0},{5,1},{6,2},{7,3},{8,12},{9,13},{10,... | collective-permute-start | bytes 516104 | tf_op jit(solution)/shard_map/ppermute | solution.py:194
  25.3 10.4 %collective-permute-done.1 = bf16[2,336,128]{2,1,0:T(8,128)(2,1)S(1)} collective-permute-done((bf16[2,336,128]{2,1,0:T(8,128)(2,1)S(1)}, bf16[2,336,128]{2,1,0:T(8,128)(2,1)S(1)}, u32[]{:S(2)}, u32[]{:S(2)}) %collective-permute-start.1) | collective-permute-done | bytes 172064 | tf_op jit(solution)/shard_map/ppermute | solution.py:194
  35.8 6.3 %collective-permute-done.2 = bf16[2,336,128]{2,1,0:T(8,128)(2,1)S(1)} collective-permute-done((bf16[2,336,128]{2,1,0:T(8,128)(2,1)S(1)}, bf16[2,336,128]{2,1,0:T(8,128)(2,1)S(1)}, u32[]{:S(2)}, u32[]{:S(2)}) %collective-permute-start.2) | collective-permute-done | bytes 172064 | tf_op jit(solution)/shard_map/ppermute | solution.py:194
  45.6 3.4 %collective-permute-start.10 = (bf16[320,640]{1,0:T(8,128)(2,1)S(1)}, bf16[320,640]{1,0:T(8,128)(2,1)S(1)}, u32[]{:S(2)}, u32[]{:S(2)}) collective-permute-start(bf16[320,640]{1,0:T(8,128)(2,1)S(1)} %collective-permute-done.8), channel_id=1, source_target_pairs={{0,1},{1,0},{2,3},{3,2},{4,5},{5,4},{8,9},{9,8},{10,11},{11,10},{1... | collective-permute-start | bytes 1228808 | tf_op jit(solution)/shard_map/ppermute | solution.py:186
  54.1 7.8 %collective-permute-done.12 = bf16[320,640]{1,0:T(8,128)(2,1)S(1)} collective-permute-done((bf16[320,640]{1,0:T(8,128)(2,1)S(1)}, bf16[320,640]{1,0:T(8,128)(2,1)S(1)}, u32[]{:S(2)}, u32[]{:S(2)}) %collective-permute-start.12) | collective-permute-done | bytes 409632 | tf_op jit(solution)/shard_map/ppermute | solution.py:190
  61.9 3.4 %collective-permute-start.14 = (bf16[320,640]{1,0:T(8,128)(2,1)S(1)}, bf16[320,640]{1,0:T(8,128)(2,1)S(1)}, u32[]{:S(2)}, u32[]{:S(2)}) collective-permute-start(bf16[320,640]{1,0:T(8,128)(2,1)S(1)} %collective-permute-done.12), channel_id=1, source_target_pairs={{0,1},{1,0},{2,3},{3,2},{8,9},{9,8},{10,11},{11,10},{16,17},{17,16... | collective-permute-start | bytes 1228808 | tf_op jit(solution)/shard_map/ppermute | solution.py:186
  73.2 2.7 %collective-permute-done.16 = bf16[320,640]{1,0:T(8,128)(2,1)S(1)} collective-permute-done((bf16[320,640]{1,0:T(8,128)(2,1)S(1)}, bf16[320,640]{1,0:T(8,128)(2,1)S(1)}, u32[]{:S(2)}, u32[]{:S(2)}) %collective-permute-start.16) | collective-permute-done | bytes 409632 | tf_op jit(solution)/shard_map/ppermute | solution.py:190
  75.9 2.4 %collective-permute-start.18 = (bf16[320,640]{1,0:T(8,128)(2,1)S(1)}, bf16[320,640]{1,0:T(8,128)(2,1)S(1)}, u32[]{:S(2)}, u32[]{:S(2)}) collective-permute-start(bf16[320,640]{1,0:T(8,128)(2,1)S(1)} %collective-permute-done.16), channel_id=1, source_target_pairs={{0,1},{1,0},{8,9},{9,8},{16,17},{17,16},{24,25},{25,24}} | collective-permute-start | bytes 1228808 | tf_op jit(solution)/shard_map/ppermute | solution.py:186
  82.4 4.6 %collective-permute-done.18 = bf16[320,640]{1,0:T(8,128)(2,1)S(1)} collective-permute-done((bf16[320,640]{1,0:T(8,128)(2,1)S(1)}, bf16[320,640]{1,0:T(8,128)(2,1)S(1)}, u32[]{:S(2)}, u32[]{:S(2)}) %collective-permute-start.18) | collective-permute-done | bytes 409632 | tf_op jit(solution)/shard_map/ppermute | solution.py:186
  87.8 2.2 %slice.18 = bf16[8,320,640]{2,1,0:T(8,128)(2,1)S(1)} slice(bf16[9,320,640]{2,1,0:T(8,128)(2,1)} %bitcast_dynamic-update-slice_fusion), slice={[0:8], [0:320], [0:640]} | slice | bytes 6553600 | tf_op jit(solution)/shard_map/slice | solution.py:254
  92.8 3.4 %copy.25 = bf16[2560,320]{0,1:T(8,128)(2,1)} copy(bf16[2560,320]{1,0:T(8,128)(2,1)S(1)} %constant_dynamic-slice_fusion.1) | data formatting | bytes 3276800
  96.2 3.6 %collective-permute-start.22 = (bf16[2560,320]{0,1:T(8,128)(2,1)}, bf16[2560,320]{0,1:T(8,128)(2,1)}, u32[]{:S(2)}, u32[]{:S(2)}) collective-permute-start(bf16[2560,320]{0,1:T(8,128)(2,1)} %copy.25), channel_id=1, source_target_pairs={{0,16},{1,17},{10,26},{11,27},{20,4},{21,5},{30,14},{31,15}} | collective-permute-start | bytes 4915208 | tf_op jit(solution)/shard_map/ppermute | solution.py:323
  99.7 3.3 %maximum_select_fusion = bf16[4,2,336,2,2,128]{5,2,1,0,4,3:T(8,128)(2,1)S(1)} fusion(bf16[4,2,336,2,1,128]{5,2,1,0,4,3:T(8,128)(2,1)} %maximum_select_fusion.1, pred[]{:T(512)S(6)} %eq.24, bf16[4,2,336,2,128]{4,2,1,0,3:T(8,128)(2,1)} %collective-permute-done.5), kind=kLoop, calls=%fused_computation | loop fusion | flops 12386304 | bytes 5505025 | tf_op jit(solution)/shard_map/jit(_where)/select_n | solution.py:222
  103.1 2.8 %copy.19 = bf16[4,2,336,2,2,128]{5,4,3,2,1,0:T(2,128)(2,1)S(1)} copy(bf16[4,2,336,2,2,128]{5,2,1,0,4,3:T(8,128)(2,1)S(1)} %maximum_select_fusion) | data formatting | bytes 5505024 | tf_op jit(solution)/shard_map/jit(_where)/select_n | solution.py:222
  105.9 2.6 %select_n.275 = bf16[8,336,512]{2,1,0:T(8,128)(2,1)} reshape(bf16[4,2,336,2,2,128]{5,4,3,2,1,0:T(2,128)(2,1)S(1)} %copy.19) | data formatting | bytes 5505024 | tf_op jit(solution)/shard_map/jit(_where)/select_n | solution.py:222
  108.5 4.8 %convolution_bitcast_fusion = f32[640,512]{1,0:T(8,128)S(1)} fusion(bf16[9,320,640]{2,1,0:T(8,128)(2,1)} %bitcast_dynamic-update-slice_fusion, bf16[8,336,512]{2,1,0:T(8,128)(2,1)} %select_n.275), kind=kOutput, calls=%fused_computation.9 | convolution fusion | flops 1677721600 | bytes 7618560 | tf_op jit(solution)/shard_map/dot_general | solution.py:256
  122.9 2.2 %constant_dynamic-slice_fusion.5 = (bf16[2,320,640]{2,1,0:T(8,128)(2,1)S(1)}, bf16[2,320,640]{2,1,0:T(8,128)(2,1)S(1)}, bf16[2,320,640]{2,1,0:T(8,128)(2,1)S(1)}, bf16[2,320,640]{2,1,0:T(8,128)(2,1)S(1)}) fusion(bf16[9,320,640]{2,1,0:T(8,128)(2,1)} %bitcast_dynamic-update-slice_fusion, s32[]{:T(128)S(6)} %select_n.302, s32[]{:T(128)S(6)} %select_n.305, ...), kind=kLoop, calls=%fused_computation.64 | loop fusion | bytes 6553616 | tf_op jit(solution)/shard_map/dynamic_slice | solution.py:310
  127.8 7.5 %collective-permute-done.25 = f32[160,512]{1,0:T(8,128)S(1)} collective-permute-done((f32[160,512]{1,0:T(8,128)S(1)}, f32[160,512]{1,0:T(8,128)S(1)}, u32[]{:S(2)}, u32[]{:S(2)}) %collective-permute-start.25) | collective-permute-done | bytes 327712 | tf_op jit(solution)/shard_map/ppermute | solution.py:197
  136.9 5.0 %collective-permute-start.23 = (bf16[2560,320]{0,1:T(8,128)(2,1)}, bf16[2560,320]{0,1:T(8,128)(2,1)}, u32[]{:S(2)}, u32[]{:S(2)}) collective-permute-start(bf16[2560,320]{0,1:T(8,128)(2,1)} %broadcast_select_fusion), channel_id=1, source_target_pairs={{0,8},{16,24},{1,9},{17,25},{10,2},{26,18},{11,3},{27,19},{20,28},... | collective-permute-start | bytes 4915208 | tf_op jit(solution)/shard_map/ppermute | solution.py:328
  144.5 2.6 %shard_map.67 = f32[64,640]{1,0:T(8,128)} custom-call(f32[320,512]{1,0:T(8,128)} %maximum_select_fusion.3.power_ref), custom_call_target="tpu_custom_call" | custom-call | tf_op jit(solution)/shard_map/pallas_call | solution.py:285
  147.7 5.0 %collective-permute-done.27 = f32[64,640]{1,0:T(8,128)S(1)} collective-permute-done((f32[64,640]{1,0:T(8,128)}, f32[64,640]{1,0:T(8,128)S(1)}, u32[]{:S(2)}, u32[]{:S(2)}) %collective-permute-start.27) | collective-permute-done | bytes 163872 | tf_op jit(solution)/shard_map/ppermute | solution.py:197
  153.7 5.3 %collective-permute-done.28 = f32[64,640]{1,0:T(8,128)S(1)} collective-permute-done((f32[64,640]{1,0:T(8,128)S(1)}, f32[64,640]{1,0:T(8,128)S(1)}, u32[]{:S(2)}, u32[]{:S(2)}) %collective-permute-start.28) | collective-permute-done | bytes 163872 | tf_op jit(solution)/shard_map/ppermute | solution.py:197
  159.1 8.0 %collective-permute-done.29 = f32[64,640]{1,0:T(8,128)S(1)} collective-permute-done((f32[64,640]{1,0:T(8,128)S(1)}, f32[64,640]{1,0:T(8,128)S(1)}, u32[]{:S(2)}, u32[]{:S(2)}) %collective-permute-start.29) | collective-permute-done | bytes 163872 | tf_op jit(solution)/shard_map/ppermute | solution.py:197
  168.8 3.6 %collective-permute-done.30 = f32[64,640]{1,0:T(8,128)S(1)} collective-permute-done((f32[64,640]{1,0:T(8,128)S(1)}, f32[64,640]{1,0:T(8,128)S(1)}, u32[]{:S(2)}, u32[]{:S(2)}) %collective-permute-start.30) | collective-permute-done | bytes 163872 | tf_op jit(solution)/shard_map/ppermute | solution.py:197
  172.6 2.6 %fusion.7 = f32[320,640]{1,0:T(8,128)} fusion(f32[320,640]{1,0:T(8,128)} %collective-permute-done.21, f32[320,640]{1,0:T(8,128)S(1)} %collective-permute-done.19, bf16[640,640]{1,0:T(8,128)(2,1)S(1)} %bitcast.101, bf16[320,640]{1,0:T(8,128)(2,1)S(1)} %copy-done, f32[320,640]{1,0:T(8,128)S(1)} %copy-done.4, f32[]{:T(128)S(6)} %mul_shard_map.3), kind=kOutput, calls=%fused_computation.21 | convolution fusion | flops 263168000 | bytes 4505604 | tf_op jit(solution)/shard_map/dot_general | solution.py:311
  176.1 24.5 %shard_map.68 = f32[320,128]{1,0:T(8,128)} custom-call(f32[4,64,640]{2,1,0:T(8,128)} %bitcast.108, f32[320,512]{1,0:T(8,128)} %maximum_select_fusion.3.power_ref), custom_call_target="tpu_custom_call" | custom-call | tf_op jit(solution)/shard_map/pallas_call | solution.py:299
  200.6 4.8 %fusion.14 = f32[320,640]{1,0:T(8,128)} fusion(bf16[2560,640]{1,0:T(8,128)(2,1)} %bitcast.98, bf16[2560,320]{0,1:T(8,128)(2,1)} %broadcast_select_fusion, bf16[2560,320]{0,1:T(8,128)(2,1)} %collective-permute-done.23, pred[]{:T(512)S(6)} %eq.27, f32[320,640]{1,0:T(8,128)S(1)} %copy-done.5, f32[]{:T(128)S(6)} %mul_shard_map.3), kind=kOutput, calls=%fused_computation.29 | convolution fusion | flops 1050009600 | bytes 8192005 | tf_op jit(solution)/shard_map/dot_general | solution.py:333
  (109 shorter events, 47.5 us)
Async XLA Ops:
  8.5 8.4 %collective-permute-start = (bf16[336,128]{1,0:T(8,128)(2,1)S(1)}, bf16[336,128]{1,0:T(8,128)(2,1)S(1)}, u32[]{:S(2)}, u32[]{:S(2)}) collective-permute-start(bf16[336,128]{1,0:T(8,128)(2,1)S(1)} %concatenate.51), channel_id=1, source_target_pairs={{0,1},{1,0},{2,3},{3,2},{4,5},{5,4},{6,7},{7,6},{8,9},{9,8},{10,11... | collective-permute-start | bytes 258056 | tf_op jit(solution)/shard_map/ppermute | solution.py:186
  11.6 37.4 %collective-permute-start.6 = (bf16[320,640]{1,0:T(8,128)(2,1)}, bf16[320,640]{1,0:T(8,128)(2,1)S(1)}, u32[]{:S(2)}, u32[]{:S(2)}) collective-permute-start(bf16[320,640]{1,0:T(8,128)(2,1)} %param.4), channel_id=1, source_target_pairs={{0,1},{1,0},{2,3},{3,2},{4,5},{5,4},{6,7},{7,6},{8,9},{9,8},{10,11... | collective-permute-start | bytes 1228808 | tf_op jit(solution)/shard_map/ppermute | solution.py:186
  11.6 32.5 %collective-permute-start.7 = (bf16[320,640]{1,0:T(8,128)(2,1)}, bf16[320,640]{1,0:T(8,128)(2,1)S(1)}, u32[]{:S(2)}, u32[]{:S(2)}) collective-permute-start(bf16[320,640]{1,0:T(8,128)(2,1)} %param.4), channel_id=1, source_target_pairs={{0,2},{1,3},{2,4},{3,5},{4,6},{5,7},{8,10},{9,11},{10,12},{11,13},... | collective-permute-start | bytes 1228808 | tf_op jit(solution)/shard_map/ppermute | solution.py:190
  15.6 30.0 %collective-permute-start.8 = (bf16[320,640]{1,0:T(8,128)(2,1)}, bf16[320,640]{1,0:T(8,128)(2,1)S(1)}, u32[]{:S(2)}, u32[]{:S(2)}) collective-permute-start(bf16[320,640]{1,0:T(8,128)(2,1)} %param.4), channel_id=1, source_target_pairs={{2,0},{3,1},{4,2},{5,3},{6,4},{7,5},{10,8},{11,9},{12,10},{13,11},... | collective-permute-start | bytes 1228808 | tf_op jit(solution)/shard_map/ppermute | solution.py:190
  17.0 18.8 %collective-permute-start.1 = (bf16[2,336,128]{2,1,0:T(8,128)(2,1)S(1)}, bf16[2,336,128]{2,1,0:T(8,128)(2,1)S(1)}, u32[]{:S(2)}, u32[]{:S(2)}) collective-permute-start(bf16[2,336,128]{2,1,0:T(8,128)(2,1)S(1)} %maximum_select_fusion.8), channel_id=1, source_target_pairs={{0,2},{1,3},{2,4},{3,5},{4,6},{5,7},{6,0},{7,1},{8,10},{9,11},{10,... | collective-permute-start | bytes 516104 | tf_op jit(solution)/shard_map/ppermute | solution.py:194
  22.6 19.5 %collective-permute-start.2 = (bf16[2,336,128]{2,1,0:T(8,128)(2,1)S(1)}, bf16[2,336,128]{2,1,0:T(8,128)(2,1)S(1)}, u32[]{:S(2)}, u32[]{:S(2)}) collective-permute-start(bf16[2,336,128]{2,1,0:T(8,128)(2,1)S(1)} %maximum_select_fusion.8), channel_id=1, source_target_pairs={{0,4},{1,5},{2,6},{3,7},{4,0},{5,1},{6,2},{7,3},{8,12},{9,13},{10,... | collective-permute-start | bytes 516104 | tf_op jit(solution)/shard_map/ppermute | solution.py:194
  35.8 6.8 %collective-permute-start.3 = (bf16[2,336,128]{2,1,0:T(8,128)(2,1)S(1)}, bf16[2,336,128]{2,1,0:T(8,128)(2,1)S(1)}, u32[]{:S(2)}, u32[]{:S(2)}) collective-permute-start(bf16[2,336,128]{2,1,0:T(8,128)(2,1)S(1)} %maximum_select_fusion.8), channel_id=1, source_target_pairs={{0,6},{1,7},{2,0},{3,1},{4,2},{5,3},{6,4},{7,5},{8,14},{9,15},{10,... | collective-permute-start | bytes 516104 | tf_op jit(solution)/shard_map/ppermute | solution.py:194
  42.6 27.2 %collective-permute-start.4 = (bf16[4,2,336,128]{3,2,1,0:T(8,128)(2,1)S(1)}, bf16[4,2,336,128]{3,2,1,0:T(8,128)(2,1)S(1)}, u32[]{:S(2)}, u32[]{:S(2)}) collective-permute-start(bf16[4,2,336,128]{3,2,1,0:T(8,128)(2,1)S(1)} %bitcast_dynamic-update-slice_fusion.14), channel_id=1, source_target_pairs={{0,16},{8,24},{16,0},{24,8},{1,17},{9,25},{17,1},{25,9},{2,18},{10... | collective-permute-start | bytes 2064392 | tf_op jit(solution)/shard_map/ppermute | solution.py:197
  44.2 9.2 %collective-permute-start.9 = (bf16[320,640]{1,0:T(8,128)(2,1)S(1)}, bf16[320,640]{1,0:T(8,128)(2,1)S(1)}, u32[]{:S(2)}, u32[]{:S(2)}) collective-permute-start(bf16[320,640]{1,0:T(8,128)(2,1)S(1)} %collective-permute-done.7), channel_id=1, source_target_pairs={{2,3},{3,2},{4,5},{5,4},{6,7},{7,6},{10,11},{11,10},{12,13},{13,12... | collective-permute-start | bytes 1228808 | tf_op jit(solution)/shard_map/ppermute | solution.py:186
  44.9 7.8 %collective-permute-start.11 = (bf16[320,640]{1,0:T(8,128)(2,1)S(1)}, bf16[320,640]{1,0:T(8,128)(2,1)S(1)}, u32[]{:S(2)}, u32[]{:S(2)}) collective-permute-start(bf16[320,640]{1,0:T(8,128)(2,1)S(1)} %collective-permute-done.7), channel_id=1, source_target_pairs={{2,4},{3,5},{4,6},{5,7},{10,12},{11,13},{12,14},{13,15},{18,20},{1... | collective-permute-start | bytes 1228808 | tf_op jit(solution)/shard_map/ppermute | solution.py:190
  45.6 20.5 %collective-permute-start.10 = (bf16[320,640]{1,0:T(8,128)(2,1)S(1)}, bf16[320,640]{1,0:T(8,128)(2,1)S(1)}, u32[]{:S(2)}, u32[]{:S(2)}) collective-permute-start(bf16[320,640]{1,0:T(8,128)(2,1)S(1)} %collective-permute-done.8), channel_id=1, source_target_pairs={{0,1},{1,0},{2,3},{3,2},{4,5},{5,4},{8,9},{9,8},{10,11},{11,10},{1... | collective-permute-start | bytes 1228808 | tf_op jit(solution)/shard_map/ppermute | solution.py:186
  49.0 12.9 %collective-permute-start.12 = (bf16[320,640]{1,0:T(8,128)(2,1)S(1)}, bf16[320,640]{1,0:T(8,128)(2,1)S(1)}, u32[]{:S(2)}, u32[]{:S(2)}) collective-permute-start(bf16[320,640]{1,0:T(8,128)(2,1)S(1)} %collective-permute-done.8), channel_id=1, source_target_pairs={{2,0},{3,1},{4,2},{5,3},{10,8},{11,9},{12,10},{13,11},{18,16},{19,... | collective-permute-start | bytes 1228808 | tf_op jit(solution)/shard_map/ppermute | solution.py:190
  52.7 25.7 %collective-permute-start.13 = (bf16[320,640]{1,0:T(8,128)(2,1)S(1)}, bf16[320,640]{1,0:T(8,128)(2,1)S(1)}, u32[]{:S(2)}, u32[]{:S(2)}) collective-permute-start(bf16[320,640]{1,0:T(8,128)(2,1)S(1)} %collective-permute-done.11), channel_id=1, source_target_pairs={{4,5},{5,4},{6,7},{7,6},{12,13},{13,12},{14,15},{15,14},{20,21},{2... | collective-permute-start | bytes 1228808 | tf_op jit(solution)/shard_map/ppermute | solution.py:186
  53.4 19.1 %collective-permute-start.15 = (bf16[320,640]{1,0:T(8,128)(2,1)S(1)}, bf16[320,640]{1,0:T(8,128)(2,1)S(1)}, u32[]{:S(2)}, u32[]{:S(2)}) collective-permute-start(bf16[320,640]{1,0:T(8,128)(2,1)S(1)} %collective-permute-done.11), channel_id=1, source_target_pairs={{4,6},{5,7},{12,14},{13,15},{20,22},{21,23},{28,30},{29,31}} | collective-permute-start | bytes 1228808 | tf_op jit(solution)/shard_map/ppermute | solution.py:190
  61.9 17.3 %collective-permute-start.14 = (bf16[320,640]{1,0:T(8,128)(2,1)S(1)}, bf16[320,640]{1,0:T(8,128)(2,1)S(1)}, u32[]{:S(2)}, u32[]{:S(2)}) collective-permute-start(bf16[320,640]{1,0:T(8,128)(2,1)S(1)} %collective-permute-done.12), channel_id=1, source_target_pairs={{0,1},{1,0},{2,3},{3,2},{8,9},{9,8},{10,11},{11,10},{16,17},{17,16... | collective-permute-start | bytes 1228808 | tf_op jit(solution)/shard_map/ppermute | solution.py:186
  66.1 9.8 %collective-permute-start.16 = (bf16[320,640]{1,0:T(8,128)(2,1)S(1)}, bf16[320,640]{1,0:T(8,128)(2,1)S(1)}, u32[]{:S(2)}, u32[]{:S(2)}) collective-permute-start(bf16[320,640]{1,0:T(8,128)(2,1)S(1)} %collective-permute-done.12), channel_id=1, source_target_pairs={{2,0},{3,1},{10,8},{11,9},{18,16},{19,17},{26,24},{27,25}} | collective-permute-start | bytes 1228808 | tf_op jit(solution)/shard_map/ppermute | solution.py:190
  71.1 28.6 %collective-permute-start.5 = (bf16[4,2,336,2,128]{4,2,1,0,3:T(8,128)(2,1)}, bf16[4,2,336,2,128]{4,2,1,0,3:T(8,128)(2,1)}, u32[]{:S(2)}, u32[]{:S(2)}) collective-permute-start(bf16[4,2,336,2,128]{4,2,1,0,3:T(8,128)(2,1)} %maximum_select_fusion.2), channel_id=1, source_target_pairs={{0,8},{8,0},{16,24},{24,16},{1,9},{9,1},{17,25},{25,17},{2,10},{10... | collective-permute-start | bytes 4128776 | tf_op jit(solution)/shard_map/ppermute | solution.py:197
  72.5 9.1 %collective-permute-start.17 = (bf16[320,640]{1,0:T(8,128)(2,1)S(1)}, bf16[320,640]{1,0:T(8,128)(2,1)S(1)}, u32[]{:S(2)}, u32[]{:S(2)}) collective-permute-start(bf16[320,640]{1,0:T(8,128)(2,1)S(1)} %collective-permute-done.15), channel_id=1, source_target_pairs={{6,7},{7,6},{14,15},{15,14},{22,23},{23,22},{30,31},{31,30}} | collective-permute-start | bytes 1228808 | tf_op jit(solution)/shard_map/ppermute | solution.py:186
  75.9 11.0 %collective-permute-start.18 = (bf16[320,640]{1,0:T(8,128)(2,1)S(1)}, bf16[320,640]{1,0:T(8,128)(2,1)S(1)}, u32[]{:S(2)}, u32[]{:S(2)}) collective-permute-start(bf16[320,640]{1,0:T(8,128)(2,1)S(1)} %collective-permute-done.16), channel_id=1, source_target_pairs={{0,1},{1,0},{8,9},{9,8},{16,17},{17,16},{24,25},{25,24}} | collective-permute-start | bytes 1228808 | tf_op jit(solution)/shard_map/ppermute | solution.py:186
  96.2 39.3 %collective-permute-start.22 = (bf16[2560,320]{0,1:T(8,128)(2,1)}, bf16[2560,320]{0,1:T(8,128)(2,1)}, u32[]{:S(2)}, u32[]{:S(2)}) collective-permute-start(bf16[2560,320]{0,1:T(8,128)(2,1)} %copy.25), channel_id=1, source_target_pairs={{0,16},{1,17},{10,26},{11,27},{20,4},{21,5},{30,14},{31,15}} | collective-permute-start | bytes 4915208 | tf_op jit(solution)/shard_map/ppermute | solution.py:323
  122.8 2.3 %collective-permute-start.24 = (f32[160,512]{1,0:T(8,128)S(1)}, f32[160,512]{1,0:T(8,128)S(1)}, u32[]{:S(2)}, u32[]{:S(2)}) collective-permute-start(f32[160,512]{1,0:T(8,128)S(1)} %dynamic-slice_bitcast_fusion), channel_id=1, source_target_pairs={{0,8},{8,0},{16,24},{24,16},{1,9},{9,1},{17,25},{25,17},{2,10},{10... | collective-permute-start | bytes 983048 | tf_op jit(solution)/shard_map/ppermute | solution.py:197
  125.2 10.1 %collective-permute-start.25 = (f32[160,512]{1,0:T(8,128)S(1)}, f32[160,512]{1,0:T(8,128)S(1)}, u32[]{:S(2)}, u32[]{:S(2)}) collective-permute-start(f32[160,512]{1,0:T(8,128)S(1)} %bitcast_add_fusion), channel_id=1, source_target_pairs={{0,16},{8,24},{16,0},{24,8},{1,17},{9,25},{17,1},{25,9},{2,18},{10... | collective-permute-start | bytes 983048 | tf_op jit(solution)/shard_map/ppermute | solution.py:197
  125.8 16.1 %collective-permute-start.20 = (f32[320,640]{1,0:T(8,128)S(1)}, f32[320,640]{1,0:T(8,128)S(1)}, u32[]{:S(2)}, u32[]{:S(2)}) collective-permute-start(f32[320,640]{1,0:T(8,128)S(1)} %convolution_bitcast_fusion.1), channel_id=1, source_target_pairs={{0,8},{8,0},{16,24},{24,16},{1,9},{9,1},{17,25},{25,17},{2,10},{10... | collective-permute-start | bytes 2457608 | tf_op jit(solution)/shard_map/ppermute | solution.py:197
  127.7 44.8 %collective-permute-start.19 = (f32[320,640]{1,0:T(8,128)}, f32[320,640]{1,0:T(8,128)S(1)}, u32[]{:S(2)}, u32[]{:S(2)}) collective-permute-start(f32[320,640]{1,0:T(8,128)} %convolution_bitcast_fusion.3), channel_id=1, source_target_pairs={{0,8},{8,0},{16,24},{24,16},{1,9},{9,1},{17,25},{25,17},{2,10},{10... | collective-permute-start | bytes 2457608 | tf_op jit(solution)/shard_map/ppermute | solution.py:197
  135.3 8.3 %collective-permute-start.26 = (f32[160,512]{1,0:T(8,128)S(1)}, f32[160,512]{1,0:T(8,128)S(1)}, u32[]{:S(2)}, u32[]{:S(2)}) collective-permute-start(f32[160,512]{1,0:T(8,128)S(1)} %add.279), channel_id=1, source_target_pairs={{0,8},{8,0},{16,24},{24,16},{1,9},{9,1},{17,25},{25,17},{2,10},{10... | collective-permute-start | bytes 983048 | tf_op jit(solution)/shard_map/ppermute | solution.py:197
  136.9 63.7 %collective-permute-start.23 = (bf16[2560,320]{0,1:T(8,128)(2,1)}, bf16[2560,320]{0,1:T(8,128)(2,1)}, u32[]{:S(2)}, u32[]{:S(2)}) collective-permute-start(bf16[2560,320]{0,1:T(8,128)(2,1)} %broadcast_select_fusion), channel_id=1, source_target_pairs={{0,8},{16,24},{1,9},{17,25},{10,2},{26,18},{11,3},{27,19},{20,28},... | collective-permute-start | bytes 4915208 | tf_op jit(solution)/shard_map/ppermute | solution.py:328
  143.3 29.2 %collective-permute-start.21 = (f32[320,640]{1,0:T(8,128)}, f32[320,640]{1,0:T(8,128)}, u32[]{:S(2)}, u32[]{:S(2)}) collective-permute-start(f32[320,640]{1,0:T(8,128)} %fusion.8), channel_id=1, source_target_pairs={{0,16},{8,24},{16,0},{24,8},{1,17},{9,25},{17,1},{25,9},{2,18},{10... | collective-permute-start | bytes 2457608 | tf_op jit(solution)/shard_map/ppermute | solution.py:197
  147.1 5.5 %collective-permute-start.27 = (f32[64,640]{1,0:T(8,128)}, f32[64,640]{1,0:T(8,128)S(1)}, u32[]{:S(2)}, u32[]{:S(2)}) collective-permute-start(f32[64,640]{1,0:T(8,128)} %shard_map.67), channel_id=1, source_target_pairs={{0,1},{1,0},{2,3},{3,2},{4,5},{5,4},{6,7},{7,6},{8,9},{9,8},{10,11... | collective-permute-start | bytes 491528 | tf_op jit(solution)/shard_map/ppermute | solution.py:197
  153.6 5.4 %collective-permute-start.28 = (f32[64,640]{1,0:T(8,128)S(1)}, f32[64,640]{1,0:T(8,128)S(1)}, u32[]{:S(2)}, u32[]{:S(2)}) collective-permute-start(f32[64,640]{1,0:T(8,128)S(1)} %add.280), channel_id=1, source_target_pairs={{0,2},{1,3},{2,0},{3,1},{4,6},{5,7},{6,4},{7,5},{8,10},{9,11},{10,... | collective-permute-start | bytes 491528 | tf_op jit(solution)/shard_map/ppermute | solution.py:197
  159.0 8.0 %collective-permute-start.29 = (f32[64,640]{1,0:T(8,128)S(1)}, f32[64,640]{1,0:T(8,128)S(1)}, u32[]{:S(2)}, u32[]{:S(2)}) collective-permute-start(f32[64,640]{1,0:T(8,128)S(1)} %add.281), channel_id=1, source_target_pairs={{0,4},{1,5},{2,6},{3,7},{4,0},{5,1},{6,2},{7,3},{8,12},{9,13},{10,... | collective-permute-start | bytes 491528 | tf_op jit(solution)/shard_map/ppermute | solution.py:197
  167.1 5.4 %collective-permute-start.30 = (f32[64,640]{1,0:T(8,128)S(1)}, f32[64,640]{1,0:T(8,128)S(1)}, u32[]{:S(2)}, u32[]{:S(2)}) collective-permute-start(f32[64,640]{1,0:T(8,128)S(1)} %add.282), channel_id=1, source_target_pairs={{0,16},{8,24},{16,0},{24,8},{1,17},{9,25},{17,1},{25,9},{2,18},{10... | collective-permute-start | bytes 491528 | tf_op jit(solution)/shard_map/ppermute | solution.py:197
  172.5 2.7 %collective-permute-start.31 = (f32[2,64,640]{2,1,0:T(8,128)S(1)}, f32[2,64,640]{2,1,0:T(8,128)S(1)}, u32[]{:S(2)}, u32[]{:S(2)}) collective-permute-start(f32[2,64,640]{2,1,0:T(8,128)S(1)} %maximum_select_fusion.6), channel_id=1, source_target_pairs={{0,8},{8,0},{16,24},{24,16},{1,9},{9,1},{17,25},{25,17},{2,10},{10... | collective-permute-start | bytes 983048 | tf_op jit(solution)/shard_map/ppermute | solution.py:197
  (6 other events, 65.8 us)

commit v3 on v2

v3 whole, which is shorter than its diff:
```python
import functools

import jax
import jax.numpy as jnp
from jax import lax
from jax.experimental import pallas as pl
from jax.experimental.pallas import tpu as pltpu
from jax.sharding import PartitionSpec as P

smoothing = 0.95
clip_ratio = 4.0
epsilon_value = 1e-06
HI = lax.Precision.HIGHEST
BLOCK, PANEL = 128, 8


def factor_block(t_ref):
    w = PANEL
    sub = lax.broadcasted_iota(jnp.int32, (w, 128), 0)
    full = lambda v: jnp.broadcast_to(v, (w, 128))
    for p in range(BLOCK // w):
        c0 = p * w
        left, right = t_ref[c0:c0 + w, 0:128], t_ref[c0:c0 + w, 128:256]
        cols = [full(left[:, c0 + k:c0 + k + 1]) for k in range(w)]
        e = {(i, k): full(cols[k][i:i + 1, :]) for i in range(w) for k in range(i + 1)}
        l, inv, rs = {}, [], []
        for j in range(w):
            r = 1.0 / e[j, j]
            inv.append(r); rs.append(lax.rsqrt(e[j, j]))
            for i in range(j + 1, w):
                l[i, j] = e[i, j] * r
            for i in range(j + 1, w):
                for k in range(j + 1, i + 1):
                    e[i, k] = e[i, k] - l[i, j] * e[k, j]
        li = {}
        for k in range(w):
            for i in range(k + 1, w):
                acc = l[i, k]
                for m in range(k + 1, i):
                    acc = acc + l[i, m] * li[m, k]
                li[i, k] = -acc

        def pick(vals):
            out = jnp.zeros((w, 128), jnp.float32)
            for i, v in vals.items():
                out = jnp.where(sub == i, v, out)
            return out

        zl, zr = left, right
        for k in range(w - 1):
            coef = pick({i: li[i, k] for i in range(k + 1, w)})
            zl = zl + coef * full(left[k:k + 1, :])
            zr = zr + coef * full(right[k:k + 1, :])
        dinv = pick(dict(enumerate(inv)))
        ul, ur = dinv * zl, dinv * zr
        vl, vr = ul, ur
        for k in range(1, w):
            coef = pick({i: li[k, i] for i in range(k)})
            vl = vl + coef * full(ul[k:k + 1, :])
            vr = vr + coef * full(ur[k:k + 1, :])
        vlb = [full(vl[k:k + 1, :]) for k in range(w)]
        vrb = [full(vr[k:k + 1, :]) for k in range(w)]
        for q in range(p + 1, BLOCK // w):
            rows = slice(q * w, q * w + w)
            al, ar = t_ref[rows, 0:128], t_ref[rows, 128:256]
            nl, nr = al, ar
            for k in range(w):
                a = full(al[:, c0 + k:c0 + k + 1])
                nl = nl - a * vlb[k]
                nr = nr - a * vrb[k]
            t_ref[rows, 0:128] = nl
            t_ref[rows, 128:256] = nr
        scale = pick(dict(enumerate(rs)))
        t_ref[c0:c0 + w, 0:128] = scale * zl
        t_ref[c0:c0 + w, 128:256] = scale * zr


GRANT = {"message": 8, "parts": 20, "power": 24, "gram": 12, "basis": 16, "sides": 24, "right": 20}


def strip_of(order, roles, role, which):
    height = order // (2 * roles)
    strip = role if which == 0 else 2 * roles - 1 - role
    return strip * height, height, strip * height // BLOCK * BLOCK


def packed_width(order, roles):
    return max(
        sum(order - strip_of(order, roles, role, which)[2] for which in (0, 1)) for role in range(roles)
    )


def product(a, b, contract, precision=None):
    return lax.dot_general(
        a, b, ((contract[:1], contract[1:]), ((), ())), precision=precision, preferred_element_type=jnp.float32
    )


def eye(n):
    return (
        lax.broadcasted_iota(jnp.int32, (n, n), 0) == lax.broadcasted_iota(jnp.int32, (n, n), 1)
    ).astype(jnp.float32)


def rounded_parts(value):
    high = value.astype(jnp.bfloat16)
    rest = value - high.astype(jnp.float32)
    middle = rest.astype(jnp.bfloat16)
    return high, middle, (rest - middle.astype(jnp.float32)).astype(jnp.bfloat16)


def fetch(pieces, held, sems):
    line = held.shape[0]
    line_at = lax.axis_index("shard") // 2
    start = lambda ref, dz, dx: pltpu.make_async_copy(ref, held.at[dz, dx], sems.at[dz, dx]).start()
    start(pieces[0], 0, 0)
    start(pieces[1], 0, 1)
    for by in range(1, line):
        low, high, low_side, high_side = pieces[4 * by - 1 : 4 * by + 3]
        skip = 1 if by == 1 else 0

        @pl.when(line_at >= by)
        def _():
            start(low, by, 0)

        @pl.when(line_at >= by + skip)
        def _():
            start(low_side, by, 1)

        @pl.when(line_at + by < line)
        def _():
            start(high, line - by, 0)

        @pl.when(line_at + by + skip < line)
        def _():
            start(high_side, line - by, 1)

    @pl.when(line_at == 1)
    def _():
        start(pieces[2], 1, 1)

    @pl.when(line_at == line - 2)
    def _():
        start(pieces[2], line - 1, 1)

    def wait(dz):
        for dx in (0, 1):
            pltpu.make_async_copy(pieces[0], held.at[dz, dx], sems.at[dz, dx]).wait()

    return wait


def message_kernel(gradient_ref, basis_ref, out_ref):
    rows, vec = basis_ref.shape
    wide = gradient_ref[...].astype(jnp.float32)
    squares = jnp.broadcast_to(jnp.sum(jnp.sum(wide * wide, axis=0, keepdims=True), axis=1, keepdims=True), (16, vec))
    out_ref[:rows, :] = basis_ref[...]
    at = lax.broadcasted_iota(jnp.int32, (16, vec), 0)
    tail = jnp.zeros((16, vec), jnp.float32)
    for i, part in enumerate(rounded_parts(squares)):
        tail = jnp.where(at == i, part.astype(jnp.float32), tail)
    out_ref[rows:, :] = tail.astype(jnp.bfloat16)


def basis_parts_kernel(order_size, left_ref, *refs):
    given, (turned_ref, old_ref, weight_ref, rows_ref) = refs[:8], refs[8:]
    rows, cols = left_ref.shape
    line, _, vec = given[0].shape
    per_role = cols // rows
    shard_at, role_at = lax.axis_index("shard"), lax.axis_index("role")
    line_at, side_at = shard_at // 2, shard_at % 2
    total = jnp.zeros((1, vec), jnp.float32)
    for bits, refs in zip((0, 2, 1, 3), (given[0:2], given[2:4], given[4:6], given[6:8])):
        at = pl.multiple_of((role_at ^ bits) * vec, BLOCK)
        whole = jnp.concatenate([refs[dx][dz, :rows, :] for dz in range(line) for dx in (0, 1)])
        turned_ref[pl.ds(at, vec), :] = whole.astype(jnp.float32).T.astype(jnp.bfloat16)
        for i in range(per_role):
            shard = role_at * per_role + i
            dz = lax.rem(line_at - shard // 2 + line, line)
            for dx in (0, 1):

                @pl.when((shard + side_at) % 2 == dx)
                def _():
                    rows_ref[i * rows : (i + 1) * rows, pl.ds(at, vec)] = refs[dx][dz, :rows, :]

        for ref in refs:
            for dz in range(line):
                total = total + jnp.sum(ref[dz, rows:, :].astype(jnp.float32), axis=0, keepdims=True)
    factor = jnp.minimum(
        1.0, clip_ratio * jnp.sqrt(jnp.float32(order_size)) / jnp.sqrt(total + epsilon_value)
    )
    weight_ref[...] = jnp.broadcast_to((1.0 - smoothing) * (factor * factor), weight_ref.shape)
    old = jnp.zeros(old_ref.shape, jnp.float32)
    for part in rounded_parts(left_ref[...]):
        old = old + product(part, rows_ref[...], (1, 0))
    old_ref[...] = smoothing * old


def power_kernel(count, *refs):
    pieces, (turned_ref, old_ref, weight_ref, keep_ref, send_ref, held, part_ref, sems) = refs[:count], refs[count:]
    line, _, rows, cols = held.shape
    order = turned_ref.shape[0]
    wait = fetch(pieces, held, sems)
    for dz in range(line):
        wait(dz)
    turned = product(turned_ref[...], held[...].reshape(2 * line * rows, cols), (1, 0))
    own = held[0, 0]
    new = jnp.zeros((rows, order), jnp.float32)
    for part in rounded_parts(turned):
        new = new + product(own, part, (1, 1))
    part_ref[...] = old_ref[...] + weight_ref[0:1, 0:1] * new
    half = rows // 2
    core_at = lax.axis_index("role") % 2
    for core in (0, 1):

        @pl.when(core_at == core)
        def _():
            keep_ref[...] = part_ref[core * half : (core + 1) * half, :]
            send_ref[...] = part_ref[(1 - core) * half : (2 - core) * half, :]


def gram_kernel(roles, keep_ref, across_ref, out_ref, power_ref):
    order = power_ref.shape[1]
    half = keep_ref.shape[0]
    here = lax.axis_index("role")
    for core in (0, 1):

        @pl.when(here % 2 == core)
        def _():
            power_ref[core * half : (core + 1) * half, :] = keep_ref[...]
            power_ref[(1 - core) * half : (2 - core) * half, :] = across_ref[...]

    for role in range(roles):

        @pl.when(here == role)
        def _():
            at = 0
            for which in (0, 1):
                row, height, first = strip_of(order, roles, role, which)
                out_ref[:, at : at + order - first] = product(
                    power_ref[:, row : row + height], power_ref[:, first:], (0, 0), HI
                )
                at += order - first
            if at < out_ref.shape[1]:
                out_ref[:, at:] = jnp.zeros((out_ref.shape[0], out_ref.shape[1] - at), jnp.float32)


def basis_kernel(roles, *refs):
    given, (power_ref, out_ref, m_ref, t_ref) = refs[:4], refs[4:]
    n = power_ref.shape[1]
    nb = n // BLOCK
    here = lax.axis_index("role")
    for bits, ref in zip((0, 2, 1, 3), given):
        for role in range(roles):

            @pl.when(here ^ bits == role)
            def _():
                at = 0
                for which in (0, 1):
                    row, height, first = strip_of(n, roles, role, which)
                    m_ref[row : row + height, first:n] = ref[:, at : at + n - first]
                    at += n - first

    m_ref[:, n:] = eye(n)

    @pl.loop(0, nb)
    def _(b):
        start = pl.multiple_of(b * BLOCK, BLOCK)
        t_ref[:, :BLOCK] = m_ref[pl.ds(start, BLOCK), pl.ds(start, BLOCK)]
        t_ref[:, BLOCK:] = eye(BLOCK)
        factor_block(t_ref)
        for c in range(nb):

            @pl.when(b == c)
            def _():
                lo, hi = c * BLOCK, n + (c + 1) * BLOCK
                rows = jnp.dot(
                    t_ref[:, BLOCK:],
                    m_ref[lo : lo + BLOCK, lo:hi],
                    precision=HI,
                    preferred_element_type=jnp.float32,
                )
                m_ref[lo : lo + BLOCK, lo:hi] = rows
                if c + 1 < nb:
                    m_ref[lo + BLOCK :, lo + BLOCK : hi] -= lax.dot_general(
                        rows[:, BLOCK : n - lo],
                        rows[:, BLOCK:],
                        (((0,), (0,)), ((), ())),
                        precision=HI,
                        preferred_element_type=jnp.float32,
                    )

    width = out_ref.shape[1]
    mine = pl.multiple_of(here * width, BLOCK)
    out_ref[...] = product(power_ref[...], m_ref[pl.ds(mine, width), n:], (1, 1), HI)


def sides_kernel(count, *refs):
    pieces, outs, (slab_ref, held, block_ref, sems) = refs[:count], refs[count:-4], refs[-4:]
    line, _, rows, cols = held.shape
    per_role = cols // rows
    shard_at, role_at = lax.axis_index("shard"), lax.axis_index("role")
    line_at, side_at = shard_at // 2, shard_at % 2
    wait = fetch(pieces, held, sems)
    for dz in range(line):
        wait(dz)
    own = held[0, 0]
    for bits, out in zip((3, 1, 2, 0), outs):
        for i in range(per_role):
            shard = (role_at ^ bits) * per_role + i
            dz = lax.rem(line_at - shard // 2 + line, line)
            block_ref[i * rows : (i + 1) * rows, :] = held[dz, (shard + side_at) % 2]
        out[...] = product(own, block_ref[...], (1, 1))
    for i in range(per_role):

        @pl.when(shard_at % per_role == i)
        def _():
            slab = held[:, :, :, i * rows : (i + 1) * rows].reshape(2 * line * rows, rows)
            slab_ref[...] = slab.astype(jnp.float32).T.astype(jnp.bfloat16)


def right_kernel(count, *refs):
    pieces, slabs = refs[:count], refs[count : count + 4]
    old_ref, weight_ref, out_ref, held, slab, sems, slab_sem = refs[count + 4 :]
    line, _, rows, cols = held.shape
    owner = lax.axis_index("shard") * rows // cols
    wait = fetch(pieces, held, sems)
    for bits, ref in enumerate(slabs):

        @pl.when(lax.axis_index("role") ^ owner == bits)
        def _():
            pltpu.make_async_copy(ref, slab, slab_sem).start()

    pltpu.make_async_copy(slabs[0], slab, slab_sem).wait()
    for dz in range(line):
        wait(dz)
    gram = product(slab[...], held[...].reshape(2 * line * rows, cols), (1, 0))
    out_ref[...] = smoothing * old_ref[...] + weight_ref[0:1, 0:1] * gram


def step(gradient, left_old, right_old, basis_old):
    rows, cols = gradient.shape
    vec = basis_old.shape[1]
    shards, roles = lax.axis_size("shard"), lax.axis_size("role")
    order_size, order = rows * shards, vec * roles
    line = shards // 2

    def other_side(value, first=0, last=line - 1):
        pairs = [(2 * z + x, 2 * z + 1 - x) for z in range(first, last + 1) for x in (0, 1)]
        return lax.ppermute(value, "shard", pairs)

    def along(value, first, last, by):
        pairs = [(2 * z + x, 2 * (z + by) + x) for z in range(first, last + 1) for x in (0, 1)]
        return lax.ppermute(value, "shard", pairs)

    def around(value, by):
        pairs = [(2 * z + x, 2 * ((z + by) % line) + x) for z in range(line) for x in (0, 1)]
        return lax.ppermute(value, "shard", pairs)

    def flip(value, axis, size, bit):
        return lax.ppermute(value, axis, [(i, i ^ bit) for i in range(size)])

    other_core = lambda value: flip(value, "role", roles, 1)
    other_half = lambda value: flip(value, "role", roles, 2)

    side = other_side(gradient)
    inward = [(2 * z + x, 2 * to + x) for z, to in ((0, 1), (line - 1, line - 2)) for x in (0, 1)]
    pieces = [gradient, side, lax.ppermute(side, "shard", inward)]
    low = high = gradient
    for by in range(1, line):
        low = along(low, by - 1, line - 2, 1)
        high = along(high, 1, line - by, -1)
        pieces += [low, high]
        skip = 1 if by == 1 else 0
        pieces.append(other_side(low, by + skip, line - 1))
        pieces.append(other_side(high, 0, line - 1 - by - skip))

    def call(name, kernel, out_shape, **options):
        return pl.pallas_call(
            kernel,
            out_shape=out_shape,
            compiler_params=pltpu.CompilerParams(vmem_limit_bytes=GRANT[name] << 20),
            **options,
        )

    anywhere = pl.BlockSpec(memory_space=pl.ANY)
    in_vmem = pl.BlockSpec(memory_space=pltpu.VMEM)
    count = len(pieces)
    held = pltpu.VMEM((line, 2, rows, cols), jnp.bfloat16)
    sems = pltpu.SemaphoreType.DMA((line, 2))
    shape = lambda *dims, dtype=jnp.float32: jax.ShapeDtypeStruct(dims, dtype)

    message = call("message", message_kernel, shape(rows + 16, vec, dtype=jnp.bfloat16))(gradient, basis_old)
    column = jnp.stack([message] + [around(message, by) for by in range(1, line)])
    across = other_side(column)
    mine = [column, across]
    yours = [other_half(column), other_half(across)]
    theirs = [other_core(value) for value in mine + yours]
    turned, old_part, weight = call(
        "parts",
        functools.partial(basis_parts_kernel, order_size),
        (shape(order, order_size, dtype=jnp.bfloat16), shape(rows, order), shape(8, BLOCK)),
        scratch_shapes=[pltpu.VMEM((cols, order), jnp.bfloat16)],
    )(left_old, *mine, *yours, *theirs)

    half_rows = rows // 2
    keep, send = call(
        "power",
        functools.partial(power_kernel, count),
        out_shape=(shape(half_rows, order), shape(half_rows, order)),
        in_specs=[anywhere] * count + [in_vmem] * 3,
        scratch_shapes=[held, pltpu.VMEM((rows, order), jnp.float32), sems],
    )(*pieces, turned, old_part, weight)
    keep = keep + other_core(send)
    keep = keep + other_half(keep)

    packed, power = call(
        "gram",
        functools.partial(gram_kernel, roles),
        out_shape=(shape(order // (2 * roles), packed_width(order, roles)), shape(rows, order)),
    )(keep, other_core(keep))
    bit = 1
    while bit < shards:
        packed = packed + flip(packed, "shard", shards, bit)
        bit *= 2
    yours = other_half(packed)
    left_basis = call(
        "basis",
        functools.partial(basis_kernel, roles),
        out_shape=shape(rows, vec),
        scratch_shapes=[
            pltpu.VMEM((order, 2 * order), jnp.float32),
            pltpu.VMEM((BLOCK, 2 * BLOCK), jnp.float32),
        ],
    )(packed, yours, other_core(packed), other_core(yours), power)

    *shares, slab = call(
        "sides",
        functools.partial(sides_kernel, count),
        out_shape=(shape(rows, cols),) * 4 + (shape(rows, order_size, dtype=jnp.bfloat16),),
        in_specs=[anywhere] * count,
        scratch_shapes=[held, pltpu.VMEM((cols, cols), jnp.bfloat16), sems],
    )(*pieces)
    away = shares[2] + other_core(shares[0])
    here = shares[3] + other_core(shares[1])
    left_stat = smoothing * left_old + weight[0, 0] * (here + other_half(away))

    owner_of = lambda shard: shard * rows // cols

    def from_owner(value, source, target):
        pairs = [
            tuple((owner_of(s) ^ bits) * shards + s for bits in (source, target)) for s in range(shards)
        ]
        return lax.ppermute(value, ("role", "shard"), pairs)

    crossed = from_owner(slab, 0, 2)
    right_stat = call(
        "right",
        functools.partial(right_kernel, count),
        out_shape=shape(rows, cols),
        in_specs=[anywhere] * (count + 4) + [in_vmem] * 2,
        scratch_shapes=[
            held,
            pltpu.VMEM((rows, order_size), jnp.bfloat16),
            sems,
            pltpu.SemaphoreType.DMA,
        ],
    )(*pieces, slab, from_owner(slab, 0, 1), crossed, from_owner(crossed, 2, 3), right_old, weight)
    return (left_stat, right_stat, left_basis)


def solution(mesh):
    return jax.shard_map(
        step,
        mesh=mesh,
        in_specs=(P("shard", "role"), P("shard", "role"), P("shard", "role"), P("shard", "role")),
        out_specs=(P("shard", "role"), P("shard", "role"), P("shard", "role")),
        check_vma=False,
    )
```

time: 206 us -> 182 us (0.88)
  local copies, waits for them, and re-layouts: 34.3 us -> 1.53 us
  matrix products: 20.7 us -> 0 us
  waiting for transfers between devices: 61.8 us -> 82.1 us
  Pallas kernels: 27.1 us -> 41.2 us
  starting transfers between devices: 42.6 us -> 53.7 us
  other arithmetic: 12.1 us -> 2 us
  between operations: 6.79 us -> 1.14 us
    dot_general x10 -> x0, matrix products: 20.7 us -> none  [the longest x4 5.97 us: left_for(): lax.dot_general(gradient, block, (((1,), (1,)), ((), ())), preferred_elem...]
    ppermute x13 -> x18, waiting for transfers between devices: 29.4 us -> 45 us  [flip(): return lax.ppermute(value, axis, [(i, i ^ bit) for i in range(size)])]
    pallas_call x2 -> x7, Pallas kernels: 27.1 us -> 41.2 us  [the longest x1 23.3 us: step(): call('basis', functools.partial(basis_kernel, roles), out_shape=shape(row...]
    ppermute x8, waiting for transfers between devices: 4.64 us -> 17.2 us  [other_side(): return lax.ppermute(value, 'shard', pairs)]
    dynamic_update_slice x17 -> x0, local copies, waits for them, and re-layouts: 11.2 us -> none  [the longest x14 11.1 us: put(): return lax.dynamic_update_slice(gathered, value[None], (place, 0, 0))]
    ppermute x3, waiting for transfers between devices: 17.2 us -> 6.39 us  [around(): return lax.ppermute(value, 'shard', pairs)]
    select_n x9 -> x0, other arithmetic: 8.5 us -> none  [the longest x1 3.31 us: step(): jnp.where(core_at == 0, jnp.stack([two, their], axis=4), jnp.stack([their...]
    ppermute x13 -> x18, starting transfers between devices: 5.18 us -> 13 us  [flip(): return lax.ppermute(value, axis, [(i, i ^ bit) for i in range(size)])]
  transfers between devices with their start and end apart: 32 -> 39, of which waited for: 11 -> 17; matrix products, arithmetic and copies ran while one was open for 28% -> 1% of each run, Pallas kernels for 13% -> 18%
where the time goes in v3:
time: 182 us
  waiting for transfers between devices  82.1 us (45%)
  starting transfers between devices  53.7 us (30%)
  Pallas kernels  41.2 us (23%)
  other arithmetic  2 us (1%)
    ppermute x18, waiting for transfers between devices, flip(): return lax.ppermute(value, axis, [(i, i ^ bit) for i in range(size)])  45 us
    pallas_call x1, Pallas kernels, step(): call('basis', functools.partial(basis_kernel, roles), out_shape=shape(row...  23.3 us
    ppermute x8, waiting for transfers between devices, other_side(): return lax.ppermute(value, 'shard', pairs)  17.2 us
    ppermute x8, starting transfers between devices, other_side(): return lax.ppermute(value, 'shard', pairs)  14 us
    ppermute x6, waiting for transfers between devices, along(): return lax.ppermute(value, 'shard', pairs)  13.5 us
    ppermute x18, starting transfers between devices, flip(): return lax.ppermute(value, axis, [(i, i ^ bit) for i in range(size)])  13 us
    ppermute x6, starting transfers between devices, along(): return lax.ppermute(value, 'shard', pairs)  10.8 us
    ppermute x1, starting transfers between devices, step(): pieces = [gradient, side, lax.ppermute(side, 'shard', inward)]  7.56 us
  transfers between devices with their start and end apart: 39, of which 17 were waited for; matrix products, arithmetic and copies ran while one was open for 1% of the time, Pallas kernels for 18%

profile of v3, /device:TPU:0, one launch (start us, length us, event | category | flops | bytes accessed | tf_op | source)
XLA Modules:
  0.0 181.7 jit_solution(12051063376491058084)
XLA Ops:
  1.9 5.6 %collective-permute-start.12 = (bf16[320,640]{1,0:T(8,128)(2,1)}, bf16[320,640]{1,0:T(8,128)(2,1)S(1)}, u32[]{:S(2)}, u32[]{:S(2)}) collective-permute-start(bf16[320,640]{1,0:T(8,128)(2,1)} %refs_0_.5), channel_id=1, source_target_pairs={{0,2},{1,3},{2,4},{3,5},{4,6},{5,7},{8,10},{9,11},{10,12},{11,13},... | collective-permute-start | bytes 1228808 | tf_op jit(solution)/shard_map/ppermute | solution.py:354
  7.6 7.7 %collective-permute-done.13.refs_4_ = bf16[320,640]{1,0:T(8,128)(2,1)S(1)} collective-permute-done((bf16[320,640]{1,0:T(8,128)(2,1)}, bf16[320,640]{1,0:T(8,128)(2,1)S(1)}, u32[]{:S(2)}, u32[]{:S(2)}) %collective-permute-start.13) | collective-permute-done | bytes 409632 | tf_op jit(solution)/shard_map/ppermute | solution.py:354
  19.0 2.3 %collective-permute-start.15 = (bf16[320,640]{1,0:T(8,128)(2,1)S(1)}, bf16[320,640]{1,0:T(8,128)(2,1)S(1)}, u32[]{:S(2)}, u32[]{:S(2)}) collective-permute-start(bf16[320,640]{1,0:T(8,128)(2,1)S(1)} %collective-permute-done.13.refs_4_), channel_id=1, source_target_pairs={{0,1},{1,0},{2,3},{3,2},{8,9},{9,8},{10,11},{11,10},{16,17},{17,16... | collective-permute-start | bytes 1228808 | tf_op jit(solution)/shard_map/ppermute | solution.py:350
  21.9 5.8 %collective-permute-done.17.refs_8_ = bf16[320,640]{1,0:T(8,128)(2,1)S(1)} collective-permute-done((bf16[320,640]{1,0:T(8,128)(2,1)S(1)}, bf16[320,640]{1,0:T(8,128)(2,1)S(1)}, u32[]{:S(2)}, u32[]{:S(2)}) %collective-permute-start.17) | collective-permute-done | bytes 409632 | tf_op jit(solution)/shard_map/ppermute | solution.py:354
  29.9 7.6 %collective-permute-start.11 = (bf16[320,640]{1,0:T(8,128)(2,1)S(1)}, bf16[320,640]{1,0:T(8,128)(2,1)S(1)}, u32[]{:S(2)}, u32[]{:S(2)}) collective-permute-start(bf16[320,640]{1,0:T(8,128)(2,1)S(1)} %collective-permute-done.10.refs_1_), channel_id=1, source_target_pairs={{0,2},{1,3},{6,4},{7,5},{8,10},{9,11},{14,12},{15,13},{16,18},{17,... | collective-permute-start | bytes 1228808 | tf_op jit(solution)/shard_map/ppermute | solution.py:368
  37.4 3.4 %collective-permute-start.19 = (bf16[320,640]{1,0:T(8,128)(2,1)S(1)}, bf16[320,640]{1,0:T(8,128)(2,1)S(1)}, u32[]{:S(2)}, u32[]{:S(2)}) collective-permute-start(bf16[320,640]{1,0:T(8,128)(2,1)S(1)} %collective-permute-done.17.refs_8_), channel_id=1, source_target_pairs={{0,1},{1,0},{2,3},{3,2},{8,9},{9,8},{10,11},{11,10},{16,17},{17,16... | collective-permute-start | bytes 1228808 | tf_op jit(solution)/shard_map/ppermute | solution.py:350
  41.6 2.4 %collective-permute-start.23 = (bf16[320,640]{1,0:T(8,128)(2,1)S(1)}, bf16[320,640]{1,0:T(8,128)(2,1)S(1)}, u32[]{:S(2)}, u32[]{:S(2)}) collective-permute-start(bf16[320,640]{1,0:T(8,128)(2,1)S(1)} %collective-permute-done.21.refs_12_), channel_id=1, source_target_pairs={{0,1},{1,0},{8,9},{9,8},{16,17},{17,16},{24,25},{25,24}} | collective-permute-start | bytes 1228808 | tf_op jit(solution)/shard_map/ppermute | solution.py:350
  44.7 6.9 %collective-permute-done.19.refs_10_ = bf16[320,640]{1,0:T(8,128)(2,1)S(1)} collective-permute-done((bf16[320,640]{1,0:T(8,128)(2,1)S(1)}, bf16[320,640]{1,0:T(8,128)(2,1)S(1)}, u32[]{:S(2)}, u32[]{:S(2)}) %collective-permute-start.19) | collective-permute-done | bytes 409632 | tf_op jit(solution)/shard_map/ppermute | solution.py:350
  51.7 5.7 %collective-permute-done.23.refs_14_ = bf16[320,640]{1,0:T(8,128)(2,1)S(1)} collective-permute-done((bf16[320,640]{1,0:T(8,128)(2,1)S(1)}, bf16[320,640]{1,0:T(8,128)(2,1)S(1)}, u32[]{:S(2)}, u32[]{:S(2)}) %collective-permute-start.23) | collective-permute-done | bytes 409632 | tf_op jit(solution)/shard_map/ppermute | solution.py:350
  58.4 4.2 %shard_map.69 = (f32[320,640]{1,0:T(8,128)S(1)}, f32[320,640]{1,0:T(8,128)S(1)}, f32[320,640]{1,0:T(8,128)S(1)}, f32[320,640]{1,0:T(8,128)S(1)}, bf16[320,2560]{1,0:T(8,128)(2,1)S(1)}) custom-call(bf16[320,640]{1,0:T(8,128)(2,1)S(1)} %copy-done, bf16[320,640]{1,0:T(8,128)(2,1)S(1)} %collective-permute-done.10.refs_1_, ...), custom_call_target="tpu_custom_call" | custom-call | tf_op jit(solution)/shard_map/pallas_call | solution.py:437
  62.6 3.3 %collective-permute-start.28 = (bf16[320,2560]{1,0:T(8,128)(2,1)S(1)}, bf16[320,2560]{1,0:T(8,128)(2,1)S(1)}, u32[]{:S(2)}, u32[]{:S(2)}) collective-permute-start(bf16[320,2560]{1,0:T(8,128)(2,1)S(1)} %get-tuple-element.20.refs_15_), channel_id=1, source_target_pairs={{0,16},{1,17},{10,26},{11,27},{20,4},{21,5},{30,14},{31,15}} | collective-permute-start | bytes 4915208 | tf_op jit(solution)/shard_map/ppermute | solution.py:454
  68.3 3.0 %collective-permute-done.2 = bf16[336,128]{1,0:T(8,128)(2,1)S(1)} collective-permute-done((bf16[336,128]{1,0:T(8,128)(2,1)S(1)}, bf16[336,128]{1,0:T(8,128)(2,1)S(1)}, u32[]{:S(2)}, u32[]{:S(2)}) %collective-permute-start.2) | collective-permute-done | bytes 86048 | tf_op jit(solution)/shard_map/ppermute | solution.py:358
  71.3 3.4 %collective-permute-done.1 = bf16[336,128]{1,0:T(8,128)(2,1)S(1)} collective-permute-done((bf16[336,128]{1,0:T(8,128)(2,1)S(1)}, bf16[336,128]{1,0:T(8,128)(2,1)S(1)}, u32[]{:S(2)}, u32[]{:S(2)}) %collective-permute-start.1) | collective-permute-done | bytes 86048 | tf_op jit(solution)/shard_map/ppermute | solution.py:358
  74.8 2.1 %collective-permute-start.3 = (bf16[4,336,128]{2,1,0:T(8,128)(2,1)S(1)}, bf16[4,336,128]{2,1,0:T(8,128)(2,1)S(1)}, u32[]{:S(2)}, u32[]{:S(2)}) collective-permute-start(bf16[4,336,128]{2,1,0:T(8,128)(2,1)S(1)} %pad_maximum_fusion.refs_0_), channel_id=1, source_target_pairs={{0,1},{1,0},{2,3},{3,2},{4,5},{5,4},{6,7},{7,6},{8,9},{9,8},{10,11... | collective-permute-start | bytes 1032200 | tf_op jit(solution)/shard_map/ppermute | solution.py:350
  77.7 4.4 %collective-permute-done.3.refs_1_ = bf16[4,336,128]{2,1,0:T(8,128)(2,1)S(1)} collective-permute-done((bf16[4,336,128]{2,1,0:T(8,128)(2,1)S(1)}, bf16[4,336,128]{2,1,0:T(8,128)(2,1)S(1)}, u32[]{:S(2)}, u32[]{:S(2)}) %collective-permute-start.3) | collective-permute-done | bytes 344096 | tf_op jit(solution)/shard_map/ppermute | solution.py:350
  82.1 1.8 collective-permute-start.5
  84.4 11.1 %collective-permute-done.4.refs_2_ = bf16[4,336,128]{2,1,0:T(8,128)(2,1)S(1)} collective-permute-done((bf16[4,336,128]{2,1,0:T(8,128)(2,1)S(1)}, bf16[4,336,128]{2,1,0:T(8,128)(2,1)S(1)}, u32[]{:S(2)}, u32[]{:S(2)}) %collective-permute-start.4) | collective-permute-done | bytes 344096 | tf_op jit(solution)/shard_map/ppermute | solution.py:361
  95.5 3.7 %collective-permute-done.5.refs_3_ = bf16[4,336,128]{2,1,0:T(8,128)(2,1)S(1)} collective-permute-done((bf16[4,336,128]{2,1,0:T(8,128)(2,1)S(1)}, bf16[4,336,128]{2,1,0:T(8,128)(2,1)S(1)}, u32[]{:S(2)}, u32[]{:S(2)}) %collective-permute-start.5) | collective-permute-done | bytes 344096 | tf_op jit(solution)/shard_map/ppermute | solution.py:361
  100.8 2.1 %shard_map.68 = (bf16[512,2560]{1,0:T(8,128)(2,1)S(1)}, f32[320,512]{1,0:T(8,128)S(1)}, f32[8,128]{1,0:T(8,128)S(1)}) custom-call(f32[320,640]{1,0:T(8,128)S(1)} %copy-done.2, bf16[4,336,128]{2,1,0:T(8,128)(2,1)S(1)} %pad_maximum_fusion.refs_0_, bf16[4,336,128]{2,1,0:T(8,128)(2,1)S(1)} %collective-permute-done.3.refs_1_, ...), custom_call_target="tpu_custom_call" | custom-call | tf_op jit(solution)/shard_map/pallas_call | solution.py:399
  102.9 6.3 %shard_map.71 = (f32[160,512]{1,0:T(8,128)S(1)}, f32[160,512]{1,0:T(8,128)S(1)}) custom-call(bf16[320,640]{1,0:T(8,128)(2,1)S(1)} %copy-done.1, bf16[320,640]{1,0:T(8,128)(2,1)S(1)} %collective-permute-done.10.refs_1_, bf16[320,640]{1,0:T(8,128)(2,1)S(1)} %collective-permute-done.11.refs_2_, bf16[320,640]{1,0:T(8,128)(2,1)S(1)} %collective-permute-done.12.refs_3_, ...), custom_call_target="tpu_custom_call" | custom-call | tf_op jit(solution)/shard_map/pallas_call | solution.py:407
  110.9 2.5 %collective-permute-start.31 = (f32[160,512]{1,0:T(8,128)S(1)}, f32[160,512]{1,0:T(8,128)S(1)}, u32[]{:S(2)}, u32[]{:S(2)}) collective-permute-start(f32[160,512]{1,0:T(8,128)S(1)} %add.31), channel_id=1, source_target_pairs={{0,16},{8,24},{16,0},{24,8},{1,17},{9,25},{17,1},{25,9},{2,18},{10... | collective-permute-start | bytes 983048 | tf_op jit(solution)/shard_map/ppermute | solution.py:361
  113.5 1.9 %collective-permute-start.27 = (bf16[320,2560]{1,0:T(8,128)(2,1)S(1)}, bf16[320,2560]{1,0:T(8,128)(2,1)S(1)}, u32[]{:S(2)}, u32[]{:S(2)}) collective-permute-start(bf16[320,2560]{1,0:T(8,128)(2,1)S(1)} %get-tuple-element.20.refs_15_), channel_id=1, source_target_pairs={{0,8},{1,9},{10,2},{11,3},{20,28},{21,29},{30,22},{31,23}} | collective-permute-start | bytes 4915208 | tf_op jit(solution)/shard_map/ppermute | solution.py:454
  116.3 5.2 %collective-permute-done.31 = f32[160,512]{1,0:T(8,128)S(1)} collective-permute-done((f32[160,512]{1,0:T(8,128)S(1)}, f32[160,512]{1,0:T(8,128)S(1)}, u32[]{:S(2)}, u32[]{:S(2)}) %collective-permute-start.31) | collective-permute-done | bytes 327712 | tf_op jit(solution)/shard_map/ppermute | solution.py:361
  122.2 1.8 collective-permute-start.26
  124.7 2.1 %collective-permute-start.33 = (f32[64,640]{1,0:T(8,128)S(1)}, f32[64,640]{1,0:T(8,128)S(1)}, u32[]{:S(2)}, u32[]{:S(2)}) collective-permute-start(f32[64,640]{1,0:T(8,128)S(1)} %get-tuple-element.25), channel_id=1, source_target_pairs={{0,1},{1,0},{2,3},{3,2},{4,5},{5,4},{6,7},{7,6},{8,9},{9,8},{10,11... | collective-permute-start | bytes 491528 | tf_op jit(solution)/shard_map/ppermute | solution.py:361
  126.8 4.2 %collective-permute-done.33 = f32[64,640]{1,0:T(8,128)S(1)} collective-permute-done((f32[64,640]{1,0:T(8,128)S(1)}, f32[64,640]{1,0:T(8,128)S(1)}, u32[]{:S(2)}, u32[]{:S(2)}) %collective-permute-start.33) | collective-permute-done | bytes 163872 | tf_op jit(solution)/shard_map/ppermute | solution.py:361
  131.1 5.4 %collective-permute-done.34 = f32[64,640]{1,0:T(8,128)S(1)} collective-permute-done((f32[64,640]{1,0:T(8,128)S(1)}, f32[64,640]{1,0:T(8,128)S(1)}, u32[]{:S(2)}, u32[]{:S(2)}) %collective-permute-start.34) | collective-permute-done | bytes 163872 | tf_op jit(solution)/shard_map/ppermute | solution.py:361
  136.6 8.9 %collective-permute-done.35 = f32[64,640]{1,0:T(8,128)S(1)} collective-permute-done((f32[64,640]{1,0:T(8,128)S(1)}, f32[64,640]{1,0:T(8,128)S(1)}, u32[]{:S(2)}, u32[]{:S(2)}) %collective-permute-start.35) | collective-permute-done | bytes 163872 | tf_op jit(solution)/shard_map/ppermute | solution.py:361
  145.5 2.2 %collective-permute-start.36 = (f32[64,640]{1,0:T(8,128)S(1)}, f32[64,640]{1,0:T(8,128)S(1)}, u32[]{:S(2)}, u32[]{:S(2)}) collective-permute-start(f32[64,640]{1,0:T(8,128)S(1)} %add.35.refs_0_), channel_id=1, source_target_pairs={{0,16},{8,24},{16,0},{24,8},{1,17},{9,25},{17,1},{25,9},{2,18},{10... | collective-permute-start | bytes 491528 | tf_op jit(solution)/shard_map/ppermute | solution.py:361
  148.2 3.8 %collective-permute-done.36.refs_1_ = f32[64,640]{1,0:T(8,128)S(1)} collective-permute-done((f32[64,640]{1,0:T(8,128)S(1)}, f32[64,640]{1,0:T(8,128)S(1)}, u32[]{:S(2)}, u32[]{:S(2)}) %collective-permute-start.36) | collective-permute-done | bytes 163872 | tf_op jit(solution)/shard_map/ppermute | solution.py:361
  153.8 23.3 %shard_map.73 = f32[320,128]{1,0:T(8,128)} custom-call(f32[64,640]{1,0:T(8,128)S(1)} %add.35.refs_0_, f32[64,640]{1,0:T(8,128)S(1)} %collective-permute-done.36.refs_1_, f32[64,640]{1,0:T(8,128)S(1)} %collective-permute-done.37.refs_2_, f32[64,640]{1,0:T(8,128)S(1)} %collective-permute-done.38.refs_3_, f32[320,512]{1,0:T(8,128)S(1)} %get-tuple-element.26.refs_4_), custom_call_target="tpu_custom_call" | custom-call | tf_op jit(solution)/shard_map/pallas_call | solution.py:427
  177.0 4.5 %shard_map.70 = f32[320,640]{1,0:T(8,128)} custom-call(bf16[320,640]{1,0:T(8,128)(2,1)S(1)} %copy-done.1, bf16[320,640]{1,0:T(8,128)(2,1)S(1)} %collective-permute-done.10.refs_1_, bf16[320,640]{1,0:T(8,128)(2,1)S(1)} %collective-permute-done.11.refs_2_, bf16[320,640]{1,0:T(8,128)(2,1)S(1)} %collective-permute-done.12.refs_3_, ...), custom_call_target="tpu_custom_call" | custom-call | tf_op jit(solution)/shard_map/pallas_call | solution.py:457
  (72 shorter events, 22.1 us)
Async XLA Ops:
  0.6 14.6 %collective-permute-start.13 = (bf16[320,640]{1,0:T(8,128)(2,1)}, bf16[320,640]{1,0:T(8,128)(2,1)S(1)}, u32[]{:S(2)}, u32[]{:S(2)}) collective-permute-start(bf16[320,640]{1,0:T(8,128)(2,1)} %refs_0_.5), channel_id=1, source_target_pairs={{2,0},{3,1},{4,2},{5,3},{6,4},{7,5},{10,8},{11,9},{12,10},{13,11},... | collective-permute-start | bytes 1228808 | tf_op jit(solution)/shard_map/ppermute | solution.py:354
  1.9 14.6 %collective-permute-start.12 = (bf16[320,640]{1,0:T(8,128)(2,1)}, bf16[320,640]{1,0:T(8,128)(2,1)S(1)}, u32[]{:S(2)}, u32[]{:S(2)}) collective-permute-start(bf16[320,640]{1,0:T(8,128)(2,1)} %refs_0_.5), channel_id=1, source_target_pairs={{0,2},{1,3},{2,4},{3,5},{4,6},{5,7},{8,10},{9,11},{10,12},{11,13},... | collective-permute-start | bytes 1228808 | tf_op jit(solution)/shard_map/ppermute | solution.py:354
  15.3 12.5 %collective-permute-start.17 = (bf16[320,640]{1,0:T(8,128)(2,1)S(1)}, bf16[320,640]{1,0:T(8,128)(2,1)S(1)}, u32[]{:S(2)}, u32[]{:S(2)}) collective-permute-start(bf16[320,640]{1,0:T(8,128)(2,1)S(1)} %collective-permute-done.13.refs_4_), channel_id=1, source_target_pairs={{2,0},{3,1},{4,2},{5,3},{10,8},{11,9},{12,10},{13,11},{18,16},{19,... | collective-permute-start | bytes 1228808 | tf_op jit(solution)/shard_map/ppermute | solution.py:354
  16.6 12.5 %collective-permute-start.16 = (bf16[320,640]{1,0:T(8,128)(2,1)S(1)}, bf16[320,640]{1,0:T(8,128)(2,1)S(1)}, u32[]{:S(2)}, u32[]{:S(2)}) collective-permute-start(bf16[320,640]{1,0:T(8,128)(2,1)S(1)} %collective-permute-done.12.refs_3_), channel_id=1, source_target_pairs={{2,4},{3,5},{4,6},{5,7},{10,12},{11,13},{12,14},{13,15},{18,20},{1... | collective-permute-start | bytes 1228808 | tf_op jit(solution)/shard_map/ppermute | solution.py:354
  17.3 12.6 %collective-permute-start.10 = (bf16[320,640]{1,0:T(8,128)(2,1)}, bf16[320,640]{1,0:T(8,128)(2,1)S(1)}, u32[]{:S(2)}, u32[]{:S(2)}) collective-permute-start(bf16[320,640]{1,0:T(8,128)(2,1)} %refs_0_.5), channel_id=1, source_target_pairs={{0,1},{1,0},{2,3},{3,2},{4,5},{5,4},{6,7},{7,6},{8,9},{9,8},{10,11... | collective-permute-start | bytes 1228808 | tf_op jit(solution)/shard_map/ppermute | solution.py:350
  19.0 18.5 %collective-permute-start.15 = (bf16[320,640]{1,0:T(8,128)(2,1)S(1)}, bf16[320,640]{1,0:T(8,128)(2,1)S(1)}, u32[]{:S(2)}, u32[]{:S(2)}) collective-permute-start(bf16[320,640]{1,0:T(8,128)(2,1)S(1)} %collective-permute-done.13.refs_4_), channel_id=1, source_target_pairs={{0,1},{1,0},{2,3},{3,2},{8,9},{9,8},{10,11},{11,10},{16,17},{17,16... | collective-permute-start | bytes 1228808 | tf_op jit(solution)/shard_map/ppermute | solution.py:350
  21.2 19.6 %collective-permute-start.14 = (bf16[320,640]{1,0:T(8,128)(2,1)S(1)}, bf16[320,640]{1,0:T(8,128)(2,1)S(1)}, u32[]{:S(2)}, u32[]{:S(2)}) collective-permute-start(bf16[320,640]{1,0:T(8,128)(2,1)S(1)} %collective-permute-done.12.refs_3_), channel_id=1, source_target_pairs={{4,5},{5,4},{6,7},{7,6},{12,13},{13,12},{14,15},{15,14},{20,21},{2... | collective-permute-start | bytes 1228808 | tf_op jit(solution)/shard_map/ppermute | solution.py:350
  27.8 13.8 %collective-permute-start.21 = (bf16[320,640]{1,0:T(8,128)(2,1)S(1)}, bf16[320,640]{1,0:T(8,128)(2,1)S(1)}, u32[]{:S(2)}, u32[]{:S(2)}) collective-permute-start(bf16[320,640]{1,0:T(8,128)(2,1)S(1)} %collective-permute-done.17.refs_8_), channel_id=1, source_target_pairs={{2,0},{3,1},{10,8},{11,9},{18,16},{19,17},{26,24},{27,25}} | collective-permute-start | bytes 1228808 | tf_op jit(solution)/shard_map/ppermute | solution.py:354
  29.1 14.9 %collective-permute-start.20 = (bf16[320,640]{1,0:T(8,128)(2,1)S(1)}, bf16[320,640]{1,0:T(8,128)(2,1)S(1)}, u32[]{:S(2)}, u32[]{:S(2)}) collective-permute-start(bf16[320,640]{1,0:T(8,128)(2,1)S(1)} %collective-permute-done.16.refs_7_), channel_id=1, source_target_pairs={{4,6},{5,7},{12,14},{13,15},{20,22},{21,23},{28,30},{29,31}} | collective-permute-start | bytes 1228808 | tf_op jit(solution)/shard_map/ppermute | solution.py:354
  29.9 14.9 %collective-permute-start.11 = (bf16[320,640]{1,0:T(8,128)(2,1)S(1)}, bf16[320,640]{1,0:T(8,128)(2,1)S(1)}, u32[]{:S(2)}, u32[]{:S(2)}) collective-permute-start(bf16[320,640]{1,0:T(8,128)(2,1)S(1)} %collective-permute-done.10.refs_1_), channel_id=1, source_target_pairs={{0,2},{1,3},{6,4},{7,5},{8,10},{9,11},{14,12},{15,13},{16,18},{17,... | collective-permute-start | bytes 1228808 | tf_op jit(solution)/shard_map/ppermute | solution.py:368
  37.4 14.2 %collective-permute-start.19 = (bf16[320,640]{1,0:T(8,128)(2,1)S(1)}, bf16[320,640]{1,0:T(8,128)(2,1)S(1)}, u32[]{:S(2)}, u32[]{:S(2)}) collective-permute-start(bf16[320,640]{1,0:T(8,128)(2,1)S(1)} %collective-permute-done.17.refs_8_), channel_id=1, source_target_pairs={{0,1},{1,0},{2,3},{3,2},{8,9},{9,8},{10,11},{11,10},{16,17},{17,16... | collective-permute-start | bytes 1228808 | tf_op jit(solution)/shard_map/ppermute | solution.py:350
  40.9 10.8 %collective-permute-start.18 = (bf16[320,640]{1,0:T(8,128)(2,1)S(1)}, bf16[320,640]{1,0:T(8,128)(2,1)S(1)}, u32[]{:S(2)}, u32[]{:S(2)}) collective-permute-start(bf16[320,640]{1,0:T(8,128)(2,1)S(1)} %collective-permute-done.16.refs_7_), channel_id=1, source_target_pairs={{4,5},{5,4},{6,7},{7,6},{12,13},{13,12},{14,15},{15,14},{20,21},{2... | collective-permute-start | bytes 1228808 | tf_op jit(solution)/shard_map/ppermute | solution.py:350
  41.6 15.8 %collective-permute-start.23 = (bf16[320,640]{1,0:T(8,128)(2,1)S(1)}, bf16[320,640]{1,0:T(8,128)(2,1)S(1)}, u32[]{:S(2)}, u32[]{:S(2)}) collective-permute-start(bf16[320,640]{1,0:T(8,128)(2,1)S(1)} %collective-permute-done.21.refs_12_), channel_id=1, source_target_pairs={{0,1},{1,0},{8,9},{9,8},{16,17},{17,16},{24,25},{25,24}} | collective-permute-start | bytes 1228808 | tf_op jit(solution)/shard_map/ppermute | solution.py:350
  44.0 13.3 %collective-permute-start.22 = (bf16[320,640]{1,0:T(8,128)(2,1)S(1)}, bf16[320,640]{1,0:T(8,128)(2,1)S(1)}, u32[]{:S(2)}, u32[]{:S(2)}) collective-permute-start(bf16[320,640]{1,0:T(8,128)(2,1)S(1)} %collective-permute-done.20.refs_11_), channel_id=1, source_target_pairs={{6,7},{7,6},{14,15},{15,14},{22,23},{23,22},{30,31},{31,30}} | collective-permute-start | bytes 1228808 | tf_op jit(solution)/shard_map/ppermute | solution.py:350
  62.6 52.8 %collective-permute-start.28 = (bf16[320,2560]{1,0:T(8,128)(2,1)S(1)}, bf16[320,2560]{1,0:T(8,128)(2,1)S(1)}, u32[]{:S(2)}, u32[]{:S(2)}) collective-permute-start(bf16[320,2560]{1,0:T(8,128)(2,1)S(1)} %get-tuple-element.20.refs_15_), channel_id=1, source_target_pairs={{0,16},{1,17},{10,26},{11,27},{20,4},{21,5},{30,14},{31,15}} | collective-permute-start | bytes 4915208 | tf_op jit(solution)/shard_map/ppermute | solution.py:454
  67.7 7.0 %collective-permute-start.1 = (bf16[336,128]{1,0:T(8,128)(2,1)S(1)}, bf16[336,128]{1,0:T(8,128)(2,1)S(1)}, u32[]{:S(2)}, u32[]{:S(2)}) collective-permute-start(bf16[336,128]{1,0:T(8,128)(2,1)S(1)} %shard_map.67), channel_id=1, source_target_pairs={{0,4},{1,5},{2,6},{3,7},{4,0},{5,1},{6,2},{7,3},{8,12},{9,13},{10,... | collective-permute-start | bytes 258056 | tf_op jit(solution)/shard_map/ppermute | solution.py:358
  67.7 7.0 %collective-permute-start = (bf16[336,128]{1,0:T(8,128)(2,1)S(1)}, bf16[336,128]{1,0:T(8,128)(2,1)S(1)}, u32[]{:S(2)}, u32[]{:S(2)}) collective-permute-start(bf16[336,128]{1,0:T(8,128)(2,1)S(1)} %shard_map.67), channel_id=1, source_target_pairs={{0,2},{1,3},{2,4},{3,5},{4,6},{5,7},{6,0},{7,1},{8,10},{9,11},{10,... | collective-permute-start | bytes 258056 | tf_op jit(solution)/shard_map/ppermute | solution.py:358
  74.8 7.3 %collective-permute-start.3 = (bf16[4,336,128]{2,1,0:T(8,128)(2,1)S(1)}, bf16[4,336,128]{2,1,0:T(8,128)(2,1)S(1)}, u32[]{:S(2)}, u32[]{:S(2)}) collective-permute-start(bf16[4,336,128]{2,1,0:T(8,128)(2,1)S(1)} %pad_maximum_fusion.refs_0_), channel_id=1, source_target_pairs={{0,1},{1,0},{2,3},{3,2},{4,5},{5,4},{6,7},{7,6},{8,9},{9,8},{10,11... | collective-permute-start | bytes 1032200 | tf_op jit(solution)/shard_map/ppermute | solution.py:350
  76.9 18.6 %collective-permute-start.4 = (bf16[4,336,128]{2,1,0:T(8,128)(2,1)S(1)}, bf16[4,336,128]{2,1,0:T(8,128)(2,1)S(1)}, u32[]{:S(2)}, u32[]{:S(2)}) collective-permute-start(bf16[4,336,128]{2,1,0:T(8,128)(2,1)S(1)} %pad_maximum_fusion.refs_0_), channel_id=1, source_target_pairs={{0,16},{8,24},{16,0},{24,8},{1,17},{9,25},{17,1},{25,9},{2,18},{10... | collective-permute-start | bytes 1032200 | tf_op jit(solution)/shard_map/ppermute | solution.py:361
  82.1 17.0 %collective-permute-start.5 = (bf16[4,336,128]{2,1,0:T(8,128)(2,1)S(1)}, bf16[4,336,128]{2,1,0:T(8,128)(2,1)S(1)}, u32[]{:S(2)}, u32[]{:S(2)}) collective-permute-start(bf16[4,336,128]{2,1,0:T(8,128)(2,1)S(1)} %collective-permute-done.3.refs_1_), channel_id=1, source_target_pairs={{0,16},{8,24},{16,0},{24,8},{1,17},{9,25},{17,1},{25,9},{2,18},{10... | collective-permute-start | bytes 1032200 | tf_op jit(solution)/shard_map/ppermute | solution.py:361
  83.9 15.3 %collective-permute-start.6 = (bf16[4,336,128]{2,1,0:T(8,128)(2,1)S(1)}, bf16[4,336,128]{2,1,0:T(8,128)(2,1)S(1)}, u32[]{:S(2)}, u32[]{:S(2)}) collective-permute-start(bf16[4,336,128]{2,1,0:T(8,128)(2,1)S(1)} %pad_maximum_fusion.refs_0_), channel_id=1, source_target_pairs={{0,8},{8,0},{16,24},{24,16},{1,9},{9,1},{17,25},{25,17},{2,10},{10... | collective-permute-start | bytes 1032200 | tf_op jit(solution)/shard_map/ppermute | solution.py:361
  83.9 15.3 %collective-permute-start.7 = (bf16[4,336,128]{2,1,0:T(8,128)(2,1)S(1)}, bf16[4,336,128]{2,1,0:T(8,128)(2,1)S(1)}, u32[]{:S(2)}, u32[]{:S(2)}) collective-permute-start(bf16[4,336,128]{2,1,0:T(8,128)(2,1)S(1)} %collective-permute-done.3.refs_1_), channel_id=1, source_target_pairs={{0,8},{8,0},{16,24},{24,16},{1,9},{9,1},{17,25},{25,17},{2,10},{10... | collective-permute-start | bytes 1032200 | tf_op jit(solution)/shard_map/ppermute | solution.py:361
  109.4 12.8 %collective-permute-start.25 = (f32[320,640]{1,0:T(8,128)S(1)}, f32[320,640]{1,0:T(8,128)S(1)}, u32[]{:S(2)}, u32[]{:S(2)}) collective-permute-start(f32[320,640]{1,0:T(8,128)S(1)} %get-tuple-element.19), channel_id=1, source_target_pairs={{0,8},{8,0},{16,24},{24,16},{1,9},{9,1},{17,25},{25,17},{2,10},{10... | collective-permute-start | bytes 2457608 | tf_op jit(solution)/shard_map/ppermute | solution.py:361
  110.9 10.6 %collective-permute-start.31 = (f32[160,512]{1,0:T(8,128)S(1)}, f32[160,512]{1,0:T(8,128)S(1)}, u32[]{:S(2)}, u32[]{:S(2)}) collective-permute-start(f32[160,512]{1,0:T(8,128)S(1)} %add.31), channel_id=1, source_target_pairs={{0,16},{8,24},{16,0},{24,8},{1,17},{9,25},{17,1},{25,9},{2,18},{10... | collective-permute-start | bytes 983048 | tf_op jit(solution)/shard_map/ppermute | solution.py:361
  113.5 63.6 %collective-permute-start.27 = (bf16[320,2560]{1,0:T(8,128)(2,1)S(1)}, bf16[320,2560]{1,0:T(8,128)(2,1)S(1)}, u32[]{:S(2)}, u32[]{:S(2)}) collective-permute-start(bf16[320,2560]{1,0:T(8,128)(2,1)S(1)} %get-tuple-element.20.refs_15_), channel_id=1, source_target_pairs={{0,8},{1,9},{10,2},{11,3},{20,28},{21,29},{30,22},{31,23}} | collective-permute-start | bytes 4915208 | tf_op jit(solution)/shard_map/ppermute | solution.py:454
  115.4 61.7 %collective-permute-start.29 = (bf16[320,2560]{1,0:T(8,128)(2,1)S(1)}, bf16[320,2560]{1,0:T(8,128)(2,1)S(1)}, u32[]{:S(2)}, u32[]{:S(2)}) collective-permute-start(bf16[320,2560]{1,0:T(8,128)(2,1)S(1)} %collective-permute-done.28.refs_17_), channel_id=1, source_target_pairs={{16,24},{17,25},{26,18},{27,19},{4,12},{5,13},{14,6},{15,7}} | collective-permute-start | bytes 4915208 | tf_op jit(solution)/shard_map/ppermute | solution.py:454
  121.6 26.6 %collective-permute-start.24 = (f32[320,640]{1,0:T(8,128)S(1)}, f32[320,640]{1,0:T(8,128)S(1)}, u32[]{:S(2)}, u32[]{:S(2)}) collective-permute-start(f32[320,640]{1,0:T(8,128)S(1)} %get-tuple-element.17), channel_id=1, source_target_pairs={{0,8},{8,0},{16,24},{24,16},{1,9},{9,1},{17,25},{25,17},{2,10},{10... | collective-permute-start | bytes 2457608 | tf_op jit(solution)/shard_map/ppermute | solution.py:361
  122.2 29.8 %collective-permute-start.26 = (f32[320,640]{1,0:T(8,128)S(1)}, f32[320,640]{1,0:T(8,128)S(1)}, u32[]{:S(2)}, u32[]{:S(2)}) collective-permute-start(f32[320,640]{1,0:T(8,128)S(1)} %add.28), channel_id=1, source_target_pairs={{0,16},{8,24},{16,0},{24,8},{1,17},{9,25},{17,1},{25,9},{2,18},{10... | collective-permute-start | bytes 2457608 | tf_op jit(solution)/shard_map/ppermute | solution.py:361
  124.7 6.3 %collective-permute-start.33 = (f32[64,640]{1,0:T(8,128)S(1)}, f32[64,640]{1,0:T(8,128)S(1)}, u32[]{:S(2)}, u32[]{:S(2)}) collective-permute-start(f32[64,640]{1,0:T(8,128)S(1)} %get-tuple-element.25), channel_id=1, source_target_pairs={{0,1},{1,0},{2,3},{3,2},{4,5},{5,4},{6,7},{7,6},{8,9},{9,8},{10,11... | collective-permute-start | bytes 491528 | tf_op jit(solution)/shard_map/ppermute | solution.py:361
  136.5 9.0 %collective-permute-start.35 = (f32[64,640]{1,0:T(8,128)S(1)}, f32[64,640]{1,0:T(8,128)S(1)}, u32[]{:S(2)}, u32[]{:S(2)}) collective-permute-start(f32[64,640]{1,0:T(8,128)S(1)} %add.34), channel_id=1, source_target_pairs={{0,4},{1,5},{2,6},{3,7},{4,0},{5,1},{6,2},{7,3},{8,12},{9,13},{10,... | collective-permute-start | bytes 491528 | tf_op jit(solution)/shard_map/ppermute | solution.py:361
  145.5 6.5 %collective-permute-start.36 = (f32[64,640]{1,0:T(8,128)S(1)}, f32[64,640]{1,0:T(8,128)S(1)}, u32[]{:S(2)}, u32[]{:S(2)}) collective-permute-start(f32[64,640]{1,0:T(8,128)S(1)} %add.35.refs_0_), channel_id=1, source_target_pairs={{0,16},{8,24},{16,0},{24,8},{1,17},{9,25},{17,1},{25,9},{2,18},{10... | collective-permute-start | bytes 491528 | tf_op jit(solution)/shard_map/ppermute | solution.py:361
  148.2 5.5 %collective-permute-start.37 = (f32[64,640]{1,0:T(8,128)S(1)}, f32[64,640]{1,0:T(8,128)S(1)}, u32[]{:S(2)}, u32[]{:S(2)}) collective-permute-start(f32[64,640]{1,0:T(8,128)S(1)} %add.35.refs_0_), channel_id=1, source_target_pairs={{0,8},{8,0},{16,24},{24,16},{1,9},{9,1},{17,25},{25,17},{2,10},{10... | collective-permute-start | bytes 491528 | tf_op jit(solution)/shard_map/ppermute | solution.py:361
  (12 other events, 120.0 us)

commit v4 on v3

v4 whole, which is shorter than its diff:
```python
import functools

import jax
import jax.numpy as jnp
from jax import lax
from jax.experimental import pallas as pl
from jax.experimental.pallas import tpu as pltpu
from jax.sharding import PartitionSpec as P

smoothing = 0.95
clip_ratio = 4.0
epsilon_value = 1e-06
HI = lax.Precision.HIGHEST
BLOCK, PANEL = 128, 8


def factor_block(sides, column_ref):
    w = PANEL
    sub = lax.broadcasted_iota(jnp.int32, (w, BLOCK), 0)
    full = lambda v: jnp.broadcast_to(v, (w, BLOCK))
    for p in range(BLOCK // w):
        c0 = p * w
        left = sides[0][c0 : c0 + w, :]
        cols = [full(left[:, c0 + k : c0 + k + 1]) for k in range(w)]
        for k in range(w):
            column_ref[k * w : k * w + w, :] = cols[k]
        e = {(i, k): column_ref[pl.ds(k * w + i, w, stride=0), :] for i in range(w) for k in range(i + 1)}
        rows = [[t[pl.ds(c0 + i, w, stride=0), :] for t in sides] for i in range(w)]
        l, inverse, root, done = {}, {}, [], [None] * w
        for j in range(0, w, 2):
            a, b, c = e[j, j], e[j + 1, j], e[j + 1, j + 1]
            r = 1.0 / (a * c - b * b)
            ar, br, cr = a * r, b * r, c * r
            inverse[j] = ar, br, cr
            slope = b / a
            root += [lax.rsqrt(a), lax.rsqrt(c - b * slope)]
            done[j] = rows[j]
            done[j + 1] = [y - slope * x for x, y in zip(rows[j], rows[j + 1])]
            for i in range(j + 2, w):
                x, y = e[i, j], e[i, j + 1]
                l[i, j], l[i, j + 1] = x * cr - y * br, y * ar - x * br
            for i in range(j + 2, w):
                for k in range(j + 2, i + 1):
                    e[i, k] = e[i, k] - (l[i, j] * e[k, j] + l[i, j + 1] * e[k, j + 1])
                rows[i] = [z - (l[i, j] * x + l[i, j + 1] * y) for x, y, z in zip(rows[j], rows[j + 1], rows[i])]
        for n, side in enumerate(sides):
            out = root[0] * done[0][n]
            for i in range(1, w):
                out = jnp.where(sub == i, root[i] * done[i][n], out)
            side[c0 : c0 + w, :] = out
        if c0 + w == BLOCK:
            break
        v = [None] * w
        for j in reversed(range(0, w, 2)):
            ar, br, cr = inverse[j]
            x, y = rows[j], rows[j + 1]
            v[j] = [cr * a - br * b for a, b in zip(x, y)]
            v[j + 1] = [ar * b - br * a for a, b in zip(x, y)]
            for k in (j, j + 1):
                for i in range(j + 2, w):
                    v[k] = [a - l[i, k] * b for a, b in zip(v[k], v[i])]
        for q in range(p + 1, BLOCK // w):
            at = slice(q * w, q * w + w)
            old = [t[at, :] for t in sides]
            c = [full(old[0][:, c0 + k : c0 + k + 1]) for k in range(w)]
            for n, side in enumerate(sides):
                terms = [c[k] * v[k][n] for k in range(w)]
                while len(terms) > 1:
                    terms = [a + b for a, b in zip(terms[::2], terms[1::2])]
                side[at, :] = old[n] - terms[0]


GRANT = {"message": 8, "parts": 20, "near": 24, "power": 24, "gram": 12, "basis": 16, "sides": 24, "right": 20, "left": 8, "last": 8}


def strip_of(order, roles, role, which):
    height = order // (2 * roles)
    strip = role if which == 0 else 2 * roles - 1 - role
    return strip * height, height, strip * height // BLOCK * BLOCK


def packed_width(order, roles):
    return max(
        sum(order - strip_of(order, roles, role, which)[2] for which in (0, 1)) for role in range(roles)
    )


def product(a, b, contract, precision=None):
    return lax.dot_general(
        a, b, ((contract[:1], contract[1:]), ((), ())), precision=precision, preferred_element_type=jnp.float32
    )


def eye(n):
    return (
        lax.broadcasted_iota(jnp.int32, (n, n), 0) == lax.broadcasted_iota(jnp.int32, (n, n), 1)
    ).astype(jnp.float32)


def rounded_parts(value):
    high = value.astype(jnp.bfloat16)
    rest = value - high.astype(jnp.float32)
    middle = rest.astype(jnp.bfloat16)
    return high, middle, (rest - middle.astype(jnp.float32)).astype(jnp.bfloat16)


def late_slots(line):
    line_at = lax.axis_index("shard") // 2
    return ((line_at >= line - 2, line - 2), (line_at < 2, 2))


def near_kernel(count, *refs):
    pieces, (turned_ref, held_ref, sum_ref, sems) = refs[:count], refs[count:]
    line, _, rows, cols = held_ref.shape
    line_at = lax.axis_index("shard") // 2
    side, inward, opposite, low_far, high_far = pieces[1:6]
    moves = [
        (pieces[0], 0, 0, line_at >= 0),
        (side, 0, 1, line_at >= 0),
        (inward, 1, 1, line_at == 1),
        (inward, line - 1, 1, line_at == line - 2),
        (opposite, 1, 1, line_at == 0),
        (opposite, line - 1, 1, line_at == line - 1),
        (high_far, 1, 0, line_at == 0),
        (low_far, line - 1, 0, line_at == line - 1),
    ]
    for by in range(1, line - 1):
        low, high, *sides = pieces[4 * by + 2 : 4 * by + 6]
        skip = 1 if by == 1 else 0
        moves += [(low, by, 0, line_at >= by), (high, line - by, 0, line_at + by < line)]
        if by < line - 2:
            moves += [
                (sides[0], by, 1, line_at >= by + skip),
                (sides[1], line - by, 1, line_at + by + skip < line),
            ]
    for start in (True, False):
        for n, (ref, dz, dx, when) in enumerate(moves):
            copy = pltpu.make_async_copy(ref, held_ref.at[dz, dx], sems.at[n])

            @pl.when(when)
            def _():
                copy.start() if start else copy.wait()

    sum_ref[...] = jnp.zeros_like(sum_ref)
    late = late_slots(line)
    for dz in range(line):
        missing = [when for when, slot in late if slot == dz]
        turned = lambda dx: turned_ref[:, (2 * dz + dx) * rows : (2 * dz + dx + 1) * rows]
        if not missing:
            sum_ref[...] += product(
                turned_ref[:, 2 * dz * rows : 2 * (dz + 1) * rows],
                held_ref[dz].reshape(2 * rows, cols),
                (1, 0),
            )
            continue
        sum_ref[...] += product(turned(0), held_ref[dz, 0], (1, 0))

        @pl.when(jnp.logical_not(functools.reduce(jnp.logical_or, missing)))
        def _():
            sum_ref[...] += product(turned(1), held_ref[dz, 1], (1, 0))


def message_kernel(gradient_ref, basis_ref, out_ref):
    rows, vec = basis_ref.shape
    wide = gradient_ref[...].astype(jnp.float32)
    squares = jnp.broadcast_to(jnp.sum(jnp.sum(wide * wide, axis=0, keepdims=True), axis=1, keepdims=True), (16, vec))
    out_ref[:rows, :] = basis_ref[...]
    at = lax.broadcasted_iota(jnp.int32, (16, vec), 0)
    tail = jnp.zeros((16, vec), jnp.float32)
    for i, part in enumerate(rounded_parts(squares)):
        tail = jnp.where(at == i, part.astype(jnp.float32), tail)
    out_ref[rows:, :] = tail.astype(jnp.bfloat16)


def basis_parts_kernel(order_size, left_ref, *refs):
    given, (turned_ref, old_ref, weight_ref, rows_ref) = refs[:8], refs[8:]
    rows, cols = left_ref.shape
    line, _, vec = given[0].shape
    per_role = cols // rows
    shard_at, role_at = lax.axis_index("shard"), lax.axis_index("role")
    line_at, side_at = shard_at // 2, shard_at % 2
    total = jnp.zeros((1, vec), jnp.float32)
    for bits, refs in zip((0, 2, 1, 3), (given[0:2], given[2:4], given[4:6], given[6:8])):
        at = pl.multiple_of((role_at ^ bits) * vec, BLOCK)
        whole = jnp.concatenate([refs[dx][dz, :rows, :] for dz in range(line) for dx in (0, 1)])
        turned_ref[pl.ds(at, vec), :] = whole.astype(jnp.float32).T.astype(jnp.bfloat16)
        for i in range(per_role):
            shard = role_at * per_role + i
            dz = lax.rem(line_at - shard // 2 + line, line)
            for dx in (0, 1):

                @pl.when((shard + side_at) % 2 == dx)
                def _():
                    rows_ref[i * rows : (i + 1) * rows, pl.ds(at, vec)] = refs[dx][dz, :rows, :]

        for ref in refs:
            for dz in range(line):
                total = total + jnp.sum(ref[dz, rows:, :].astype(jnp.float32), axis=0, keepdims=True)
    factor = jnp.minimum(
        1.0, clip_ratio * jnp.sqrt(jnp.float32(order_size)) / jnp.sqrt(total + epsilon_value)
    )
    weight_ref[...] = jnp.broadcast_to((1.0 - smoothing) * (factor * factor), weight_ref.shape)
    old = jnp.zeros(old_ref.shape, jnp.float32)
    for part in rounded_parts(left_ref[...]):
        old = old + product(part, rows_ref[...], (1, 0))
    old_ref[...] = smoothing * old


def power_kernel(low_ref, high_ref, held_in, sum_ref, turned_ref, old_ref, weight_ref, *refs):
    del held_in
    held_ref, keep_ref, send_ref, part_ref, total_ref, sem = refs
    line, _, rows, _ = held_ref.shape
    total_ref[...] = sum_ref[...]
    for (when, dz), ref in zip(late_slots(line), (low_ref, high_ref)):

        @pl.when(when)
        def _():
            copy = pltpu.make_async_copy(ref, held_ref.at[dz, 1], sem)
            copy.start()
            at = (2 * dz + 1) * rows
            total_ref[...] += product(turned_ref[:, at : at + rows], ref[...], (1, 0))
            copy.wait()

    own = held_ref[0, 0]
    new = jnp.zeros(part_ref.shape, jnp.float32)
    for part in rounded_parts(total_ref[...]):
        new = new + product(own, part, (1, 1))
    part_ref[...] = old_ref[...] + weight_ref[0:1, 0:1] * new
    half = rows // 2
    core_at = lax.axis_index("role") % 2
    for core in (0, 1):

        @pl.when(core_at == core)
        def _():
            keep_ref[...] = part_ref[core * half : (core + 1) * half, :]
            send_ref[...] = part_ref[(1 - core) * half : (2 - core) * half, :]


def gram_kernel(roles, keep_ref, across_ref, out_ref, power_ref):
    order = power_ref.shape[1]
    half = keep_ref.shape[0]
    here = lax.axis_index("role")
    for core in (0, 1):

        @pl.when(here % 2 == core)
        def _():
            power_ref[core * half : (core + 1) * half, :] = keep_ref[...]
            power_ref[(1 - core) * half : (2 - core) * half, :] = across_ref[...]

    for role in range(roles):

        @pl.when(here == role)
        def _():
            at = 0
            for which in (0, 1):
                row, height, first = strip_of(order, roles, role, which)
                out_ref[:, at : at + order - first] = product(
                    power_ref[:, row : row + height], power_ref[:, first:], (0, 0), HI
                )
                at += order - first
            if at < out_ref.shape[1]:
                out_ref[:, at:] = jnp.zeros((out_ref.shape[0], out_ref.shape[1] - at), jnp.float32)


def basis_kernel(roles, *refs):
    given, (power_ref, out_ref, m_ref, left_ref, right_ref, column_ref) = refs[:4], refs[4:]
    n = power_ref.shape[1]
    nb = n // BLOCK
    here = lax.axis_index("role")
    for bits, ref in zip((0, 2, 1, 3), given):
        for role in range(roles):

            @pl.when(here ^ bits == role)
            def _():
                at = 0
                for which in (0, 1):
                    row, height, first = strip_of(n, roles, role, which)
                    m_ref[row : row + height, first:n] = ref[:, at : at + n - first]
                    at += n - first

    m_ref[:, n:] = eye(n)

    down, along = [], []
    for c in range(nb):
        at = slice(c * BLOCK, (c + 1) * BLOCK)
        diagonal = jnp.where(eye(BLOCK) > 0, m_ref[at, at], 0.0)
        down.append(lax.rsqrt(jnp.sum(diagonal, axis=1, keepdims=True)))
        along.append(lax.rsqrt(jnp.sum(diagonal, axis=0, keepdims=True)))
    along = jnp.concatenate(along, axis=1)
    for c in range(nb):
        at = slice(c * BLOCK, (c + 1) * BLOCK)
        m_ref[at, c * BLOCK : n] = m_ref[at, c * BLOCK : n] * down[c] * along[:, c * BLOCK :]

    @pl.loop(0, nb)
    def _(b):
        start = pl.multiple_of(b * BLOCK, BLOCK)
        left_ref[...] = m_ref[pl.ds(start, BLOCK), pl.ds(start, BLOCK)]
        right_ref[...] = eye(BLOCK)
        factor_block((left_ref, right_ref), column_ref)
        for c in range(nb):

            @pl.when(b == c)
            def _():
                lo, hi = c * BLOCK, n + (c + 1) * BLOCK
                rows = right_ref[...]
                if nb > 1:
                    others = product(rows, m_ref[lo : lo + BLOCK, lo + BLOCK : hi - BLOCK], (1, 0), HI)
                    rows = jnp.concatenate([others, rows], axis=1)
                m_ref[lo : lo + BLOCK, lo + BLOCK : hi] = rows
                for d in range(c + 1, nb):
                    at = d * BLOCK
                    shift = (d - c - 1) * BLOCK
                    m_ref[at : at + BLOCK, at:hi] -= product(
                        rows[:, shift : shift + BLOCK], rows[:, shift:], (0, 0), HI
                    )

    width = out_ref.shape[1]
    mine = pl.multiple_of(here * width, BLOCK)
    out_ref[...] = product(power_ref[...], m_ref[pl.ds(mine, width), n:] * along, (1, 1), HI)


def sides_kernel(held_ref, *refs):
    *outs, slab_ref, block_ref = refs
    line, _, rows, cols = held_ref.shape
    per_role = cols // rows
    shard_at, role_at = lax.axis_index("shard"), lax.axis_index("role")
    line_at, side_at = shard_at // 2, shard_at % 2
    own = held_ref[0, 0]
    for bits, out in zip((3, 1, 2, 0), outs):
        for i in range(per_role):
            shard = (role_at ^ bits) * per_role + i
            dz = lax.rem(line_at - shard // 2 + line, line)
            block_ref[i * rows : (i + 1) * rows, :] = held_ref[dz, (shard + side_at) % 2]
        out[...] = product(own, block_ref[...], (1, 1))
    for i in range(per_role):

        @pl.when(shard_at % per_role == i)
        def _():
            slab = held_ref[:, :, :, i * rows : (i + 1) * rows].reshape(2 * line * rows, rows)
            slab_ref[...] = slab.astype(jnp.float32).T.astype(jnp.bfloat16)


def left_kernel(old_ref, own_ref, core_ref, weight_ref, out_ref):
    out_ref[...] = smoothing * old_ref[...] + weight_ref[0:1, 0:1] * (own_ref[...] + core_ref[...])


def last_kernel(sum_ref, half_ref, weight_ref, out_ref):
    out_ref[...] = sum_ref[...] + weight_ref[0:1, 0:1] * half_ref[...]


def right_kernel(held_ref, *refs):
    slabs, (old_ref, weight_ref, out_ref) = refs[:4], refs[4:]
    line, _, rows, cols = held_ref.shape
    owner = lax.axis_index("shard") * rows // cols
    for bits, ref in enumerate(slabs):

        @pl.when(lax.axis_index("role") ^ owner == bits)
        def _():
            gram = product(ref[...], held_ref[...].reshape(2 * line * rows, cols), (1, 0))
            out_ref[...] = smoothing * old_ref[...] + weight_ref[0:1, 0:1] * gram


def step(gradient, left_old, right_old, basis_old):
    rows, cols = gradient.shape
    vec = basis_old.shape[1]
    shards, roles = lax.axis_size("shard"), lax.axis_size("role")
    order_size, order = rows * shards, vec * roles
    line = shards // 2

    def other_side(value, first=0, last=line - 1):
        pairs = [(2 * z + x, 2 * z + 1 - x) for z in range(first, last + 1) for x in (0, 1)]
        return lax.ppermute(value, "shard", pairs)

    def along(value, first, last, by):
        pairs = [(2 * z + x, 2 * (z + by) + x) for z in range(first, last + 1) for x in (0, 1)]
        return lax.ppermute(value, "shard", pairs)

    def around(value, by):
        pairs = [(2 * z + x, 2 * ((z + by) % line) + x) for z in range(line) for x in (0, 1)]
        return lax.ppermute(value, "shard", pairs)

    def flip(value, axis, size, bit):
        return lax.ppermute(value, axis, [(i, i ^ bit) for i in range(size)])

    other_core = lambda value: flip(value, "role", roles, 1)
    other_half = lambda value: flip(value, "role", roles, 2)

    side = other_side(gradient)
    inward = [(2 * z + x, 2 * to + x) for z, to in ((0, 1), (line - 1, line - 2)) for x in (0, 1)]
    opposite = [(2 * z + x, 2 * (line - 1 - z) + x) for z in (0, line - 1) for x in (0, 1)]
    chain = []
    low = high = gradient
    for by in range(1, line):
        low = along(low, by - 1, line - 2, 1)
        high = along(high, 1, line - by, -1)
        chain += [low, high]
        if by < line - 1:
            skip = 1 if by == 1 else 0
            chain.append(other_side(low, by + skip, line - 1))
            chain.append(other_side(high, 0, line - 1 - by - skip))
    *chain, low_late, high_late, low_far, high_far = chain
    pieces = [
        gradient,
        side,
        lax.ppermute(side, "shard", inward),
        lax.ppermute(side, "shard", opposite),
        low_far,
        high_far,
        *chain,
    ]

    def call(name, kernel, out_shape, **options):
        return pl.pallas_call(
            kernel,
            out_shape=out_shape,
            compiler_params=pltpu.CompilerParams(vmem_limit_bytes=GRANT[name] << 20),
            **options,
        )

    anywhere = pl.BlockSpec(memory_space=pl.ANY)
    in_vmem = pl.BlockSpec(memory_space=pltpu.VMEM)
    shape = lambda *dims, dtype=jnp.float32: jax.ShapeDtypeStruct(dims, dtype)

    message = call("message", message_kernel, shape(rows + 16, vec, dtype=jnp.bfloat16))(gradient, basis_old)
    column = jnp.stack([message] + [around(message, by) for by in range(1, line)])
    across = other_side(column)
    mine = [column, across]
    yours = [other_half(column), other_half(across)]
    theirs = [other_core(value) for value in mine + yours]
    turned, old_part, weight = call(
        "parts",
        functools.partial(basis_parts_kernel, order_size),
        (shape(order, order_size, dtype=jnp.bfloat16), shape(rows, order), shape(8, BLOCK)),
        scratch_shapes=[pltpu.VMEM((cols, order), jnp.bfloat16)],
    )(left_old, *mine, *yours, *theirs)

    half_rows = rows // 2
    held, turned_sum = call(
        "near",
        functools.partial(near_kernel, len(pieces)),
        (shape(line, 2, rows, cols, dtype=jnp.bfloat16), shape(order, cols)),
        in_specs=[anywhere] * len(pieces) + [in_vmem],
        scratch_shapes=[pltpu.SemaphoreType.DMA((4 * line,))],
    )(*pieces, turned)
    held, keep, send = call(
        "power",
        power_kernel,
        (shape(line, 2, rows, cols, dtype=jnp.bfloat16), shape(half_rows, order), shape(half_rows, order)),
        in_specs=[in_vmem] * 7,
        input_output_aliases={2: 0},
        scratch_shapes=[
            pltpu.VMEM((rows, order), jnp.float32),
            pltpu.VMEM((order, cols), jnp.float32),
            pltpu.SemaphoreType.DMA,
        ],
    )(low_late, high_late, held, turned_sum, turned, old_part, weight)
    keep = keep + other_core(send)
    keep = keep + other_half(keep)

    packed, power = call(
        "gram",
        functools.partial(gram_kernel, roles),
        out_shape=(shape(order // (2 * roles), packed_width(order, roles)), shape(rows, order)),
    )(keep, other_core(keep))
    bit = 1
    while bit < shards:
        packed = packed + flip(packed, "shard", shards, bit)
        bit *= 2
    yours = other_half(packed)
    left_basis = call(
        "basis",
        functools.partial(basis_kernel, roles),
        out_shape=shape(rows, vec),
        scratch_shapes=[
            pltpu.VMEM((order, 2 * order), jnp.float32),
            pltpu.VMEM((BLOCK, BLOCK), jnp.float32),
            pltpu.VMEM((BLOCK, BLOCK), jnp.float32),
            pltpu.VMEM((PANEL * PANEL, BLOCK), jnp.float32),
        ],
    )(packed, yours, other_core(packed), other_core(yours), power)

    *shares, slab = call(
        "sides",
        sides_kernel,
        (shape(rows, cols),) * 4 + (shape(rows, order_size, dtype=jnp.bfloat16),),
        scratch_shapes=[pltpu.VMEM((cols, cols), jnp.bfloat16)],
    )(held)
    away = shares[2] + other_core(shares[0])
    left_sum = call("left", left_kernel, shape(rows, cols))(left_old, shares[3], other_core(shares[1]), weight)
    left_stat = call("last", last_kernel, shape(rows, cols))(left_sum, other_half(away), weight)
    owner_of = lambda shard: shard * rows // cols

    def from_owner(value, source, target):
        pairs = [
            tuple((owner_of(s) ^ bits) * shards + s for bits in (source, target)) for s in range(shards)
        ]
        return lax.ppermute(value, ("role", "shard"), pairs)

    crossed = from_owner(slab, 0, 2)
    right_stat = call("right", right_kernel, shape(rows, cols))(
        held, slab, from_owner(slab, 0, 1), crossed, from_owner(crossed, 2, 3), right_old, weight
    )
    return (left_stat, right_stat, left_basis)


def solution(mesh):
    return jax.shard_map(
        step,
        mesh=mesh,
        in_specs=(P("shard", "role"), P("shard", "role"), P("shard", "role"), P("shard", "role")),
        out_specs=(P("shard", "role"), P("shard", "role"), P("shard", "role")),
        check_vma=False,
    )
```

time: 182 us -> 164 us (0.901)
  waiting for transfers between devices: 82.1 us -> 70.7 us
  Pallas kernels: 41.2 us -> 34.3 us
  starting transfers between devices: 53.7 us -> 56.7 us
    ppermute x3, waiting for transfers between devices: 0.01 us -> 19.4 us  [from_owner(): return lax.ppermute(value, ('role', 'shard'), pairs)]
    ppermute x8 -> x6, waiting for transfers between devices: 17.2 us -> 1.61 us  [other_side(): return lax.ppermute(value, 'shard', pairs)]
    ppermute x18, waiting for transfers between devices: 45 us -> 33.5 us  [flip(): return lax.ppermute(value, axis, [(i, i ^ bit) for i in range(size)])]
    ppermute x1 -> x2, waiting for transfers between devices: 0.01 us -> 10.6 us  [the longest x1 6.85 us: step(): lax.ppermute(side, 'shard', inward)]
    ppermute x6, waiting for transfers between devices: 13.5 us -> 5.59 us  [along(): return lax.ppermute(value, 'shard', pairs)]
    ppermute x3, waiting for transfers between devices: 6.39 us -> 0.01 us  [around(): return lax.ppermute(value, 'shard', pairs)]
    ppermute x18, starting transfers between devices: 13 us -> 18.2 us  [flip(): return lax.ppermute(value, axis, [(i, i ^ bit) for i in range(size)])]
    pallas_call x1, Pallas kernels: 23.3 us -> 18.4 us  [step(): call('basis', functools.partial(basis_kernel, roles), out_shape=shape(row...]
  transfers between devices with their start and end apart: 39 -> 38, of which waited for: 17 -> 15; matrix products, arithmetic and copies ran while one was open for 1% -> 0% of each run, Pallas kernels for 18% -> 16%
where the time goes in v4:
time: 164 us
  waiting for transfers between devices  70.7 us (43%)
  starting transfers between devices  56.7 us (35%)
  Pallas kernels  34.3 us (21%)
    ppermute x18, waiting for transfers between devices, flip(): return lax.ppermute(value, axis, [(i, i ^ bit) for i in range(size)])  33.5 us
    ppermute x3, waiting for transfers between devices, from_owner(): return lax.ppermute(value, ('role', 'shard'), pairs)  19.4 us
    pallas_call x1, Pallas kernels, step(): call('basis', functools.partial(basis_kernel, roles), out_shape=shape(row...  18.4 us
    ppermute x18, starting transfers between devices, flip(): return lax.ppermute(value, axis, [(i, i ^ bit) for i in range(size)])  18.2 us
    ppermute x6, starting transfers between devices, other_side(): return lax.ppermute(value, 'shard', pairs)  10.5 us
    ppermute x6, starting transfers between devices, along(): return lax.ppermute(value, 'shard', pairs)  10.3 us
    ppermute x1, waiting for transfers between devices, step(): lax.ppermute(side, 'shard', inward)  6.85 us
    ppermute x3, starting transfers between devices, around(): return lax.ppermute(value, 'shard', pairs)  6.09 us
  transfers between devices with their start and end apart: 38, of which 15 were waited for; matrix products, arithmetic and copies ran while one was open for 0% of the time, Pallas kernels for 16%

profile of v4, /device:TPU:0, one launch (start us, length us, event | category | flops | bytes accessed | tf_op | source)
XLA Modules:
  0.0 164.0 jit_solution(8828958357074071684)
XLA Ops:
  2.8 5.1 %collective-permute-start.15 = (bf16[336,128]{1,0:T(8,128)(2,1)S(1)}, bf16[336,128]{1,0:T(8,128)(2,1)S(1)}, u32[]{:S(2)}, u32[]{:S(2)}) collective-permute-start(bf16[336,128]{1,0:T(8,128)(2,1)S(1)} %shard_map.67), channel_id=1, source_target_pairs={{0,6},{1,7},{2,0},{3,1},{4,2},{5,3},{6,4},{7,5},{8,14},{9,15},{10,... | collective-permute-start | bytes 258056 | tf_op jit(solution)/shard_map/ppermute | solution.py:380
  8.9 1.5 collective-permute-start.6
  11.6 5.0 %collective-permute-start = (bf16[320,640]{1,0:T(8,128)(2,1)}, bf16[320,640]{1,0:T(8,128)(2,1)S(1)}, u32[]{:S(2)}, u32[]{:S(2)}) collective-permute-start(bf16[320,640]{1,0:T(8,128)(2,1)} %refs_0_.1), channel_id=1, source_target_pairs={{0,2},{1,3},{2,4},{3,5},{4,6},{5,7},{8,10},{9,11},{10,12},{11,13},... | collective-permute-start | bytes 1228808 | tf_op jit(solution)/shard_map/ppermute | solution.py:376
  16.8 1.6 collective-permute-start.17
  19.5 6.0 %collective-permute-done.17.refs_2_ = bf16[4,336,128]{2,1,0:T(8,128)(2,1)S(1)} collective-permute-done((bf16[4,336,128]{2,1,0:T(8,128)(2,1)S(1)}, bf16[4,336,128]{2,1,0:T(8,128)(2,1)S(1)}, u32[]{:S(2)}, u32[]{:S(2)}) %collective-permute-start.17) | collective-permute-done | bytes 344096 | tf_op jit(solution)/shard_map/ppermute | solution.py:383
  25.5 1.3 collective-permute-done.16.refs_1_
  26.8 1.5 collective-permute-start.18
  28.3 5.0 %collective-permute-start.8 = (bf16[320,640]{1,0:T(8,128)(2,1)S(1)}, bf16[320,640]{1,0:T(8,128)(2,1)S(1)}, u32[]{:S(2)}, u32[]{:S(2)}) collective-permute-start(bf16[320,640]{1,0:T(8,128)(2,1)S(1)} %collective-permute-done.6.refs_1_), channel_id=1, source_target_pairs={{0,6},{1,7},{6,0},{7,1},{8,14},{9,15},{14,8},{15,9},{16,22},{17,23... | collective-permute-start | bytes 1228808 | tf_op jit(solution)/shard_map/ppermute | solution.py:406
  33.3 1.3 collective-permute-start.7
  37.3 3.4 %collective-permute-start.12 = (bf16[320,640]{1,0:T(8,128)(2,1)S(1)}, bf16[320,640]{1,0:T(8,128)(2,1)S(1)}, u32[]{:S(2)}, u32[]{:S(2)}) collective-permute-start(bf16[320,640]{1,0:T(8,128)(2,1)S(1)} %collective-permute-done.3.refs_7_), channel_id=1, source_target_pairs={{0,1},{1,0},{2,3},{3,2},{8,9},{9,8},{10,11},{11,10},{16,17},{17,16... | collective-permute-start | bytes 1228808 | tf_op jit(solution)/shard_map/ppermute | solution.py:372
  40.7 3.8 %collective-permute-done.8.refs_3_ = bf16[320,640]{1,0:T(8,128)(2,1)S(1)} collective-permute-done((bf16[320,640]{1,0:T(8,128)(2,1)S(1)}, bf16[320,640]{1,0:T(8,128)(2,1)S(1)}, u32[]{:S(2)}, u32[]{:S(2)}) %collective-permute-start.8) | collective-permute-done | bytes 409632 | tf_op jit(solution)/shard_map/ppermute | solution.py:406
  44.4 6.8 %collective-permute-done.7.refs_2_ = bf16[320,640]{1,0:T(8,128)(2,1)S(1)} collective-permute-done((bf16[320,640]{1,0:T(8,128)(2,1)S(1)}, bf16[320,640]{1,0:T(8,128)(2,1)S(1)}, u32[]{:S(2)}, u32[]{:S(2)}) %collective-permute-start.7) | collective-permute-done | bytes 409632 | tf_op jit(solution)/shard_map/ppermute | solution.py:405
  54.5 3.4 %collective-permute-start.5 = (bf16[320,640]{1,0:T(8,128)(2,1)S(1)}, bf16[320,640]{1,0:T(8,128)(2,1)S(1)}, u32[]{:S(2)}, u32[]{:S(2)}) collective-permute-start(bf16[320,640]{1,0:T(8,128)(2,1)S(1)} %collective-permute-done.4.refs_11_), channel_id=1, source_target_pairs={{0,1},{1,0},{2,3},{3,2},{8,9},{9,8},{10,11},{11,10},{16,17},{17,16... | collective-permute-start | bytes 1228808 | tf_op jit(solution)/shard_map/ppermute | solution.py:372
  58.6 2.1 %shard_map.68 = (bf16[512,2560]{1,0:T(8,128)(2,1)S(1)}, f32[320,512]{1,0:T(8,128)S(1)}, f32[8,128]{1,0:T(8,128)S(1)}) custom-call(f32[320,640]{1,0:T(8,128)S(1)} %copy-done, bf16[4,336,128]{2,1,0:T(8,128)(2,1)S(1)} %pad_maximum_fusion.refs_0_, bf16[4,336,128]{2,1,0:T(8,128)(2,1)S(1)} %collective-permute-done.16.refs_1_, ...), custom_call_target="tpu_custom_call" | custom-call | tf_op jit(solution)/shard_map/pallas_call | solution.py:430
  60.7 5.1 %collective-permute-done.10.refs_5_ = bf16[320,640]{1,0:T(8,128)(2,1)S(1)} collective-permute-done((bf16[320,640]{1,0:T(8,128)(2,1)S(1)}, bf16[320,640]{1,0:T(8,128)(2,1)S(1)}, u32[]{:S(2)}, u32[]{:S(2)}) %collective-permute-start.10) | collective-permute-done | bytes 409632 | tf_op jit(solution)/shard_map/ppermute | solution.py:376
  65.8 3.9 %shard_map.69 = (bf16[4,2,320,640]{3,2,1,0:T(8,128)(2,1)S(1)}, f32[512,640]{1,0:T(8,128)S(1)}) custom-call(bf16[320,640]{1,0:T(8,128)(2,1)} %refs_0_.1, bf16[320,640]{1,0:T(8,128)(2,1)S(1)} %collective-permute-done.6.refs_1_, bf16[320,640]{1,0:T(8,128)(2,1)S(1)} %collective-permute-done.7.refs_2_, bf16[320,640]{1,0:T(8,128)(2,1)S(1)} %collective-permute-done.8.refs_3_, ...), custom_call_target="tpu_custom_call" | custom-call | tf_op jit(solution)/shard_map/pallas_call | solution.py:438
  69.7 1.9 %shard_map.70 = (bf16[4,2,320,640]{3,2,1,0:T(8,128)(2,1)S(1)}, f32[160,512]{1,0:T(8,128)S(1)}, f32[160,512]{1,0:T(8,128)S(1)}) custom-call(bf16[320,640]{1,0:T(8,128)(2,1)S(1)} %collective-permute-done.2.low_ref, bf16[320,640]{1,0:T(8,128)(2,1)S(1)} %collective-permute-done.5.high_ref, ...), custom_call_target="tpu_custom_call", output_to_operand_aliasing={{0}: (2, {})} | custom-call | tf_op jit(solution)/shard_map/pallas_call | solution.py:445
  71.6 2.5 %shard_map.71 = (f32[320,640]{1,0:T(8,128)S(1)}, f32[320,640]{1,0:T(8,128)S(1)}, f32[320,640]{1,0:T(8,128)S(1)}, f32[320,640]{1,0:T(8,128)S(1)}, bf16[320,2560]{1,0:T(8,128)(2,1)S(1)}) custom-call(bf16[4,2,320,640]{3,2,1,0:T(8,128)(2,1)S(1)} %get-tuple-element.23.held_ref), custom_call_target="tpu_custom_call" | custom-call | tf_op jit(solution)/shard_map/pallas_call | solution.py:482
  74.2 2.5 %collective-permute-start.27 = (bf16[320,2560]{1,0:T(8,128)(2,1)S(1)}, bf16[320,2560]{1,0:T(8,128)(2,1)S(1)}, u32[]{:S(2)}, u32[]{:S(2)}) collective-permute-start(bf16[320,2560]{1,0:T(8,128)(2,1)S(1)} %get-tuple-element.28.refs_0_), channel_id=1, source_target_pairs={{0,16},{1,17},{10,26},{11,27},{20,4},{21,5},{30,14},{31,15}} | collective-permute-start | bytes 4915208 | tf_op jit(solution)/shard_map/ppermute | solution.py:497
  77.3 2.1 %collective-permute-start.26 = (bf16[320,2560]{1,0:T(8,128)(2,1)S(1)}, bf16[320,2560]{1,0:T(8,128)(2,1)S(1)}, u32[]{:S(2)}, u32[]{:S(2)}) collective-permute-start(bf16[320,2560]{1,0:T(8,128)(2,1)S(1)} %get-tuple-element.28.refs_0_), channel_id=1, source_target_pairs={{0,8},{1,9},{10,2},{11,3},{20,28},{21,29},{30,22},{31,23}} | collective-permute-start | bytes 4915208 | tf_op jit(solution)/shard_map/ppermute | solution.py:497
  79.3 19.4 %collective-permute-done.27.refs_2_ = bf16[320,2560]{1,0:T(8,128)(2,1)S(1)} collective-permute-done((bf16[320,2560]{1,0:T(8,128)(2,1)S(1)}, bf16[320,2560]{1,0:T(8,128)(2,1)S(1)}, u32[]{:S(2)}, u32[]{:S(2)}) %collective-permute-start.27) | collective-permute-done | bytes 1638432 | tf_op jit(solution)/shard_map/ppermute | solution.py:497
  99.5 3.2 %collective-permute-start.30 = (f32[160,512]{1,0:T(8,128)S(1)}, f32[160,512]{1,0:T(8,128)S(1)}, u32[]{:S(2)}, u32[]{:S(2)}) collective-permute-start(f32[160,512]{1,0:T(8,128)S(1)} %add.19), channel_id=1, source_target_pairs={{0,16},{8,24},{16,0},{24,8},{1,17},{9,25},{17,1},{25,9},{2,18},{10... | collective-permute-start | bytes 983048 | tf_op jit(solution)/shard_map/ppermute | solution.py:383
  102.7 5.1 %collective-permute-done.30 = f32[160,512]{1,0:T(8,128)S(1)} collective-permute-done((f32[160,512]{1,0:T(8,128)S(1)}, f32[160,512]{1,0:T(8,128)S(1)}, u32[]{:S(2)}, u32[]{:S(2)}) %collective-permute-start.30) | collective-permute-done | bytes 327712 | tf_op jit(solution)/shard_map/ppermute | solution.py:383
  110.2 2.1 %collective-permute-start.32 = (f32[64,640]{1,0:T(8,128)S(1)}, f32[64,640]{1,0:T(8,128)S(1)}, u32[]{:S(2)}, u32[]{:S(2)}) collective-permute-start(f32[64,640]{1,0:T(8,128)S(1)} %get-tuple-element.31), channel_id=1, source_target_pairs={{0,1},{1,0},{2,3},{3,2},{4,5},{5,4},{6,7},{7,6},{8,9},{9,8},{10,11... | collective-permute-start | bytes 491528 | tf_op jit(solution)/shard_map/ppermute | solution.py:383
  112.4 2.1 %collective-permute-start.25 = (f32[320,640]{1,0:T(8,128)S(1)}, f32[320,640]{1,0:T(8,128)S(1)}, u32[]{:S(2)}, u32[]{:S(2)}) collective-permute-start(f32[320,640]{1,0:T(8,128)S(1)} %add.18), channel_id=1, source_target_pairs={{0,16},{8,24},{16,0},{24,8},{1,17},{9,25},{17,1},{25,9},{2,18},{10... | collective-permute-start | bytes 2457608 | tf_op jit(solution)/shard_map/ppermute | solution.py:383
  114.5 2.4 %collective-permute-done.32 = f32[64,640]{1,0:T(8,128)S(1)} collective-permute-done((f32[64,640]{1,0:T(8,128)S(1)}, f32[64,640]{1,0:T(8,128)S(1)}, u32[]{:S(2)}, u32[]{:S(2)}) %collective-permute-start.32) | collective-permute-done | bytes 163872 | tf_op jit(solution)/shard_map/ppermute | solution.py:383
  117.0 5.7 %collective-permute-done.33 = f32[64,640]{1,0:T(8,128)S(1)} collective-permute-done((f32[64,640]{1,0:T(8,128)S(1)}, f32[64,640]{1,0:T(8,128)S(1)}, u32[]{:S(2)}, u32[]{:S(2)}) %collective-permute-start.33) | collective-permute-done | bytes 163872 | tf_op jit(solution)/shard_map/ppermute | solution.py:383
  122.7 6.3 %collective-permute-start.34 = (f32[64,640]{1,0:T(8,128)S(1)}, f32[64,640]{1,0:T(8,128)S(1)}, u32[]{:S(2)}, u32[]{:S(2)}) collective-permute-start(f32[64,640]{1,0:T(8,128)S(1)} %add.22), channel_id=1, source_target_pairs={{0,4},{1,5},{2,6},{3,7},{4,0},{5,1},{6,2},{7,3},{8,12},{9,13},{10,... | collective-permute-start | bytes 491528 | tf_op jit(solution)/shard_map/ppermute | solution.py:383
  129.0 6.6 %collective-permute-done.34 = f32[64,640]{1,0:T(8,128)S(1)} collective-permute-done((f32[64,640]{1,0:T(8,128)S(1)}, f32[64,640]{1,0:T(8,128)S(1)}, u32[]{:S(2)}, u32[]{:S(2)}) %collective-permute-start.34) | collective-permute-done | bytes 163872 | tf_op jit(solution)/shard_map/ppermute | solution.py:383
  135.9 6.0 %collective-permute-done.35.refs_1_ = f32[64,640]{1,0:T(8,128)S(1)} collective-permute-done((f32[64,640]{1,0:T(8,128)S(1)}, f32[64,640]{1,0:T(8,128)S(1)}, u32[]{:S(2)}, u32[]{:S(2)}) %collective-permute-start.35) | collective-permute-done | bytes 163872 | tf_op jit(solution)/shard_map/ppermute | solution.py:383
  143.3 18.4 %shard_map.76 = f32[320,128]{1,0:T(8,128)} custom-call(f32[64,640]{1,0:T(8,128)S(1)} %add.23.refs_0_, f32[64,640]{1,0:T(8,128)S(1)} %collective-permute-done.35.refs_1_, f32[64,640]{1,0:T(8,128)S(1)} %collective-permute-done.36.refs_2_, f32[64,640]{1,0:T(8,128)S(1)} %collective-permute-done.37.refs_3_, f32[320,512]{1,0:T(8,128)S(1)} %get-tuple-element.32.refs_4_), custom_call_target="tpu_custom_call" | custom-call | tf_op jit(solution)/shard_map/pallas_call | solution.py:470
  161.6 2.4 %shard_map.74 = f32[320,640]{1,0:T(8,128)} custom-call(bf16[4,2,320,640]{3,2,1,0:T(8,128)(2,1)S(1)} %get-tuple-element.23.held_ref, bf16[320,2560]{1,0:T(8,128)(2,1)S(1)} %get-tuple-element.28.refs_0_, bf16[320,2560]{1,0:T(8,128)(2,1)S(1)} %collective-permute-done.26.refs_1_, bf16[320,2560]{1,0:T(8,128)(2,1)S(1)} %collective-permute-done.27.refs_2_, ...), custom_call_target="tpu_custom_call" | custom-call | tf_op jit(solution)/shard_map/pallas_call | solution.py:500
  (67 shorter events, 17.7 us)
Async XLA Ops:
  2.8 8.9 %collective-permute-start.15 = (bf16[336,128]{1,0:T(8,128)(2,1)S(1)}, bf16[336,128]{1,0:T(8,128)(2,1)S(1)}, u32[]{:S(2)}, u32[]{:S(2)}) collective-permute-start(bf16[336,128]{1,0:T(8,128)(2,1)S(1)} %shard_map.67), channel_id=1, source_target_pairs={{0,6},{1,7},{2,0},{3,1},{4,2},{5,3},{6,4},{7,5},{8,14},{9,15},{10,... | collective-permute-start | bytes 258056 | tf_op jit(solution)/shard_map/ppermute | solution.py:380
  7.8 8.9 %collective-permute-start.14 = (bf16[336,128]{1,0:T(8,128)(2,1)S(1)}, bf16[336,128]{1,0:T(8,128)(2,1)S(1)}, u32[]{:S(2)}, u32[]{:S(2)}) collective-permute-start(bf16[336,128]{1,0:T(8,128)(2,1)S(1)} %shard_map.67), channel_id=1, source_target_pairs={{0,4},{1,5},{2,6},{3,7},{4,0},{5,1},{6,2},{7,3},{8,12},{9,13},{10,... | collective-permute-start | bytes 258056 | tf_op jit(solution)/shard_map/ppermute | solution.py:380
  7.8 8.9 %collective-permute-start.13 = (bf16[336,128]{1,0:T(8,128)(2,1)S(1)}, bf16[336,128]{1,0:T(8,128)(2,1)S(1)}, u32[]{:S(2)}, u32[]{:S(2)}) collective-permute-start(bf16[336,128]{1,0:T(8,128)(2,1)S(1)} %shard_map.67), channel_id=1, source_target_pairs={{0,2},{1,3},{2,4},{3,5},{4,6},{5,7},{6,0},{7,1},{8,10},{9,11},{10,... | collective-permute-start | bytes 258056 | tf_op jit(solution)/shard_map/ppermute | solution.py:380
  8.9 10.7 %collective-permute-start.6 = (bf16[320,640]{1,0:T(8,128)(2,1)}, bf16[320,640]{1,0:T(8,128)(2,1)S(1)}, u32[]{:S(2)}, u32[]{:S(2)}) collective-permute-start(bf16[320,640]{1,0:T(8,128)(2,1)} %refs_0_.1), channel_id=1, source_target_pairs={{0,1},{1,0},{2,3},{3,2},{4,5},{5,4},{6,7},{7,6},{8,9},{9,8},{10,11... | collective-permute-start | bytes 1228808 | tf_op jit(solution)/shard_map/ppermute | solution.py:372
  10.3 16.5 %collective-permute-start.3 = (bf16[320,640]{1,0:T(8,128)(2,1)}, bf16[320,640]{1,0:T(8,128)(2,1)S(1)}, u32[]{:S(2)}, u32[]{:S(2)}) collective-permute-start(bf16[320,640]{1,0:T(8,128)(2,1)} %refs_0_.1), channel_id=1, source_target_pairs={{2,0},{3,1},{4,2},{5,3},{6,4},{7,5},{10,8},{11,9},{12,10},{13,11},... | collective-permute-start | bytes 1228808 | tf_op jit(solution)/shard_map/ppermute | solution.py:376
  11.6 16.7 %collective-permute-start = (bf16[320,640]{1,0:T(8,128)(2,1)}, bf16[320,640]{1,0:T(8,128)(2,1)S(1)}, u32[]{:S(2)}, u32[]{:S(2)}) collective-permute-start(bf16[320,640]{1,0:T(8,128)(2,1)} %refs_0_.1), channel_id=1, source_target_pairs={{0,2},{1,3},{2,4},{3,5},{4,6},{5,7},{8,10},{9,11},{10,12},{11,13},... | collective-permute-start | bytes 1228808 | tf_op jit(solution)/shard_map/ppermute | solution.py:376
  16.8 8.7 %collective-permute-start.17 = (bf16[4,336,128]{2,1,0:T(8,128)(2,1)S(1)}, bf16[4,336,128]{2,1,0:T(8,128)(2,1)S(1)}, u32[]{:S(2)}, u32[]{:S(2)}) collective-permute-start(bf16[4,336,128]{2,1,0:T(8,128)(2,1)S(1)} %pad_maximum_fusion.refs_0_), channel_id=1, source_target_pairs={{0,16},{8,24},{16,0},{24,8},{1,17},{9,25},{17,1},{25,9},{2,18},{10... | collective-permute-start | bytes 1032200 | tf_op jit(solution)/shard_map/ppermute | solution.py:383
  18.3 8.5 %collective-permute-start.16 = (bf16[4,336,128]{2,1,0:T(8,128)(2,1)S(1)}, bf16[4,336,128]{2,1,0:T(8,128)(2,1)S(1)}, u32[]{:S(2)}, u32[]{:S(2)}) collective-permute-start(bf16[4,336,128]{2,1,0:T(8,128)(2,1)S(1)} %pad_maximum_fusion.refs_0_), channel_id=1, source_target_pairs={{0,1},{1,0},{2,3},{3,2},{4,5},{5,4},{6,7},{7,6},{8,9},{9,8},{10,11... | collective-permute-start | bytes 1032200 | tf_op jit(solution)/shard_map/ppermute | solution.py:372
  19.5 13.8 %collective-permute-start.19 = (bf16[4,336,128]{2,1,0:T(8,128)(2,1)S(1)}, bf16[4,336,128]{2,1,0:T(8,128)(2,1)S(1)}, u32[]{:S(2)}, u32[]{:S(2)}) collective-permute-start(bf16[4,336,128]{2,1,0:T(8,128)(2,1)S(1)} %pad_maximum_fusion.refs_0_), channel_id=1, source_target_pairs={{0,8},{8,0},{16,24},{24,16},{1,9},{9,1},{17,25},{25,17},{2,10},{10... | collective-permute-start | bytes 1032200 | tf_op jit(solution)/shard_map/ppermute | solution.py:383
  25.5 9.2 %collective-permute-start.21 = (bf16[4,336,128]{2,1,0:T(8,128)(2,1)S(1)}, bf16[4,336,128]{2,1,0:T(8,128)(2,1)S(1)}, u32[]{:S(2)}, u32[]{:S(2)}) collective-permute-start(bf16[4,336,128]{2,1,0:T(8,128)(2,1)S(1)} %collective-permute-done.17.refs_2_), channel_id=1, source_target_pairs={{0,8},{8,0},{16,24},{24,16},{1,9},{9,1},{17,25},{25,17},{2,10},{10... | collective-permute-start | bytes 1032200 | tf_op jit(solution)/shard_map/ppermute | solution.py:383
  26.8 9.2 %collective-permute-start.20 = (bf16[4,336,128]{2,1,0:T(8,128)(2,1)S(1)}, bf16[4,336,128]{2,1,0:T(8,128)(2,1)S(1)}, u32[]{:S(2)}, u32[]{:S(2)}) collective-permute-start(bf16[4,336,128]{2,1,0:T(8,128)(2,1)S(1)} %collective-permute-done.16.refs_1_), channel_id=1, source_target_pairs={{0,8},{8,0},{16,24},{24,16},{1,9},{9,1},{17,25},{25,17},{2,10},{10... | collective-permute-start | bytes 1032200 | tf_op jit(solution)/shard_map/ppermute | solution.py:383
  26.8 10.5 %collective-permute-start.18 = (bf16[4,336,128]{2,1,0:T(8,128)(2,1)S(1)}, bf16[4,336,128]{2,1,0:T(8,128)(2,1)S(1)}, u32[]{:S(2)}, u32[]{:S(2)}) collective-permute-start(bf16[4,336,128]{2,1,0:T(8,128)(2,1)S(1)} %collective-permute-done.16.refs_1_), channel_id=1, source_target_pairs={{0,16},{8,24},{16,0},{24,8},{1,17},{9,25},{17,1},{25,9},{2,18},{10... | collective-permute-start | bytes 1032200 | tf_op jit(solution)/shard_map/ppermute | solution.py:383
  28.3 16.1 %collective-permute-start.8 = (bf16[320,640]{1,0:T(8,128)(2,1)S(1)}, bf16[320,640]{1,0:T(8,128)(2,1)S(1)}, u32[]{:S(2)}, u32[]{:S(2)}) collective-permute-start(bf16[320,640]{1,0:T(8,128)(2,1)S(1)} %collective-permute-done.6.refs_1_), channel_id=1, source_target_pairs={{0,6},{1,7},{6,0},{7,1},{8,14},{9,15},{14,8},{15,9},{16,22},{17,23... | collective-permute-start | bytes 1228808 | tf_op jit(solution)/shard_map/ppermute | solution.py:406
  33.3 17.9 %collective-permute-start.7 = (bf16[320,640]{1,0:T(8,128)(2,1)S(1)}, bf16[320,640]{1,0:T(8,128)(2,1)S(1)}, u32[]{:S(2)}, u32[]{:S(2)}) collective-permute-start(bf16[320,640]{1,0:T(8,128)(2,1)S(1)} %collective-permute-done.6.refs_1_), channel_id=1, source_target_pairs={{0,2},{1,3},{6,4},{7,5},{8,10},{9,11},{14,12},{15,13},{16,18},{17,... | collective-permute-start | bytes 1228808 | tf_op jit(solution)/shard_map/ppermute | solution.py:405
  34.7 17.8 %collective-permute-start.4 = (bf16[320,640]{1,0:T(8,128)(2,1)S(1)}, bf16[320,640]{1,0:T(8,128)(2,1)S(1)}, u32[]{:S(2)}, u32[]{:S(2)}) collective-permute-start(bf16[320,640]{1,0:T(8,128)(2,1)S(1)} %collective-permute-done.3.refs_7_), channel_id=1, source_target_pairs={{2,0},{3,1},{4,2},{5,3},{10,8},{11,9},{12,10},{13,11},{18,16},{19,... | collective-permute-start | bytes 1228808 | tf_op jit(solution)/shard_map/ppermute | solution.py:376
  36.0 17.8 %collective-permute-start.1 = (bf16[320,640]{1,0:T(8,128)(2,1)S(1)}, bf16[320,640]{1,0:T(8,128)(2,1)S(1)}, u32[]{:S(2)}, u32[]{:S(2)}) collective-permute-start(bf16[320,640]{1,0:T(8,128)(2,1)S(1)} %collective-permute-done.refs_6_), channel_id=1, source_target_pairs={{2,4},{3,5},{4,6},{5,7},{10,12},{11,13},{12,14},{13,15},{18,20},{1... | collective-permute-start | bytes 1228808 | tf_op jit(solution)/shard_map/ppermute | solution.py:376
  37.3 17.2 %collective-permute-start.12 = (bf16[320,640]{1,0:T(8,128)(2,1)S(1)}, bf16[320,640]{1,0:T(8,128)(2,1)S(1)}, u32[]{:S(2)}, u32[]{:S(2)}) collective-permute-start(bf16[320,640]{1,0:T(8,128)(2,1)S(1)} %collective-permute-done.3.refs_7_), channel_id=1, source_target_pairs={{0,1},{1,0},{2,3},{3,2},{8,9},{9,8},{10,11},{11,10},{16,17},{17,16... | collective-permute-start | bytes 1228808 | tf_op jit(solution)/shard_map/ppermute | solution.py:372
  44.4 13.5 %collective-permute-start.22 = (bf16[4,336,128]{2,1,0:T(8,128)(2,1)S(1)}, bf16[4,336,128]{2,1,0:T(8,128)(2,1)S(1)}, u32[]{:S(2)}, u32[]{:S(2)}) collective-permute-start(bf16[4,336,128]{2,1,0:T(8,128)(2,1)S(1)} %collective-permute-done.18.refs_3_), channel_id=1, source_target_pairs={{0,8},{8,0},{16,24},{24,16},{1,9},{9,1},{17,25},{25,17},{2,10},{10... | collective-permute-start | bytes 1032200 | tf_op jit(solution)/shard_map/ppermute | solution.py:383
  51.3 9.4 %collective-permute-start.11 = (bf16[320,640]{1,0:T(8,128)(2,1)S(1)}, bf16[320,640]{1,0:T(8,128)(2,1)S(1)}, u32[]{:S(2)}, u32[]{:S(2)}) collective-permute-start(bf16[320,640]{1,0:T(8,128)(2,1)S(1)} %collective-permute-done.refs_6_), channel_id=1, source_target_pairs={{4,5},{5,4},{6,7},{7,6},{12,13},{13,12},{14,15},{15,14},{20,21},{2... | collective-permute-start | bytes 1228808 | tf_op jit(solution)/shard_map/ppermute | solution.py:372
  52.5 13.3 %collective-permute-start.10 = (bf16[320,640]{1,0:T(8,128)(2,1)S(1)}, bf16[320,640]{1,0:T(8,128)(2,1)S(1)}, u32[]{:S(2)}, u32[]{:S(2)}) collective-permute-start(bf16[320,640]{1,0:T(8,128)(2,1)S(1)} %collective-permute-done.4.refs_11_), channel_id=1, source_target_pairs={{2,0},{3,1},{10,8},{11,9},{18,16},{19,17},{26,24},{27,25}} | collective-permute-start | bytes 1228808 | tf_op jit(solution)/shard_map/ppermute | solution.py:376
  53.8 12.0 %collective-permute-start.9 = (bf16[320,640]{1,0:T(8,128)(2,1)S(1)}, bf16[320,640]{1,0:T(8,128)(2,1)S(1)}, u32[]{:S(2)}, u32[]{:S(2)}) collective-permute-start(bf16[320,640]{1,0:T(8,128)(2,1)S(1)} %collective-permute-done.1.refs_10_), channel_id=1, source_target_pairs={{4,6},{5,7},{12,14},{13,15},{20,22},{21,23},{28,30},{29,31}} | collective-permute-start | bytes 1228808 | tf_op jit(solution)/shard_map/ppermute | solution.py:376
  54.5 15.2 %collective-permute-start.5 = (bf16[320,640]{1,0:T(8,128)(2,1)S(1)}, bf16[320,640]{1,0:T(8,128)(2,1)S(1)}, u32[]{:S(2)}, u32[]{:S(2)}) collective-permute-start(bf16[320,640]{1,0:T(8,128)(2,1)S(1)} %collective-permute-done.4.refs_11_), channel_id=1, source_target_pairs={{0,1},{1,0},{2,3},{3,2},{8,9},{9,8},{10,11},{11,10},{16,17},{17,16... | collective-permute-start | bytes 1228808 | tf_op jit(solution)/shard_map/ppermute | solution.py:372
  57.9 11.8 %collective-permute-start.2 = (bf16[320,640]{1,0:T(8,128)(2,1)S(1)}, bf16[320,640]{1,0:T(8,128)(2,1)S(1)}, u32[]{:S(2)}, u32[]{:S(2)}) collective-permute-start(bf16[320,640]{1,0:T(8,128)(2,1)S(1)} %collective-permute-done.1.refs_10_), channel_id=1, source_target_pairs={{4,5},{5,4},{6,7},{7,6},{12,13},{13,12},{14,15},{15,14},{20,21},{2... | collective-permute-start | bytes 1228808 | tf_op jit(solution)/shard_map/ppermute | solution.py:372
  74.2 24.6 %collective-permute-start.27 = (bf16[320,2560]{1,0:T(8,128)(2,1)S(1)}, bf16[320,2560]{1,0:T(8,128)(2,1)S(1)}, u32[]{:S(2)}, u32[]{:S(2)}) collective-permute-start(bf16[320,2560]{1,0:T(8,128)(2,1)S(1)} %get-tuple-element.28.refs_0_), channel_id=1, source_target_pairs={{0,16},{1,17},{10,26},{11,27},{20,4},{21,5},{30,14},{31,15}} | collective-permute-start | bytes 4915208 | tf_op jit(solution)/shard_map/ppermute | solution.py:497
  76.7 22.8 %collective-permute-start.29 = (f32[160,512]{1,0:T(8,128)S(1)}, f32[160,512]{1,0:T(8,128)S(1)}, u32[]{:S(2)}, u32[]{:S(2)}) collective-permute-start(f32[160,512]{1,0:T(8,128)S(1)} %get-tuple-element.30), channel_id=1, source_target_pairs={{0,8},{8,0},{16,24},{24,16},{1,9},{9,1},{17,25},{25,17},{2,10},{10... | collective-permute-start | bytes 983048 | tf_op jit(solution)/shard_map/ppermute | solution.py:383
  76.8 35.5 %collective-permute-start.24 = (f32[320,640]{1,0:T(8,128)S(1)}, f32[320,640]{1,0:T(8,128)S(1)}, u32[]{:S(2)}, u32[]{:S(2)}) collective-permute-start(f32[320,640]{1,0:T(8,128)S(1)} %get-tuple-element.27), channel_id=1, source_target_pairs={{0,8},{8,0},{16,24},{24,16},{1,9},{9,1},{17,25},{25,17},{2,10},{10... | collective-permute-start | bytes 2457608 | tf_op jit(solution)/shard_map/ppermute | solution.py:383
  77.3 84.4 %collective-permute-start.26 = (bf16[320,2560]{1,0:T(8,128)(2,1)S(1)}, bf16[320,2560]{1,0:T(8,128)(2,1)S(1)}, u32[]{:S(2)}, u32[]{:S(2)}) collective-permute-start(bf16[320,2560]{1,0:T(8,128)(2,1)S(1)} %get-tuple-element.28.refs_0_), channel_id=1, source_target_pairs={{0,8},{1,9},{10,2},{11,3},{20,28},{21,29},{30,22},{31,23}} | collective-permute-start | bytes 4915208 | tf_op jit(solution)/shard_map/ppermute | solution.py:497
  98.7 62.9 %collective-permute-start.28 = (bf16[320,2560]{1,0:T(8,128)(2,1)S(1)}, bf16[320,2560]{1,0:T(8,128)(2,1)S(1)}, u32[]{:S(2)}, u32[]{:S(2)}) collective-permute-start(bf16[320,2560]{1,0:T(8,128)(2,1)S(1)} %collective-permute-done.27.refs_2_), channel_id=1, source_target_pairs={{16,24},{17,25},{26,18},{27,19},{4,12},{5,13},{14,6},{15,7}} | collective-permute-start | bytes 4915208 | tf_op jit(solution)/shard_map/ppermute | solution.py:497
  99.5 8.2 %collective-permute-start.30 = (f32[160,512]{1,0:T(8,128)S(1)}, f32[160,512]{1,0:T(8,128)S(1)}, u32[]{:S(2)}, u32[]{:S(2)}) collective-permute-start(f32[160,512]{1,0:T(8,128)S(1)} %add.19), channel_id=1, source_target_pairs={{0,16},{8,24},{16,0},{24,8},{1,17},{9,25},{17,1},{25,9},{2,18},{10... | collective-permute-start | bytes 983048 | tf_op jit(solution)/shard_map/ppermute | solution.py:383
  107.9 28.0 %collective-permute-start.23 = (f32[320,640]{1,0:T(8,128)S(1)}, f32[320,640]{1,0:T(8,128)S(1)}, u32[]{:S(2)}, u32[]{:S(2)}) collective-permute-start(f32[320,640]{1,0:T(8,128)S(1)} %get-tuple-element.25), channel_id=1, source_target_pairs={{0,8},{8,0},{16,24},{24,16},{1,9},{9,1},{17,25},{25,17},{2,10},{10... | collective-permute-start | bytes 2457608 | tf_op jit(solution)/shard_map/ppermute | solution.py:383
  112.4 29.7 %collective-permute-start.25 = (f32[320,640]{1,0:T(8,128)S(1)}, f32[320,640]{1,0:T(8,128)S(1)}, u32[]{:S(2)}, u32[]{:S(2)}) collective-permute-start(f32[320,640]{1,0:T(8,128)S(1)} %add.18), channel_id=1, source_target_pairs={{0,16},{8,24},{16,0},{24,8},{1,17},{9,25},{17,1},{25,9},{2,18},{10... | collective-permute-start | bytes 2457608 | tf_op jit(solution)/shard_map/ppermute | solution.py:383
  122.7 13.0 %collective-permute-start.34 = (f32[64,640]{1,0:T(8,128)S(1)}, f32[64,640]{1,0:T(8,128)S(1)}, u32[]{:S(2)}, u32[]{:S(2)}) collective-permute-start(f32[64,640]{1,0:T(8,128)S(1)} %add.22), channel_id=1, source_target_pairs={{0,4},{1,5},{2,6},{3,7},{4,0},{5,1},{6,2},{7,3},{8,12},{9,13},{10,... | collective-permute-start | bytes 491528 | tf_op jit(solution)/shard_map/ppermute | solution.py:383
  (9 other events, 107.5 us)

commit v5 on v4

--- a/solution.py
+++ b/solution.py
@@ -236,10 +236,10 @@
             send_ref[...] = part_ref[(1 - core) * half : (2 - core) * half, :]
 
 
-def gram_kernel(roles, keep_ref, across_ref, out_ref, power_ref):
+def gram_kernel(roles, keep_ref, across_ref, mine_ref, send_ref, power_ref):
     order = power_ref.shape[1]
     half = keep_ref.shape[0]
-    here = lax.axis_index("role")
+    here, side_at = lax.axis_index("role"), lax.axis_index("shard") % 2
     for core in (0, 1):
 
         @pl.when(here % 2 == core)
@@ -254,20 +254,28 @@
             at = 0
             for which in (0, 1):
                 row, height, first = strip_of(order, roles, role, which)
-                out_ref[:, at : at + order - first] = product(
-                    power_ref[:, row : row + height], power_ref[:, first:], (0, 0), HI
-                )
+                strip = product(power_ref[:, row : row + height], power_ref[:, first:], (0, 0), HI)
+                parts = strip[: height // 2], strip[height // 2 :]
+                for side in (0, 1):
+
+                    @pl.when(side_at == side)
+                    def _():
+                        mine_ref[:, at : at + order - first] = parts[side]
+                        send_ref[:, at : at + order - first] = parts[1 - side]
+
                 at += order - first
-            if at < out_ref.shape[1]:
-                out_ref[:, at:] = jnp.zeros((out_ref.shape[0], out_ref.shape[1] - at), jnp.float32)
+            for ref in (mine_ref, send_ref):
+                if at < ref.shape[1]:
+                    ref[:, at:] = jnp.zeros((ref.shape[0], ref.shape[1] - at), jnp.float32)
 
 
 def basis_kernel(roles, *refs):
-    given, (power_ref, out_ref, m_ref, left_ref, right_ref, column_ref) = refs[:4], refs[4:]
+    given, (power_ref, out_ref, m_ref, left_ref, right_ref, column_ref) = refs[:8], refs[8:]
     n = power_ref.shape[1]
     nb = n // BLOCK
-    here = lax.axis_index("role")
-    for bits, ref in zip((0, 2, 1, 3), given):
+    here, side_at = lax.axis_index("role"), lax.axis_index("shard") % 2
+    for number, ref in enumerate(given):
+        bits, side = ((0, 2, 1, 3)[number // 2], (side_at + number) % 2)
         for role in range(roles):
 
             @pl.when(here ^ bits == role)
@@ -275,7 +283,8 @@
                 at = 0
                 for which in (0, 1):
                     row, height, first = strip_of(n, roles, role, which)
-                    m_ref[row : row + height, first:n] = ref[:, at : at + n - first]
+                    rows = pl.ds(pl.multiple_of(row + side * (height // 2), height // 2), height // 2)
+                    m_ref[rows, first:n] = ref[:, at : at + n - first]
                     at += n - first
 
     m_ref[:, n:] = eye(n)
@@ -457,27 +466,33 @@
     keep = keep + other_core(send)
     keep = keep + other_half(keep)
 
-    packed, power = call(
-        "gram",
-        functools.partial(gram_kernel, roles),
-        out_shape=(shape(order // (2 * roles), packed_width(order, roles)), shape(rows, order)),
-    )(keep, other_core(keep))
-    bit = 1
+    piece = shape(order // (4 * roles), packed_width(order, roles))
+    packed, send, power = call("gram", functools.partial(gram_kernel, roles), (piece, piece, shape(rows, order)))(
+        keep, other_core(keep)
+    )
+    packed = packed + other_side(send)
+    bit = 2
     while bit < shards:
         packed = packed + flip(packed, "shard", shards, bit)
         bit *= 2
-    yours = other_half(packed)
+    slanted = [
+        (role * shards + shard, (role ^ 2) * shards + (shard ^ 1))
+        for role in range(roles)
+        for shard in range(shards)
+    ]
+    mine = [packed, other_side(packed), other_half(packed), lax.ppermute(packed, ("role", "shard"), slanted)]
+    theirs = [other_core(value) for value in mine]
     left_basis = call(
         "basis",
         functools.partial(basis_kernel, roles),
-        out_shape=shape(rows, vec),
+        shape(rows, vec),
         scratch_shapes=[
             pltpu.VMEM((order, 2 * order), jnp.float32),
             pltpu.VMEM((BLOCK, BLOCK), jnp.float32),
             pltpu.VMEM((BLOCK, BLOCK), jnp.float32),
             pltpu.VMEM((PANEL * PANEL, BLOCK), jnp.float32),
         ],
-    )(packed, yours, other_core(packed), other_core(yours), power)
+    )(*mine, *theirs, power)
 
     *shares, slab = call(
         "sides",

time: 164 us -> 166 us (1.012)
  starting transfers between devices: 56.7 us -> 62.5 us
  waiting for transfers between devices: 70.7 us -> 66.1 us
    ppermute x18 -> x19, waiting for transfers between devices: 33.5 us -> 24.1 us  [flip(): return lax.ppermute(value, axis, [(i, i ^ bit) for i in range(size)])]
    ppermute x6 -> x8, waiting for transfers between devices: 1.61 us -> 7.13 us  [other_side(): return lax.ppermute(value, 'shard', pairs)]
    ppermute x6 -> x8, starting transfers between devices: 10.5 us -> 14.2 us  [other_side(): return lax.ppermute(value, 'shard', pairs)]
    ppermute x3, waiting for transfers between devices: 19.4 us -> 15.9 us  [from_owner(): return lax.ppermute(value, ('role', 'shard'), pairs)]
    ppermute x0 -> x1, waiting for transfers between devices: none -> 2.62 us  [step(): lax.ppermute(packed, ('role', 'shard'), slanted)]
    ppermute x0 -> x1, starting transfers between devices: none -> 1.85 us  [step(): lax.ppermute(packed, ('role', 'shard'), slanted)]
    ppermute x18 -> x19, starting transfers between devices: 18.2 us -> 18 us  [flip(): return lax.ppermute(value, axis, [(i, i ^ bit) for i in range(size)])]
  transfers between devices with their start and end apart: 38 -> 42, of which waited for: 15 -> 18; matrix products, arithmetic and copies ran while one was open for 0% -> 0% of each run, Pallas kernels for 16% -> 16%
where the time goes in v5:
time: 166 us
  waiting for transfers between devices  66.1 us (40%)
  starting transfers between devices  62.5 us (38%)
  Pallas kernels  34.8 us (21%)
    ppermute x19, waiting for transfers between devices, flip(): return lax.ppermute(value, axis, [(i, i ^ bit) for i in range(size)])  24.1 us
    pallas_call x1, Pallas kernels, step(): call('basis', functools.partial(basis_kernel, roles), shape(rows, vec), s...  18.4 us
    ppermute x19, starting transfers between devices, flip(): return lax.ppermute(value, axis, [(i, i ^ bit) for i in range(size)])  18 us
    ppermute x3, waiting for transfers between devices, from_owner(): return lax.ppermute(value, ('role', 'shard'), pairs)  15.9 us
    ppermute x8, starting transfers between devices, other_side(): return lax.ppermute(value, 'shard', pairs)  14.2 us
    ppermute x6, starting transfers between devices, along(): return lax.ppermute(value, 'shard', pairs)  10.3 us
    ppermute x8, waiting for transfers between devices, other_side(): return lax.ppermute(value, 'shard', pairs)  7.13 us
    ppermute x1, waiting for transfers between devices, step(): lax.ppermute(side, 'shard', inward)  6.85 us
  transfers between devices with their start and end apart: 42, of which 18 were waited for; matrix products, arithmetic and copies ran while one was open for 0% of the time, Pallas kernels for 16%

profile of v5, /device:TPU:0, one launch (start us, length us, event | category | flops | bytes accessed | tf_op | source)
XLA Modules:
  0.0 165.6 jit_solution(17355695827007767858)
XLA Ops:
  2.8 5.1 %collective-permute-start.15 = (bf16[336,128]{1,0:T(8,128)(2,1)S(1)}, bf16[336,128]{1,0:T(8,128)(2,1)S(1)}, u32[]{:S(2)}, u32[]{:S(2)}) collective-permute-start(bf16[336,128]{1,0:T(8,128)(2,1)S(1)} %shard_map.67), channel_id=1, source_target_pairs={{0,6},{1,7},{2,0},{3,1},{4,2},{5,3},{6,4},{7,5},{8,14},{9,15},{10,... | collective-permute-start | bytes 258056 | tf_op jit(solution)/shard_map/ppermute | solution.py:389
  11.6 5.0 %collective-permute-start = (bf16[320,640]{1,0:T(8,128)(2,1)}, bf16[320,640]{1,0:T(8,128)(2,1)S(1)}, u32[]{:S(2)}, u32[]{:S(2)}) collective-permute-start(bf16[320,640]{1,0:T(8,128)(2,1)} %refs_0_.1), channel_id=1, source_target_pairs={{0,2},{1,3},{2,4},{3,5},{4,6},{5,7},{8,10},{9,11},{10,12},{11,13},... | collective-permute-start | bytes 1228808 | tf_op jit(solution)/shard_map/ppermute | solution.py:385
  16.8 1.6 collective-permute-start.17
  19.5 6.0 %collective-permute-done.17.refs_2_ = bf16[4,336,128]{2,1,0:T(8,128)(2,1)S(1)} collective-permute-done((bf16[4,336,128]{2,1,0:T(8,128)(2,1)S(1)}, bf16[4,336,128]{2,1,0:T(8,128)(2,1)S(1)}, u32[]{:S(2)}, u32[]{:S(2)}) %collective-permute-start.17) | collective-permute-done | bytes 344096 | tf_op jit(solution)/shard_map/ppermute | solution.py:392
  28.3 5.0 %collective-permute-start.8 = (bf16[320,640]{1,0:T(8,128)(2,1)S(1)}, bf16[320,640]{1,0:T(8,128)(2,1)S(1)}, u32[]{:S(2)}, u32[]{:S(2)}) collective-permute-start(bf16[320,640]{1,0:T(8,128)(2,1)S(1)} %collective-permute-done.6.refs_1_), channel_id=1, source_target_pairs={{0,6},{1,7},{6,0},{7,1},{8,14},{9,15},{14,8},{15,9},{16,22},{17,23... | collective-permute-start | bytes 1228808 | tf_op jit(solution)/shard_map/ppermute | solution.py:415
  37.3 3.4 %collective-permute-start.12 = (bf16[320,640]{1,0:T(8,128)(2,1)S(1)}, bf16[320,640]{1,0:T(8,128)(2,1)S(1)}, u32[]{:S(2)}, u32[]{:S(2)}) collective-permute-start(bf16[320,640]{1,0:T(8,128)(2,1)S(1)} %collective-permute-done.3.refs_7_), channel_id=1, source_target_pairs={{0,1},{1,0},{2,3},{3,2},{8,9},{9,8},{10,11},{11,10},{16,17},{17,16... | collective-permute-start | bytes 1228808 | tf_op jit(solution)/shard_map/ppermute | solution.py:381
  40.7 3.8 %collective-permute-done.8.refs_3_ = bf16[320,640]{1,0:T(8,128)(2,1)S(1)} collective-permute-done((bf16[320,640]{1,0:T(8,128)(2,1)S(1)}, bf16[320,640]{1,0:T(8,128)(2,1)S(1)}, u32[]{:S(2)}, u32[]{:S(2)}) %collective-permute-start.8) | collective-permute-done | bytes 409632 | tf_op jit(solution)/shard_map/ppermute | solution.py:415
  44.4 6.8 %collective-permute-done.7.refs_2_ = bf16[320,640]{1,0:T(8,128)(2,1)S(1)} collective-permute-done((bf16[320,640]{1,0:T(8,128)(2,1)S(1)}, bf16[320,640]{1,0:T(8,128)(2,1)S(1)}, u32[]{:S(2)}, u32[]{:S(2)}) %collective-permute-start.7) | collective-permute-done | bytes 409632 | tf_op jit(solution)/shard_map/ppermute | solution.py:414
  54.5 3.4 %collective-permute-start.5 = (bf16[320,640]{1,0:T(8,128)(2,1)S(1)}, bf16[320,640]{1,0:T(8,128)(2,1)S(1)}, u32[]{:S(2)}, u32[]{:S(2)}) collective-permute-start(bf16[320,640]{1,0:T(8,128)(2,1)S(1)} %collective-permute-done.4.refs_11_), channel_id=1, source_target_pairs={{0,1},{1,0},{2,3},{3,2},{8,9},{9,8},{10,11},{11,10},{16,17},{17,16... | collective-permute-start | bytes 1228808 | tf_op jit(solution)/shard_map/ppermute | solution.py:381
  58.6 2.1 %shard_map.68 = (bf16[512,2560]{1,0:T(8,128)(2,1)S(1)}, f32[320,512]{1,0:T(8,128)S(1)}, f32[8,128]{1,0:T(8,128)S(1)}) custom-call(f32[320,640]{1,0:T(8,128)S(1)} %copy-done, bf16[4,336,128]{2,1,0:T(8,128)(2,1)S(1)} %pad_maximum_fusion.refs_0_, bf16[4,336,128]{2,1,0:T(8,128)(2,1)S(1)} %collective-permute-done.16.refs_1_, ...), custom_call_target="tpu_custom_call" | custom-call | tf_op jit(solution)/shard_map/pallas_call | solution.py:439
  60.7 5.1 %collective-permute-done.10.refs_5_ = bf16[320,640]{1,0:T(8,128)(2,1)S(1)} collective-permute-done((bf16[320,640]{1,0:T(8,128)(2,1)S(1)}, bf16[320,640]{1,0:T(8,128)(2,1)S(1)}, u32[]{:S(2)}, u32[]{:S(2)}) %collective-permute-start.10) | collective-permute-done | bytes 409632 | tf_op jit(solution)/shard_map/ppermute | solution.py:385
  65.8 3.9 %shard_map.69 = (bf16[4,2,320,640]{3,2,1,0:T(8,128)(2,1)S(1)}, f32[512,640]{1,0:T(8,128)S(1)}) custom-call(bf16[320,640]{1,0:T(8,128)(2,1)} %refs_0_.1, bf16[320,640]{1,0:T(8,128)(2,1)S(1)} %collective-permute-done.6.refs_1_, bf16[320,640]{1,0:T(8,128)(2,1)S(1)} %collective-permute-done.7.refs_2_, bf16[320,640]{1,0:T(8,128)(2,1)S(1)} %collective-permute-done.8.refs_3_, ...), custom_call_target="tpu_custom_call" | custom-call | tf_op jit(solution)/shard_map/pallas_call | solution.py:447
  69.7 1.9 %shard_map.70 = (bf16[4,2,320,640]{3,2,1,0:T(8,128)(2,1)S(1)}, f32[160,512]{1,0:T(8,128)S(1)}, f32[160,512]{1,0:T(8,128)S(1)}) custom-call(bf16[320,640]{1,0:T(8,128)(2,1)S(1)} %collective-permute-done.2.low_ref, bf16[320,640]{1,0:T(8,128)(2,1)S(1)} %collective-permute-done.5.high_ref, ...), custom_call_target="tpu_custom_call", output_to_operand_aliasing={{0}: (2, {})} | custom-call | tf_op jit(solution)/shard_map/pallas_call | solution.py:454
  71.6 2.5 %shard_map.71 = (f32[320,640]{1,0:T(8,128)S(1)}, f32[320,640]{1,0:T(8,128)S(1)}, f32[320,640]{1,0:T(8,128)S(1)}, f32[320,640]{1,0:T(8,128)S(1)}, bf16[320,2560]{1,0:T(8,128)(2,1)S(1)}) custom-call(bf16[4,2,320,640]{3,2,1,0:T(8,128)(2,1)S(1)} %get-tuple-element.24.held_ref), custom_call_target="tpu_custom_call" | custom-call | tf_op jit(solution)/shard_map/pallas_call | solution.py:497
  74.2 2.5 %collective-permute-start.27 = (bf16[320,2560]{1,0:T(8,128)(2,1)S(1)}, bf16[320,2560]{1,0:T(8,128)(2,1)S(1)}, u32[]{:S(2)}, u32[]{:S(2)}) collective-permute-start(bf16[320,2560]{1,0:T(8,128)(2,1)S(1)} %get-tuple-element.29.refs_0_), channel_id=1, source_target_pairs={{0,16},{1,17},{10,26},{11,27},{20,4},{21,5},{30,14},{31,15}} | collective-permute-start | bytes 4915208 | tf_op jit(solution)/shard_map/ppermute | solution.py:512
  76.8 2.5 %collective-permute-start.26 = (bf16[320,2560]{1,0:T(8,128)(2,1)S(1)}, bf16[320,2560]{1,0:T(8,128)(2,1)S(1)}, u32[]{:S(2)}, u32[]{:S(2)}) collective-permute-start(bf16[320,2560]{1,0:T(8,128)(2,1)S(1)} %get-tuple-element.29.refs_0_), channel_id=1, source_target_pairs={{0,8},{1,9},{10,2},{11,3},{20,28},{21,29},{30,22},{31,23}} | collective-permute-start | bytes 4915208 | tf_op jit(solution)/shard_map/ppermute | solution.py:512
  79.3 15.9 %collective-permute-done.27.refs_2_ = bf16[320,2560]{1,0:T(8,128)(2,1)S(1)} collective-permute-done((bf16[320,2560]{1,0:T(8,128)(2,1)S(1)}, bf16[320,2560]{1,0:T(8,128)(2,1)S(1)}, u32[]{:S(2)}, u32[]{:S(2)}) %collective-permute-start.27) | collective-permute-done | bytes 1638432 | tf_op jit(solution)/shard_map/ppermute | solution.py:512
  96.0 1.6 collective-permute-done.29
  97.7 5.0 %collective-permute-start.30 = (f32[160,512]{1,0:T(8,128)S(1)}, f32[160,512]{1,0:T(8,128)S(1)}, u32[]{:S(2)}, u32[]{:S(2)}) collective-permute-start(f32[160,512]{1,0:T(8,128)S(1)} %add.19), channel_id=1, source_target_pairs={{0,16},{8,24},{16,0},{24,8},{1,17},{9,25},{17,1},{25,9},{2,18},{10... | collective-permute-start | bytes 983048 | tf_op jit(solution)/shard_map/ppermute | solution.py:392
  102.8 8.2 %collective-permute-done.30 = f32[160,512]{1,0:T(8,128)S(1)} collective-permute-done((f32[160,512]{1,0:T(8,128)S(1)}, f32[160,512]{1,0:T(8,128)S(1)}, u32[]{:S(2)}, u32[]{:S(2)}) %collective-permute-start.30) | collective-permute-done | bytes 327712 | tf_op jit(solution)/shard_map/ppermute | solution.py:392
  111.2 1.8 %collective-permute-start.25 = (f32[320,640]{1,0:T(8,128)S(1)}, f32[320,640]{1,0:T(8,128)S(1)}, u32[]{:S(2)}, u32[]{:S(2)}) collective-permute-start(f32[320,640]{1,0:T(8,128)S(1)} %add.18), channel_id=1, source_target_pairs={{0,16},{8,24},{16,0},{24,8},{1,17},{9,25},{17,1},{25,9},{2,18},{10... | collective-permute-start | bytes 2457608 | tf_op jit(solution)/shard_map/ppermute | solution.py:392
  114.1 2.0 %collective-permute-start.32 = (f32[32,640]{1,0:T(8,128)S(1)}, f32[32,640]{1,0:T(8,128)S(1)}, u32[]{:S(2)}, u32[]{:S(2)}) collective-permute-start(f32[32,640]{1,0:T(8,128)S(1)} %get-tuple-element.33), channel_id=1, source_target_pairs={{0,1},{1,0},{2,3},{3,2},{4,5},{5,4},{6,7},{7,6},{8,9},{9,8},{10,11... | collective-permute-start | bytes 245768 | tf_op jit(solution)/shard_map/ppermute | solution.py:381
  116.1 2.8 %collective-permute-done.32 = f32[32,640]{1,0:T(8,128)S(1)} collective-permute-done((f32[32,640]{1,0:T(8,128)S(1)}, f32[32,640]{1,0:T(8,128)S(1)}, u32[]{:S(2)}, u32[]{:S(2)}) %collective-permute-start.32) | collective-permute-done | bytes 81952 | tf_op jit(solution)/shard_map/ppermute | solution.py:381
  119.0 4.4 %collective-permute-done.33 = f32[32,640]{1,0:T(8,128)S(1)} collective-permute-done((f32[32,640]{1,0:T(8,128)S(1)}, f32[32,640]{1,0:T(8,128)S(1)}, u32[]{:S(2)}, u32[]{:S(2)}) %collective-permute-start.33) | collective-permute-done | bytes 81952 | tf_op jit(solution)/shard_map/ppermute | solution.py:392
  123.4 5.8 %collective-permute-start.34 = (f32[32,640]{1,0:T(8,128)S(1)}, f32[32,640]{1,0:T(8,128)S(1)}, u32[]{:S(2)}, u32[]{:S(2)}) collective-permute-start(f32[32,640]{1,0:T(8,128)S(1)} %add.22), channel_id=1, source_target_pairs={{0,4},{1,5},{2,6},{3,7},{4,0},{5,1},{6,2},{7,3},{8,12},{9,13},{10,... | collective-permute-start | bytes 245768 | tf_op jit(solution)/shard_map/ppermute | solution.py:392
  129.2 2.7 %collective-permute-done.34 = f32[32,640]{1,0:T(8,128)S(1)} collective-permute-done((f32[32,640]{1,0:T(8,128)S(1)}, f32[32,640]{1,0:T(8,128)S(1)}, u32[]{:S(2)}, u32[]{:S(2)}) %collective-permute-start.34) | collective-permute-done | bytes 81952 | tf_op jit(solution)/shard_map/ppermute | solution.py:392
  132.0 1.9 %collective-permute-start.37 = (f32[32,640]{1,0:T(8,128)S(1)}, f32[32,640]{1,0:T(8,128)S(1)}, u32[]{:S(2)}, u32[]{:S(2)}) collective-permute-start(f32[32,640]{1,0:T(8,128)S(1)} %add.23.refs_0_), channel_id=1, source_target_pairs={{0,17},{1,16},{2,19},{3,18},{4,21},{5,20},{6,23},{7,22},{8,25},{9,... | collective-permute-start | bytes 245768 | tf_op jit(solution)/shard_map/ppermute | solution.py:483
  135.3 2.6 %collective-permute-done.37.refs_3_ = f32[32,640]{1,0:T(8,128)S(1)} collective-permute-done((f32[32,640]{1,0:T(8,128)S(1)}, f32[32,640]{1,0:T(8,128)S(1)}, u32[]{:S(2)}, u32[]{:S(2)}) %collective-permute-start.37) | collective-permute-done | bytes 81952 | tf_op jit(solution)/shard_map/ppermute | solution.py:483
  137.9 1.7 %collective-permute-start.35 = (f32[32,640]{1,0:T(8,128)S(1)}, f32[32,640]{1,0:T(8,128)S(1)}, u32[]{:S(2)}, u32[]{:S(2)}) collective-permute-start(f32[32,640]{1,0:T(8,128)S(1)} %add.23.refs_0_), channel_id=1, source_target_pairs={{0,1},{1,0},{2,3},{3,2},{4,5},{5,4},{6,7},{7,6},{8,9},{9,8},{10,11... | collective-permute-start | bytes 245768 | tf_op jit(solution)/shard_map/ppermute | solution.py:381
  139.6 2.7 %collective-permute-done.35.refs_1_ = f32[32,640]{1,0:T(8,128)S(1)} collective-permute-done((f32[32,640]{1,0:T(8,128)S(1)}, f32[32,640]{1,0:T(8,128)S(1)}, u32[]{:S(2)}, u32[]{:S(2)}) %collective-permute-start.35) | collective-permute-done | bytes 81952 | tf_op jit(solution)/shard_map/ppermute | solution.py:381
  143.8 18.4 %shard_map.76 = f32[320,128]{1,0:T(8,128)} custom-call(f32[32,640]{1,0:T(8,128)S(1)} %add.23.refs_0_, f32[32,640]{1,0:T(8,128)S(1)} %collective-permute-done.35.refs_1_, f32[32,640]{1,0:T(8,128)S(1)} %collective-permute-done.36.refs_2_, f32[32,640]{1,0:T(8,128)S(1)} %collective-permute-done.37.refs_3_, f32[32,640]{1,0:T(8,128)S(1)} %collective-permute-done.38.refs_4_, ...), custom_call_target="tpu_custom_call" | custom-call | tf_op jit(solution)/shard_map/pallas_call | solution.py:485
  163.3 2.4 %shard_map.74 = f32[320,640]{1,0:T(8,128)} custom-call(bf16[4,2,320,640]{3,2,1,0:T(8,128)(2,1)S(1)} %get-tuple-element.24.held_ref, bf16[320,2560]{1,0:T(8,128)(2,1)S(1)} %get-tuple-element.29.refs_0_, bf16[320,2560]{1,0:T(8,128)(2,1)S(1)} %collective-permute-done.26.refs_1_, bf16[320,2560]{1,0:T(8,128)(2,1)S(1)} %collective-permute-done.27.refs_2_, ...), custom_call_target="tpu_custom_call" | custom-call | tf_op jit(solution)/shard_map/pallas_call | solution.py:515
  (75 shorter events, 24.1 us)
Async XLA Ops:
  2.8 8.9 %collective-permute-start.15 = (bf16[336,128]{1,0:T(8,128)(2,1)S(1)}, bf16[336,128]{1,0:T(8,128)(2,1)S(1)}, u32[]{:S(2)}, u32[]{:S(2)}) collective-permute-start(bf16[336,128]{1,0:T(8,128)(2,1)S(1)} %shard_map.67), channel_id=1, source_target_pairs={{0,6},{1,7},{2,0},{3,1},{4,2},{5,3},{6,4},{7,5},{8,14},{9,15},{10,... | collective-permute-start | bytes 258056 | tf_op jit(solution)/shard_map/ppermute | solution.py:389
  7.8 8.9 %collective-permute-start.14 = (bf16[336,128]{1,0:T(8,128)(2,1)S(1)}, bf16[336,128]{1,0:T(8,128)(2,1)S(1)}, u32[]{:S(2)}, u32[]{:S(2)}) collective-permute-start(bf16[336,128]{1,0:T(8,128)(2,1)S(1)} %shard_map.67), channel_id=1, source_target_pairs={{0,4},{1,5},{2,6},{3,7},{4,0},{5,1},{6,2},{7,3},{8,12},{9,13},{10,... | collective-permute-start | bytes 258056 | tf_op jit(solution)/shard_map/ppermute | solution.py:389
  7.8 8.9 %collective-permute-start.13 = (bf16[336,128]{1,0:T(8,128)(2,1)S(1)}, bf16[336,128]{1,0:T(8,128)(2,1)S(1)}, u32[]{:S(2)}, u32[]{:S(2)}) collective-permute-start(bf16[336,128]{1,0:T(8,128)(2,1)S(1)} %shard_map.67), channel_id=1, source_target_pairs={{0,2},{1,3},{2,4},{3,5},{4,6},{5,7},{6,0},{7,1},{8,10},{9,11},{10,... | collective-permute-start | bytes 258056 | tf_op jit(solution)/shard_map/ppermute | solution.py:389
  8.9 10.7 %collective-permute-start.6 = (bf16[320,640]{1,0:T(8,128)(2,1)}, bf16[320,640]{1,0:T(8,128)(2,1)S(1)}, u32[]{:S(2)}, u32[]{:S(2)}) collective-permute-start(bf16[320,640]{1,0:T(8,128)(2,1)} %refs_0_.1), channel_id=1, source_target_pairs={{0,1},{1,0},{2,3},{3,2},{4,5},{5,4},{6,7},{7,6},{8,9},{9,8},{10,11... | collective-permute-start | bytes 1228808 | tf_op jit(solution)/shard_map/ppermute | solution.py:381
  10.3 16.5 %collective-permute-start.3 = (bf16[320,640]{1,0:T(8,128)(2,1)}, bf16[320,640]{1,0:T(8,128)(2,1)S(1)}, u32[]{:S(2)}, u32[]{:S(2)}) collective-permute-start(bf16[320,640]{1,0:T(8,128)(2,1)} %refs_0_.1), channel_id=1, source_target_pairs={{2,0},{3,1},{4,2},{5,3},{6,4},{7,5},{10,8},{11,9},{12,10},{13,11},... | collective-permute-start | bytes 1228808 | tf_op jit(solution)/shard_map/ppermute | solution.py:385
  11.6 16.7 %collective-permute-start = (bf16[320,640]{1,0:T(8,128)(2,1)}, bf16[320,640]{1,0:T(8,128)(2,1)S(1)}, u32[]{:S(2)}, u32[]{:S(2)}) collective-permute-start(bf16[320,640]{1,0:T(8,128)(2,1)} %refs_0_.1), channel_id=1, source_target_pairs={{0,2},{1,3},{2,4},{3,5},{4,6},{5,7},{8,10},{9,11},{10,12},{11,13},... | collective-permute-start | bytes 1228808 | tf_op jit(solution)/shard_map/ppermute | solution.py:385
  16.8 8.7 %collective-permute-start.17 = (bf16[4,336,128]{2,1,0:T(8,128)(2,1)S(1)}, bf16[4,336,128]{2,1,0:T(8,128)(2,1)S(1)}, u32[]{:S(2)}, u32[]{:S(2)}) collective-permute-start(bf16[4,336,128]{2,1,0:T(8,128)(2,1)S(1)} %pad_maximum_fusion.refs_0_), channel_id=1, source_target_pairs={{0,16},{8,24},{16,0},{24,8},{1,17},{9,25},{17,1},{25,9},{2,18},{10... | collective-permute-start | bytes 1032200 | tf_op jit(solution)/shard_map/ppermute | solution.py:392
  18.3 8.5 %collective-permute-start.16 = (bf16[4,336,128]{2,1,0:T(8,128)(2,1)S(1)}, bf16[4,336,128]{2,1,0:T(8,128)(2,1)S(1)}, u32[]{:S(2)}, u32[]{:S(2)}) collective-permute-start(bf16[4,336,128]{2,1,0:T(8,128)(2,1)S(1)} %pad_maximum_fusion.refs_0_), channel_id=1, source_target_pairs={{0,1},{1,0},{2,3},{3,2},{4,5},{5,4},{6,7},{7,6},{8,9},{9,8},{10,11... | collective-permute-start | bytes 1032200 | tf_op jit(solution)/shard_map/ppermute | solution.py:381
  19.5 13.8 %collective-permute-start.19 = (bf16[4,336,128]{2,1,0:T(8,128)(2,1)S(1)}, bf16[4,336,128]{2,1,0:T(8,128)(2,1)S(1)}, u32[]{:S(2)}, u32[]{:S(2)}) collective-permute-start(bf16[4,336,128]{2,1,0:T(8,128)(2,1)S(1)} %pad_maximum_fusion.refs_0_), channel_id=1, source_target_pairs={{0,8},{8,0},{16,24},{24,16},{1,9},{9,1},{17,25},{25,17},{2,10},{10... | collective-permute-start | bytes 1032200 | tf_op jit(solution)/shard_map/ppermute | solution.py:392
  25.5 9.2 %collective-permute-start.21 = (bf16[4,336,128]{2,1,0:T(8,128)(2,1)S(1)}, bf16[4,336,128]{2,1,0:T(8,128)(2,1)S(1)}, u32[]{:S(2)}, u32[]{:S(2)}) collective-permute-start(bf16[4,336,128]{2,1,0:T(8,128)(2,1)S(1)} %collective-permute-done.17.refs_2_), channel_id=1, source_target_pairs={{0,8},{8,0},{16,24},{24,16},{1,9},{9,1},{17,25},{25,17},{2,10},{10... | collective-permute-start | bytes 1032200 | tf_op jit(solution)/shard_map/ppermute | solution.py:392
  26.8 9.2 %collective-permute-start.20 = (bf16[4,336,128]{2,1,0:T(8,128)(2,1)S(1)}, bf16[4,336,128]{2,1,0:T(8,128)(2,1)S(1)}, u32[]{:S(2)}, u32[]{:S(2)}) collective-permute-start(bf16[4,336,128]{2,1,0:T(8,128)(2,1)S(1)} %collective-permute-done.16.refs_1_), channel_id=1, source_target_pairs={{0,8},{8,0},{16,24},{24,16},{1,9},{9,1},{17,25},{25,17},{2,10},{10... | collective-permute-start | bytes 1032200 | tf_op jit(solution)/shard_map/ppermute | solution.py:392
  26.8 10.5 %collective-permute-start.18 = (bf16[4,336,128]{2,1,0:T(8,128)(2,1)S(1)}, bf16[4,336,128]{2,1,0:T(8,128)(2,1)S(1)}, u32[]{:S(2)}, u32[]{:S(2)}) collective-permute-start(bf16[4,336,128]{2,1,0:T(8,128)(2,1)S(1)} %collective-permute-done.16.refs_1_), channel_id=1, source_target_pairs={{0,16},{8,24},{16,0},{24,8},{1,17},{9,25},{17,1},{25,9},{2,18},{10... | collective-permute-start | bytes 1032200 | tf_op jit(solution)/shard_map/ppermute | solution.py:392
  28.3 16.1 %collective-permute-start.8 = (bf16[320,640]{1,0:T(8,128)(2,1)S(1)}, bf16[320,640]{1,0:T(8,128)(2,1)S(1)}, u32[]{:S(2)}, u32[]{:S(2)}) collective-permute-start(bf16[320,640]{1,0:T(8,128)(2,1)S(1)} %collective-permute-done.6.refs_1_), channel_id=1, source_target_pairs={{0,6},{1,7},{6,0},{7,1},{8,14},{9,15},{14,8},{15,9},{16,22},{17,23... | collective-permute-start | bytes 1228808 | tf_op jit(solution)/shard_map/ppermute | solution.py:415
  33.3 17.9 %collective-permute-start.7 = (bf16[320,640]{1,0:T(8,128)(2,1)S(1)}, bf16[320,640]{1,0:T(8,128)(2,1)S(1)}, u32[]{:S(2)}, u32[]{:S(2)}) collective-permute-start(bf16[320,640]{1,0:T(8,128)(2,1)S(1)} %collective-permute-done.6.refs_1_), channel_id=1, source_target_pairs={{0,2},{1,3},{6,4},{7,5},{8,10},{9,11},{14,12},{15,13},{16,18},{17,... | collective-permute-start | bytes 1228808 | tf_op jit(solution)/shard_map/ppermute | solution.py:414
  34.7 17.8 %collective-permute-start.4 = (bf16[320,640]{1,0:T(8,128)(2,1)S(1)}, bf16[320,640]{1,0:T(8,128)(2,1)S(1)}, u32[]{:S(2)}, u32[]{:S(2)}) collective-permute-start(bf16[320,640]{1,0:T(8,128)(2,1)S(1)} %collective-permute-done.3.refs_7_), channel_id=1, source_target_pairs={{2,0},{3,1},{4,2},{5,3},{10,8},{11,9},{12,10},{13,11},{18,16},{19,... | collective-permute-start | bytes 1228808 | tf_op jit(solution)/shard_map/ppermute | solution.py:385
  36.0 17.8 %collective-permute-start.1 = (bf16[320,640]{1,0:T(8,128)(2,1)S(1)}, bf16[320,640]{1,0:T(8,128)(2,1)S(1)}, u32[]{:S(2)}, u32[]{:S(2)}) collective-permute-start(bf16[320,640]{1,0:T(8,128)(2,1)S(1)} %collective-permute-done.refs_6_), channel_id=1, source_target_pairs={{2,4},{3,5},{4,6},{5,7},{10,12},{11,13},{12,14},{13,15},{18,20},{1... | collective-permute-start | bytes 1228808 | tf_op jit(solution)/shard_map/ppermute | solution.py:385
  37.3 17.2 %collective-permute-start.12 = (bf16[320,640]{1,0:T(8,128)(2,1)S(1)}, bf16[320,640]{1,0:T(8,128)(2,1)S(1)}, u32[]{:S(2)}, u32[]{:S(2)}) collective-permute-start(bf16[320,640]{1,0:T(8,128)(2,1)S(1)} %collective-permute-done.3.refs_7_), channel_id=1, source_target_pairs={{0,1},{1,0},{2,3},{3,2},{8,9},{9,8},{10,11},{11,10},{16,17},{17,16... | collective-permute-start | bytes 1228808 | tf_op jit(solution)/shard_map/ppermute | solution.py:381
  44.4 13.5 %collective-permute-start.22 = (bf16[4,336,128]{2,1,0:T(8,128)(2,1)S(1)}, bf16[4,336,128]{2,1,0:T(8,128)(2,1)S(1)}, u32[]{:S(2)}, u32[]{:S(2)}) collective-permute-start(bf16[4,336,128]{2,1,0:T(8,128)(2,1)S(1)} %collective-permute-done.18.refs_3_), channel_id=1, source_target_pairs={{0,8},{8,0},{16,24},{24,16},{1,9},{9,1},{17,25},{25,17},{2,10},{10... | collective-permute-start | bytes 1032200 | tf_op jit(solution)/shard_map/ppermute | solution.py:392
  51.3 9.4 %collective-permute-start.11 = (bf16[320,640]{1,0:T(8,128)(2,1)S(1)}, bf16[320,640]{1,0:T(8,128)(2,1)S(1)}, u32[]{:S(2)}, u32[]{:S(2)}) collective-permute-start(bf16[320,640]{1,0:T(8,128)(2,1)S(1)} %collective-permute-done.refs_6_), channel_id=1, source_target_pairs={{4,5},{5,4},{6,7},{7,6},{12,13},{13,12},{14,15},{15,14},{20,21},{2... | collective-permute-start | bytes 1228808 | tf_op jit(solution)/shard_map/ppermute | solution.py:381
  52.5 13.3 %collective-permute-start.10 = (bf16[320,640]{1,0:T(8,128)(2,1)S(1)}, bf16[320,640]{1,0:T(8,128)(2,1)S(1)}, u32[]{:S(2)}, u32[]{:S(2)}) collective-permute-start(bf16[320,640]{1,0:T(8,128)(2,1)S(1)} %collective-permute-done.4.refs_11_), channel_id=1, source_target_pairs={{2,0},{3,1},{10,8},{11,9},{18,16},{19,17},{26,24},{27,25}} | collective-permute-start | bytes 1228808 | tf_op jit(solution)/shard_map/ppermute | solution.py:385
  53.8 12.0 %collective-permute-start.9 = (bf16[320,640]{1,0:T(8,128)(2,1)S(1)}, bf16[320,640]{1,0:T(8,128)(2,1)S(1)}, u32[]{:S(2)}, u32[]{:S(2)}) collective-permute-start(bf16[320,640]{1,0:T(8,128)(2,1)S(1)} %collective-permute-done.1.refs_10_), channel_id=1, source_target_pairs={{4,6},{5,7},{12,14},{13,15},{20,22},{21,23},{28,30},{29,31}} | collective-permute-start | bytes 1228808 | tf_op jit(solution)/shard_map/ppermute | solution.py:385
  54.5 15.2 %collective-permute-start.5 = (bf16[320,640]{1,0:T(8,128)(2,1)S(1)}, bf16[320,640]{1,0:T(8,128)(2,1)S(1)}, u32[]{:S(2)}, u32[]{:S(2)}) collective-permute-start(bf16[320,640]{1,0:T(8,128)(2,1)S(1)} %collective-permute-done.4.refs_11_), channel_id=1, source_target_pairs={{0,1},{1,0},{2,3},{3,2},{8,9},{9,8},{10,11},{11,10},{16,17},{17,16... | collective-permute-start | bytes 1228808 | tf_op jit(solution)/shard_map/ppermute | solution.py:381
  57.9 11.8 %collective-permute-start.2 = (bf16[320,640]{1,0:T(8,128)(2,1)S(1)}, bf16[320,640]{1,0:T(8,128)(2,1)S(1)}, u32[]{:S(2)}, u32[]{:S(2)}) collective-permute-start(bf16[320,640]{1,0:T(8,128)(2,1)S(1)} %collective-permute-done.1.refs_10_), channel_id=1, source_target_pairs={{4,5},{5,4},{6,7},{7,6},{12,13},{13,12},{14,15},{15,14},{20,21},{2... | collective-permute-start | bytes 1228808 | tf_op jit(solution)/shard_map/ppermute | solution.py:381
  74.2 21.0 %collective-permute-start.27 = (bf16[320,2560]{1,0:T(8,128)(2,1)S(1)}, bf16[320,2560]{1,0:T(8,128)(2,1)S(1)}, u32[]{:S(2)}, u32[]{:S(2)}) collective-permute-start(bf16[320,2560]{1,0:T(8,128)(2,1)S(1)} %get-tuple-element.29.refs_0_), channel_id=1, source_target_pairs={{0,16},{1,17},{10,26},{11,27},{20,4},{21,5},{30,14},{31,15}} | collective-permute-start | bytes 4915208 | tf_op jit(solution)/shard_map/ppermute | solution.py:512
  76.7 34.4 %collective-permute-start.24 = (f32[320,640]{1,0:T(8,128)S(1)}, f32[320,640]{1,0:T(8,128)S(1)}, u32[]{:S(2)}, u32[]{:S(2)}) collective-permute-start(f32[320,640]{1,0:T(8,128)S(1)} %get-tuple-element.28), channel_id=1, source_target_pairs={{0,8},{8,0},{16,24},{24,16},{1,9},{9,1},{17,25},{25,17},{2,10},{10... | collective-permute-start | bytes 2457608 | tf_op jit(solution)/shard_map/ppermute | solution.py:392
  76.8 86.5 %collective-permute-start.26 = (bf16[320,2560]{1,0:T(8,128)(2,1)S(1)}, bf16[320,2560]{1,0:T(8,128)(2,1)S(1)}, u32[]{:S(2)}, u32[]{:S(2)}) collective-permute-start(bf16[320,2560]{1,0:T(8,128)(2,1)S(1)} %get-tuple-element.29.refs_0_), channel_id=1, source_target_pairs={{0,8},{1,9},{10,2},{11,3},{20,28},{21,29},{30,22},{31,23}} | collective-permute-start | bytes 4915208 | tf_op jit(solution)/shard_map/ppermute | solution.py:512
  95.2 68.1 %collective-permute-start.28 = (bf16[320,2560]{1,0:T(8,128)(2,1)S(1)}, bf16[320,2560]{1,0:T(8,128)(2,1)S(1)}, u32[]{:S(2)}, u32[]{:S(2)}) collective-permute-start(bf16[320,2560]{1,0:T(8,128)(2,1)S(1)} %collective-permute-done.27.refs_2_), channel_id=1, source_target_pairs={{16,24},{17,25},{26,18},{27,19},{4,12},{5,13},{14,6},{15,7}} | collective-permute-start | bytes 4915208 | tf_op jit(solution)/shard_map/ppermute | solution.py:512
  97.7 13.2 %collective-permute-start.30 = (f32[160,512]{1,0:T(8,128)S(1)}, f32[160,512]{1,0:T(8,128)S(1)}, u32[]{:S(2)}, u32[]{:S(2)}) collective-permute-start(f32[160,512]{1,0:T(8,128)S(1)} %add.19), channel_id=1, source_target_pairs={{0,16},{8,24},{16,0},{24,8},{1,17},{9,25},{17,1},{25,9},{2,18},{10... | collective-permute-start | bytes 983048 | tf_op jit(solution)/shard_map/ppermute | solution.py:392
  102.7 29.4 %collective-permute-start.23 = (f32[320,640]{1,0:T(8,128)S(1)}, f32[320,640]{1,0:T(8,128)S(1)}, u32[]{:S(2)}, u32[]{:S(2)}) collective-permute-start(f32[320,640]{1,0:T(8,128)S(1)} %get-tuple-element.26), channel_id=1, source_target_pairs={{0,8},{8,0},{16,24},{24,16},{1,9},{9,1},{17,25},{25,17},{2,10},{10... | collective-permute-start | bytes 2457608 | tf_op jit(solution)/shard_map/ppermute | solution.py:392
  111.2 51.0 %collective-permute-start.25 = (f32[320,640]{1,0:T(8,128)S(1)}, f32[320,640]{1,0:T(8,128)S(1)}, u32[]{:S(2)}, u32[]{:S(2)}) collective-permute-start(f32[320,640]{1,0:T(8,128)S(1)} %add.18), channel_id=1, source_target_pairs={{0,16},{8,24},{16,0},{24,8},{1,17},{9,25},{17,1},{25,9},{2,18},{10... | collective-permute-start | bytes 2457608 | tf_op jit(solution)/shard_map/ppermute | solution.py:392
  123.4 8.5 %collective-permute-start.34 = (f32[32,640]{1,0:T(8,128)S(1)}, f32[32,640]{1,0:T(8,128)S(1)}, u32[]{:S(2)}, u32[]{:S(2)}) collective-permute-start(f32[32,640]{1,0:T(8,128)S(1)} %add.22), channel_id=1, source_target_pairs={{0,4},{1,5},{2,6},{3,7},{4,0},{5,1},{6,2},{7,3},{8,12},{9,13},{10,... | collective-permute-start | bytes 245768 | tf_op jit(solution)/shard_map/ppermute | solution.py:392
  132.0 5.8 %collective-permute-start.37 = (f32[32,640]{1,0:T(8,128)S(1)}, f32[32,640]{1,0:T(8,128)S(1)}, u32[]{:S(2)}, u32[]{:S(2)}) collective-permute-start(f32[32,640]{1,0:T(8,128)S(1)} %add.23.refs_0_), channel_id=1, source_target_pairs={{0,17},{1,16},{2,19},{3,18},{4,21},{5,20},{6,23},{7,22},{8,25},{9,... | collective-permute-start | bytes 245768 | tf_op jit(solution)/shard_map/ppermute | solution.py:483
  (13 other events, 109.0 us)
